TPU v7x, 128 devices: a whole 4x4x4 slice. The times are simulated.
128 devices in a mesh: lat: 4 (over z_hi, core), lon: 32 (over y, x, z_lo).
Axes of the slice: x: 4, y: 4, z: 4 (z_hi: 2, z_lo: 2; z = z_hi * 2 + z_lo), core: 2. Of those that a mesh axis runs over, the one named last changes fastest.
Arguments:
- obs_feat: bfloat16 [131072, 256], P(('lat', 'lon')), may hold values from -6 to 6
- obs_owner: int32 [131072, 1], P(('lat', 'lon')), may hold values from 0 to 127; in each aligned block of 1024 rows (0 to 1023, 1024 to 2047, ...) at most 16 rows name the same one
- obs_cell: int32 [131072], P(('lat', 'lon')), may hold values from 0 to 1023
- obs_valid: int32 [131072], P(('lat', 'lon')), may hold values 0 or 1
- grid_feat: bfloat16 [64, 2048, 512], P('lat', 'lon'), may hold values from -6 to 6
- w_embed: bfloat16 [256, 512], replicated, may hold values from -0.375 to 0.375
- gains: float32 [2, 512], replicated, may hold values from 0.5 to 1.5
- w_query: bfloat16 [2, 512, 512], replicated, may hold values from -2.4748737 to 2.4748737
- w_key: bfloat16 [2, 512, 512], replicated, may hold values from -2.4748737 to 2.4748737
- w_value: bfloat16 [2, 512, 512], replicated, may hold values from -0.25 to 0.25
- w_out: bfloat16 [2, 512, 512], replicated, may hold values from -0.25 to 0.25
Outputs:
- encoded: bfloat16 [64, 2048, 512], P('lat', 'lon')
Inputs may be any that keep to these rules, and one draw needn't show every extreme that they name: `obs_owner`: owner d is the device of latitude index d // 32 and longitude index d % 32. Among the rows of one device no owner appears more than 16 times, and in some device one owner appears exactly 16 times. `obs_cell`: cell r * 64 + c is row r and column c of the owner's tile.
All inputs are finite; a program needn't handle non-finite values. No bound on the sum of `obs_valid` on one device may be relied on, other than what follows from the above.
Results may differ from a plain program's by a relative error of at most 0.015.
The roundings to bfloat16 on the way count: a program that leaves them out, or rounds other values in their place, can miss the bound.
Values may be sent and summed in bfloat16 or wider, within the bound.
No kernel may reach another device: no remote copies, remote signals or barrier semaphores. Data moves between devices by JAX's collectives and lax.ppermute only.
A program may use at most 192 MiB of HBM per device.

v0:
```python
import jax
import jax.numpy as jnp
from jax import lax
from jax.sharding import PartitionSpec as P

HEADS = 8
LAYERS = 2


def with_halo(block, sides, width, periodic):
    for axis, dim in sides:
        count = lax.axis_size(axis)
        forward = [(i, i + 1) for i in range(count - 1)]
        if periodic:
            forward.append((count - 1, 0))
        backward = [(target, source) for source, target in forward]
        low = lax.ppermute(
            lax.slice_in_dim(block, block.shape[dim] - width, None, axis=dim), axis, forward
        )
        high = lax.ppermute(lax.slice_in_dim(block, 0, width, axis=dim), axis, backward)
        block = jnp.concatenate([low, block, high], axis=dim)
    return block


def attend(query, keys, values, lat_first, lat_total):
    width = query.shape[1]
    model_width = query.shape[2]
    head_size = model_width // HEADS
    blocks_row = width // 8
    q_five = query.reshape(8, blocks_row, 8, HEADS, head_size)

    def tiles_of(array):
        tiles = array.reshape(24, blocks_row + 2, 8, model_width)
        stacked = jnp.stack([tiles[:, j : j + blocks_row] for j in range(3)], axis=2)
        return stacked.reshape(24, blocks_row, 24, HEADS, head_size)

    key_tiles = tiles_of(keys)
    value_tiles = tiles_of(values)
    scores = jnp.einsum(
        "anbhe,cnkhe->nhabck", q_five, key_tiles, preferred_element_type=jnp.float32
    ) * head_size ** (-0.5)
    rows_global = lat_first + jnp.arange(24, dtype=jnp.int32)
    inside = (rows_global >= 0) & (rows_global < lat_total)
    scores = jnp.where(inside[:, None], scores, jnp.float32(-1e30))
    flat = scores.reshape(blocks_row, HEADS, 64, 576)
    highest = jnp.max(flat, axis=-1, keepdims=True)
    expo = jnp.exp(flat - highest)
    weights = (expo / jnp.sum(expo, axis=-1, keepdims=True)).astype(jnp.bfloat16)
    weights = weights.reshape(blocks_row, HEADS, 8, 8, 24, 24)
    result = jnp.einsum(
        "nhabck,cnkhe->anbhe", weights, value_tiles, preferred_element_type=jnp.float32
    )
    return result.astype(jnp.bfloat16).reshape(8, width, model_width)


def embed_rows(raw_rows, w_embed):
    return jax.nn.gelu(jnp.dot(raw_rows, w_embed, preferred_element_type=jnp.float32)).astype(
        jnp.bfloat16
    )


def project(flat, weight):
    return jnp.dot(flat, weight, preferred_element_type=jnp.float32).astype(jnp.bfloat16)


def local(
    obs_feat,
    obs_owner,
    obs_cell,
    obs_valid,
    grid_feat,
    w_embed,
    gains,
    w_query,
    w_key,
    w_value,
    w_out,
):
    lat_count = lax.axis_size("lat")
    lon_count = lax.axis_size("lon")
    devices = lat_count * lon_count
    obs_rows = obs_feat.shape[0]
    capacity = 2 * obs_rows // devices
    lat_cells, lon_cells, model_width = grid_feat.shape
    cell_total = lat_cells * lon_cells
    owner = obs_owner[:, 0]
    onehot = (owner[:, None] == jnp.arange(devices, dtype=jnp.int32)[None, :]).astype(jnp.int32)
    ranking = jnp.sum(jnp.cumsum(onehot, axis=0) * onehot, axis=1) - 1
    target = owner * capacity + ranking
    cell_tag = jnp.where(obs_valid == 1, obs_cell, -1)
    payload = embed_rows(obs_feat, w_embed)
    send_rows = (
        jnp.zeros((devices * capacity, payload.shape[1]), jnp.bfloat16).at[target].set(payload)
    )
    send_tags = jnp.full((devices * capacity,), -1, jnp.int32).at[target].set(cell_tag)
    got_rows, got_tags = (
        lax.all_to_all(
            send_rows.reshape(devices, capacity, -1),
            ("lat", "lon"),
            split_axis=0,
            concat_axis=0,
            tiled=True,
        ),
        lax.all_to_all(
            send_tags.reshape(devices, capacity),
            ("lat", "lon"),
            split_axis=0,
            concat_axis=0,
            tiled=True,
        ),
    )
    got_rows = got_rows.reshape(devices * capacity, -1)
    got_tags = got_tags.reshape(-1)
    safe_tags = jnp.where(got_tags >= 0, got_tags, cell_total)
    sums = jax.ops.segment_sum(
        got_rows.astype(jnp.float32), safe_tags, num_segments=cell_total + 1
    )[:cell_total]
    counts = jax.ops.segment_sum(
        jnp.ones(safe_tags.shape, jnp.float32), safe_tags, num_segments=cell_total + 1
    )[:cell_total]
    hidden = (sums / jnp.maximum(counts, 1.0)[:, None]).reshape(
        lat_cells, lon_cells, model_width
    ) + grid_feat.astype(jnp.float32)
    lat_anchor = lax.axis_index("lat") * lat_cells
    lat_total = lat_cells * lat_count
    for layer in range(LAYERS):
        scale = lax.rsqrt(jnp.mean(hidden * hidden, axis=-1, keepdims=True) + 1e-06)
        normed = (hidden * scale * gains[layer]).astype(jnp.bfloat16)
        flat = normed.reshape(-1, model_width)
        query = project(flat, w_query[layer]).reshape(lat_cells, lon_cells, model_width)
        source = jnp.concatenate(
            [project(flat, w_key[layer]), project(flat, w_value[layer])], axis=-1
        ).reshape(lat_cells, lon_cells, 2 * model_width)
        banded = with_halo(source, (("lat", 0),), 8, False)
        framed = with_halo(banded, (("lon", 1),), 8, True)
        key_pad = framed[..., :model_width]
        value_pad = framed[..., model_width:]

        def one_row(index_row):
            start = index_row * 8
            query_rows = lax.dynamic_slice_in_dim(query, start, 8, 0)
            key_rows = lax.dynamic_slice_in_dim(key_pad, start, 24, 0)
            value_rows = lax.dynamic_slice_in_dim(value_pad, start, 24, 0)
            return attend(query_rows, key_rows, value_rows, lat_anchor + start - 8, lat_total)

        attended = lax.map(one_row, jnp.arange(lat_cells // 8, dtype=jnp.int32)).reshape(
            lat_cells, lon_cells, model_width
        )
        update = jnp.dot(
            attended.reshape(-1, model_width), w_out[layer], preferred_element_type=jnp.float32
        )
        hidden = hidden + update.reshape(lat_cells, lon_cells, model_width)
    return hidden.astype(jnp.bfloat16)


def solution(mesh):
    placed = (
        P(("lat", "lon"), None),
        P(("lat", "lon"), None),
        P(("lat", "lon")),
        P(("lat", "lon")),
        P("lat", "lon", None),
        P(),
        P(),
        P(),
        P(),
        P(),
        P(),
    )
    return jax.shard_map(
        local, mesh=mesh, in_specs=placed, out_specs=P("lat", "lon", None), check_vma=False
    )
```

profile of v0, /device:TPU:1, one launch (start us, length us, event | category | flops | bytes accessed | tf_op | source)
XLA Modules:
  0.0 856.3 jit_solution(1066695490612616939)
XLA Ops:
  1.7 4.3 scatter_custom_fusion
  6.8 11.5 %all-to-all-start = ((s32[128,1,16]{2,1,0:T(1,128)}), s32[128,1,16]{2,1,0:T(1,128)S(1)}, u32[]{:S(2)}, u32[]{:S(2)}) async-start(s32[128,1,16]{2,1,0:T(1,128)} %bitcast.47), calls=%async_computation | async-start | bytes 131072 | tf_op jit(solution)/shard_map/all_to_all | solution.py:104
  19.1 6.7 scatter_custom_fusion.1
  27.8 7.7 all-to-all-start.1
  37.6 12.8 %scatter_custom_fusion.3 = f32[1025]{0:T(1024)S(1)} fusion(s32[2048]{0:T(1024)S(1)} %bitcast.222, f32[2048]{0:T(1024)S(1)} %broadcast.161, f32[]{:T(128)} %constant.157.clone.1), kind=kCustom, calls=%fused_computation.138 | custom fusion | flops 2048 | bytes 4104 | tf_op jit(solution)/shard_map/scatter-add | solution.py:118
  50.4 15.7 %all-to-all-done.1 = bf16[128,16,512]{2,1,0:T(8,128)(2,1)S(1)} async-done(((bf16[128,16,512]{2,1,0:T(8,128)(2,1)}), bf16[128,16,512]{2,1,0:T(8,128)(2,1)S(1)}, u32[]{:S(2)}, u32[]{:S(2)}) %all-to-all-start.1) | async-done | bytes 2097184 | tf_op jit(solution)/shard_map/all_to_all | solution.py:97
  67.5 14.0 %scatter_custom_fusion.2 = f32[1025,512]{1,0:T(8,128)S(1)} fusion(s32[2048]{0:T(1024)S(1)} %bitcast.223, bf16[2048,512]{1,0:T(8,128)(2,1)} %bitcast.203, f32[]{:T(128)} %constant.157.clone.1), kind=kCustom, calls=%fused_computation.60 | custom fusion | flops 2097152 | bytes 4196356 | tf_op jit(solution)/shard_map/scatter-add | solution.py:115
  88.7 3.1 collective-permute-start
  98.2 2.9 copy.63
  101.1 3.2 collective-permute-done
  104.3 17.5 %collective-permute-done.1 = bf16[8,64,1024]{2,1,0:T(8,128)(2,1)} collective-permute-done((bf16[8,64,1024]{2,1,0:T(8,128)(2,1)}, bf16[8,64,1024]{2,1,0:T(8,128)(2,1)}, u32[]{:S(2)}, u32[]{:S(2)}) %collective-permute-start.1) | collective-permute-done | bytes 1048608 | tf_op jit(solution)/shard_map/ppermute | solution.py:20
  123.8 5.6 collective-permute-start.3
  129.4 3.1 convolution_convert_fusion.3
  132.5 3.8 collective-permute-done.2
  137.6 2.9 pad_maximum_fusion.4
  140.4 2.9 fusion.70
  144.5 320.9 %while.24 = (s32[]{:T(128)}, bf16[2,8,64,512]{3,2,1,0:T(8,128)(2,1)}, s32[2]{0:T(128)S(1)}, bf16[32,80,512]{2,1,0:T(8,128)(2,1)}, s32[]{:T(128)}, /*index=5*/bf1...) while((s32[]{:T(128)}, ...), condition=%wide.region_11.12_spmd, body=%wide.region_8.11_spmd.sunk | while | flops 641982592 | bytes 108610392 | solution.py:146
  151.1 12.5 %reshape.280 = bf16[24,8,24,8,64]{4,3,2,1,0:T(8,128)(2,1)} reshape(bf16[24,8,3,8,512]{4,3,2,1,0:T(8,128)(2,1)} %pad_maximum_fusion.18) | data formatting | bytes 9437184 | tf_op jit(solution)/shard_map/while/body/eval_jaxpr/reshape | solution.py:35
  165.2 44.1 %fusion.91 = (f32[8,8,8,8]{3,2,1,0:T(8,128)S(1)}, f32[8,8,8,8,24,24]{5,3,4,2,1,0:T(8,128)}) fusion(pred[24]{0:T(512)(128)(4,1)S(1)} %compare_and_fusion.4, bf16[24,8,24,8,64,1]{4,3,2,1,0,5:T(8,128)(2,1)} %bitcast.191, bf16[8,8,8,8,64,1]{4,3,2,1,0,5:T(8,128)(2,1)S(1)} %bitcast.195), kind=kOutput, calls=%fused_computation.7.clone.1 | convolution fusion | flops 309063680 | bytes 14696472 | tf_op jit(solution)/shard_map/while/body/eval_jaxpr/anbhe,cnkhe->nhabck/dot_general | solution.py:39
  209.3 25.3 %fusion.92 = f32[8,8,8,8]{3,2,1,0:T(8,128)S(1)} fusion(f32[8,8,8,8,24,24]{5,3,4,2,1,0:T(8,128)} %get-tuple-element.352, f32[8,8,8,8]{3,2,1,0:T(8,128)S(1)} %get-tuple-element.353, pred[24]{0:T(512)(128)(4,1)S(1)} %compare_and_fusion.4), kind=kLoop, calls=%fused_computation.8.clone.1 | loop fusion | flops 9433088 | bytes 9469976 | tf_op jit(solution)/shard_map/while/body/eval_jaxpr/reduce_sum | solution.py:48
  237.4 12.5 %reshape.282 = bf16[24,8,24,8,64]{4,3,2,1,0:T(8,128)(2,1)} reshape(bf16[24,8,3,8,512]{4,3,2,1,0:T(8,128)(2,1)} %pad_maximum_fusion.19) | data formatting | bytes 9437184 | tf_op jit(solution)/shard_map/while/body/eval_jaxpr/reshape | solution.py:35
  249.9 52.2 %fusion.93 = bf16[8,8,8,8,64]{4,2,0,3,1:T(8,128)(2,1)S(1)} fusion(f32[8,8,8,8,24,24]{5,3,4,2,1,0:T(8,128)} %get-tuple-element.352, f32[8,8,8,8]{3,2,1,0:T(8,128)S(1)} %fusion.92, f32[8,8,8,8]{3,2,1,0:T(8,128)S(1)} %get-tuple-element.353, pred[24]{0:T(512)(128)(4,1)S(1)} %compare_and_fusion.4, bf16[24,8,24,8,64,1]{4,3,2,1,0,5:T(8,128)(2,1)} %bitcast.193), kind=kOutput, calls=%fused_computation.24.clone.1 | convolution fusion | flops 314048512 | bytes 14712856 | tf_op jit(solution)/shard_map/while/body/eval_jaxpr/nhabck,cnkhe->anbhe/dot_general | solution.py:50
  311.2 12.5 %reshape.280 = bf16[24,8,24,8,64]{4,3,2,1,0:T(8,128)(2,1)} reshape(bf16[24,8,3,8,512]{4,3,2,1,0:T(8,128)(2,1)} %pad_maximum_fusion.18) | data formatting | bytes 9437184 | tf_op jit(solution)/shard_map/while/body/eval_jaxpr/reshape | solution.py:35
  325.3 44.1 %fusion.91 = (f32[8,8,8,8]{3,2,1,0:T(8,128)S(1)}, f32[8,8,8,8,24,24]{5,3,4,2,1,0:T(8,128)}) fusion(pred[24]{0:T(512)(128)(4,1)S(1)} %compare_and_fusion.4, bf16[24,8,24,8,64,1]{4,3,2,1,0,5:T(8,128)(2,1)} %bitcast.191, bf16[8,8,8,8,64,1]{4,3,2,1,0,5:T(8,128)(2,1)S(1)} %bitcast.195), kind=kOutput, calls=%fused_computation.7.clone.1 | convolution fusion | flops 309063680 | bytes 14696472 | tf_op jit(solution)/shard_map/while/body/eval_jaxpr/anbhe,cnkhe->nhabck/dot_general | solution.py:39
  369.4 25.3 %fusion.92 = f32[8,8,8,8]{3,2,1,0:T(8,128)S(1)} fusion(f32[8,8,8,8,24,24]{5,3,4,2,1,0:T(8,128)} %get-tuple-element.352, f32[8,8,8,8]{3,2,1,0:T(8,128)S(1)} %get-tuple-element.353, pred[24]{0:T(512)(128)(4,1)S(1)} %compare_and_fusion.4), kind=kLoop, calls=%fused_computation.8.clone.1 | loop fusion | flops 9433088 | bytes 9469976 | tf_op jit(solution)/shard_map/while/body/eval_jaxpr/reduce_sum | solution.py:48
  397.6 12.5 %reshape.282 = bf16[24,8,24,8,64]{4,3,2,1,0:T(8,128)(2,1)} reshape(bf16[24,8,3,8,512]{4,3,2,1,0:T(8,128)(2,1)} %pad_maximum_fusion.19) | data formatting | bytes 9437184 | tf_op jit(solution)/shard_map/while/body/eval_jaxpr/reshape | solution.py:35
  410.1 52.2 %fusion.93 = bf16[8,8,8,8,64]{4,2,0,3,1:T(8,128)(2,1)S(1)} fusion(f32[8,8,8,8,24,24]{5,3,4,2,1,0:T(8,128)} %get-tuple-element.352, f32[8,8,8,8]{3,2,1,0:T(8,128)S(1)} %fusion.92, f32[8,8,8,8]{3,2,1,0:T(8,128)S(1)} %get-tuple-element.353, pred[24]{0:T(512)(128)(4,1)S(1)} %compare_and_fusion.4, bf16[24,8,24,8,64,1]{4,3,2,1,0,5:T(8,128)(2,1)} %bitcast.193), kind=kOutput, calls=%fused_computation.24.clone.1 | convolution fusion | flops 314048512 | bytes 14712856 | tf_op jit(solution)/shard_map/while/body/eval_jaxpr/nhabck,cnkhe->anbhe/dot_general | solution.py:50
  465.4 3.2 multiply_reduce_fusion
  474.7 3.9 collective-permute-start.4
  487.5 4.0 collective-permute-done.4
  491.5 17.6 %collective-permute-done.5 = bf16[8,64,1024]{2,1,0:T(8,128)(2,1)} collective-permute-done((bf16[8,64,1024]{2,1,0:T(8,128)(2,1)}, bf16[8,64,1024]{2,1,0:T(8,128)(2,1)}, u32[]{:S(2)}, u32[]{:S(2)}) %collective-permute-start.5) | collective-permute-done | bytes 1048608 | tf_op jit(solution)/shard_map/ppermute | solution.py:20
  511.1 5.7 collective-permute-start.7
  516.8 3.0 convolution_convert_fusion
  519.8 3.8 collective-permute-done.6
  524.8 2.9 pad_maximum_fusion.5
  527.7 2.9 fusion.69
  531.8 320.5 %while.25 = (s32[]{:T(128)}, bf16[2,8,64,512]{3,2,1,0:T(8,128)(2,1)}, s32[2]{0:T(128)S(1)}, bf16[32,80,512]{2,1,0:T(8,128)(2,1)}, s32[]{:T(128)}, /*index=5*/bf1...) while((s32[]{:T(128)}, ...), condition=%wide.region_16.17_spmd, body=%wide.region_13.16_spmd.sunk | while | flops 641982592 | bytes 108610392 | solution.py:146
  538.3 12.5 %reshape.283 = bf16[24,8,24,8,64]{4,3,2,1,0:T(8,128)(2,1)} reshape(bf16[24,8,3,8,512]{4,3,2,1,0:T(8,128)(2,1)} %pad_maximum_fusion.20) | data formatting | bytes 9437184 | tf_op jit(solution)/shard_map/while/body/eval_jaxpr/reshape | solution.py:35
  552.4 44.1 %fusion.95 = (f32[8,8,8,8]{3,2,1,0:T(8,128)S(1)}, f32[8,8,8,8,24,24]{5,3,4,2,1,0:T(8,128)}) fusion(pred[24]{0:T(512)(128)(4,1)S(1)} %compare_and_fusion.5, bf16[24,8,24,8,64,1]{4,3,2,1,0,5:T(8,128)(2,1)} %bitcast.192, bf16[8,8,8,8,64,1]{4,3,2,1,0,5:T(8,128)(2,1)S(1)} %bitcast.196), kind=kOutput, calls=%fused_computation.34.clone.1 | convolution fusion | flops 309063680 | bytes 14696472 | tf_op jit(solution)/shard_map/while/body/eval_jaxpr/anbhe,cnkhe->nhabck/dot_general | solution.py:39
  596.5 25.3 %fusion.96 = f32[8,8,8,8]{3,2,1,0:T(8,128)S(1)} fusion(f32[8,8,8,8,24,24]{5,3,4,2,1,0:T(8,128)} %get-tuple-element.369, f32[8,8,8,8]{3,2,1,0:T(8,128)S(1)} %get-tuple-element.370, pred[24]{0:T(512)(128)(4,1)S(1)} %compare_and_fusion.5), kind=kLoop, calls=%fused_computation.35.clone.1 | loop fusion | flops 9433088 | bytes 9469976 | tf_op jit(solution)/shard_map/while/body/eval_jaxpr/reduce_sum | solution.py:48
  624.7 12.5 %reshape.285 = bf16[24,8,24,8,64]{4,3,2,1,0:T(8,128)(2,1)} reshape(bf16[24,8,3,8,512]{4,3,2,1,0:T(8,128)(2,1)} %pad_maximum_fusion.21) | data formatting | bytes 9437184 | tf_op jit(solution)/shard_map/while/body/eval_jaxpr/reshape | solution.py:35
  637.2 52.2 %fusion.97 = bf16[8,8,8,8,64]{4,2,0,3,1:T(8,128)(2,1)S(1)} fusion(f32[8,8,8,8,24,24]{5,3,4,2,1,0:T(8,128)} %get-tuple-element.369, f32[8,8,8,8]{3,2,1,0:T(8,128)S(1)} %fusion.96, f32[8,8,8,8]{3,2,1,0:T(8,128)S(1)} %get-tuple-element.370, pred[24]{0:T(512)(128)(4,1)S(1)} %compare_and_fusion.5, bf16[24,8,24,8,64,1]{4,3,2,1,0,5:T(8,128)(2,1)} %bitcast.194), kind=kOutput, calls=%fused_computation.51.clone.1 | convolution fusion | flops 314048512 | bytes 14712856 | tf_op jit(solution)/shard_map/while/body/eval_jaxpr/nhabck,cnkhe->anbhe/dot_general | solution.py:50
  698.5 12.5 %reshape.283 = bf16[24,8,24,8,64]{4,3,2,1,0:T(8,128)(2,1)} reshape(bf16[24,8,3,8,512]{4,3,2,1,0:T(8,128)(2,1)} %pad_maximum_fusion.20) | data formatting | bytes 9437184 | tf_op jit(solution)/shard_map/while/body/eval_jaxpr/reshape | solution.py:35
  712.6 44.1 %fusion.95 = (f32[8,8,8,8]{3,2,1,0:T(8,128)S(1)}, f32[8,8,8,8,24,24]{5,3,4,2,1,0:T(8,128)}) fusion(pred[24]{0:T(512)(128)(4,1)S(1)} %compare_and_fusion.5, bf16[24,8,24,8,64,1]{4,3,2,1,0,5:T(8,128)(2,1)} %bitcast.192, bf16[8,8,8,8,64,1]{4,3,2,1,0,5:T(8,128)(2,1)S(1)} %bitcast.196), kind=kOutput, calls=%fused_computation.34.clone.1 | convolution fusion | flops 309063680 | bytes 14696472 | tf_op jit(solution)/shard_map/while/body/eval_jaxpr/anbhe,cnkhe->nhabck/dot_general | solution.py:39
  756.7 25.3 %fusion.96 = f32[8,8,8,8]{3,2,1,0:T(8,128)S(1)} fusion(f32[8,8,8,8,24,24]{5,3,4,2,1,0:T(8,128)} %get-tuple-element.369, f32[8,8,8,8]{3,2,1,0:T(8,128)S(1)} %get-tuple-element.370, pred[24]{0:T(512)(128)(4,1)S(1)} %compare_and_fusion.5), kind=kLoop, calls=%fused_computation.35.clone.1 | loop fusion | flops 9433088 | bytes 9469976 | tf_op jit(solution)/shard_map/while/body/eval_jaxpr/reduce_sum | solution.py:48
  784.9 12.5 %reshape.285 = bf16[24,8,24,8,64]{4,3,2,1,0:T(8,128)(2,1)} reshape(bf16[24,8,3,8,512]{4,3,2,1,0:T(8,128)(2,1)} %pad_maximum_fusion.21) | data formatting | bytes 9437184 | tf_op jit(solution)/shard_map/while/body/eval_jaxpr/reshape | solution.py:35
  797.3 52.2 %fusion.97 = bf16[8,8,8,8,64]{4,2,0,3,1:T(8,128)(2,1)S(1)} fusion(f32[8,8,8,8,24,24]{5,3,4,2,1,0:T(8,128)} %get-tuple-element.369, f32[8,8,8,8]{3,2,1,0:T(8,128)S(1)} %fusion.96, f32[8,8,8,8]{3,2,1,0:T(8,128)S(1)} %get-tuple-element.370, pred[24]{0:T(512)(128)(4,1)S(1)} %compare_and_fusion.5, bf16[24,8,24,8,64,1]{4,3,2,1,0,5:T(8,128)(2,1)} %bitcast.194), kind=kOutput, calls=%fused_computation.51.clone.1 | convolution fusion | flops 314048512 | bytes 14712856 | tf_op jit(solution)/shard_map/while/body/eval_jaxpr/nhabck,cnkhe->anbhe/dot_general | solution.py:50
  852.3 3.8 add_convert_fusion
  (148 shorter events, 97.7 us)
Async XLA Ops:
  0.0 18.3 %copy-start = (bf16[1024,256]{1,0:T(8,128)(2,1)S(1)}, bf16[1024,256]{1,0:T(8,128)(2,1)}, u32[]{:S(2)}) copy-start(bf16[1024,256]{1,0:T(8,128)(2,1)} %param.15) | copy-start | bytes 1572868
  0.0 1.3 copy-start.14
  0.0 1.7 copy-start.16
  0.0 1.7 copy-start.17
  0.0 18.3 %copy-start.23 = (bf16[256,512]{1,0:T(8,128)(2,1)S(1)}, bf16[256,512]{1,0:T(8,128)(2,1)}, u32[]{:S(2)}) copy-start(bf16[256,512]{1,0:T(8,128)(2,1)} %param.20) | copy-start | bytes 786436
  6.8 21.1 %all-to-all-start = ((s32[128,1,16]{2,1,0:T(1,128)}), s32[128,1,16]{2,1,0:T(1,128)S(1)}, u32[]{:S(2)}, u32[]{:S(2)}) async-start(s32[128,1,16]{2,1,0:T(1,128)} %bitcast.47), calls=%async_computation | async-start | bytes 131072 | tf_op jit(solution)/shard_map/all_to_all | solution.py:104
  25.8 9.8 %copy-start.18 = (f32[2,512]{1,0:T(2,128)S(1)}, f32[2,512]{1,0:T(2,128)}, u32[]{:S(2)}) copy-start(f32[2,512]{1,0:T(2,128)} %param.21) | copy-start | bytes 12292
  27.8 38.3 %all-to-all-start.1 = ((bf16[128,16,512]{2,1,0:T(8,128)(2,1)}), bf16[128,16,512]{2,1,0:T(8,128)(2,1)S(1)}, u32[]{:S(2)}, u32[]{:S(2)}) async-start(bf16[128,16,512]{2,1,0:T(8,128)(2,1)} %bitcast.49), calls=%async_computation.1 | async-start | bytes 4194304 | tf_op jit(solution)/shard_map/all_to_all | solution.py:97
  66.2 1.3 copy-start.5
  81.5 1.6 copy-start.4
  81.7 1.3 copy-start.2
  83.4 1.2 copy-start.19
  83.5 2.0 copy-start.21
  84.0 2.2 copy-start.12
  85.4 2.0 copy-start.6
  86.2 1.0 copy-start.8
  88.7 6.7 copy-start.7
  88.7 15.5 %collective-permute-start = (bf16[8,64,1024]{2,1,0:T(8,128)(2,1)}, bf16[8,64,1024]{2,1,0:T(8,128)(2,1)}, u32[]{:S(2)}, u32[]{:S(2)}) collective-permute-start(bf16[8,64,1024]{2,1,0:T(8,128)(2,1)} %bitcast.211), channel_id=1, source_target_pairs={{0,32},{32,64},{64,96},{1,33},{33,65},{65,97},{2,34},{34,66},{66,9... | collective-permute-start | bytes 3145736 | tf_op jit(solution)/shard_map/ppermute | solution.py:17
  93.2 28.5 %collective-permute-start.1 = (bf16[8,64,1024]{2,1,0:T(8,128)(2,1)}, bf16[8,64,1024]{2,1,0:T(8,128)(2,1)}, u32[]{:S(2)}, u32[]{:S(2)}) collective-permute-start(bf16[8,64,1024]{2,1,0:T(8,128)(2,1)} %bitcast.213), channel_id=1, source_target_pairs={{32,0},{64,32},{96,64},{33,1},{65,33},{97,65},{34,2},{66,34},{98,6... | collective-permute-start | bytes 3145736 | tf_op jit(solution)/shard_map/ppermute | solution.py:20
  123.7 12.6 %collective-permute-start.2 = (bf16[32,8,1024]{2,1,0:T(8,128)(2,1)}, bf16[32,8,1024]{2,1,0:T(8,128)(2,1)S(1)}, u32[]{:S(2)}, u32[]{:S(2)}) collective-permute-start(bf16[32,8,1024]{2,1,0:T(8,128)(2,1)} %get-tuple-element.239), channel_id=1, source_target_pairs={{0,1},{1,2},{2,3},{3,4},{4,5},{5,6},{6,7},{7,8},{8,9},{9,10},{10,1... | collective-permute-start | bytes 1572872 | tf_op jit(solution)/shard_map/ppermute | solution.py:17
  123.8 13.8 %collective-permute-start.3 = (bf16[32,8,1024]{2,1,0:T(8,128)(2,1)S(1)}, bf16[32,8,1024]{2,1,0:T(8,128)(2,1)}, u32[]{:S(2)}, u32[]{:S(2)}) collective-permute-start(bf16[32,8,1024]{2,1,0:T(8,128)(2,1)S(1)} %get-tuple-element.240), channel_id=1, source_target_pairs={{1,0},{2,1},{3,2},{4,3},{5,4},{6,5},{7,6},{8,7},{9,8},{10,9},{11,1... | collective-permute-start | bytes 1572872 | tf_op jit(solution)/shard_map/ppermute | solution.py:20
  465.4 3.2 copy-start.15
  468.6 2.8 copy-start.3
  468.6 2.0 copy-start.20
  468.6 2.8 copy-start.22
  468.9 2.5 copy-start.13
  471.4 2.0 copy-start.9
  472.2 1.0 copy-start.11
  474.7 7.2 copy-start.10
  474.7 16.8 %collective-permute-start.4 = (bf16[8,64,1024]{2,1,0:T(8,128)(2,1)}, bf16[8,64,1024]{2,1,0:T(8,128)(2,1)}, u32[]{:S(2)}, u32[]{:S(2)}) collective-permute-start(bf16[8,64,1024]{2,1,0:T(8,128)(2,1)} %bitcast.212), channel_id=1, source_target_pairs={{0,32},{32,64},{64,96},{1,33},{33,65},{65,97},{2,34},{34,66},{66,9... | collective-permute-start | bytes 3145736 | tf_op jit(solution)/shard_map/ppermute | solution.py:17
  479.9 29.2 %collective-permute-start.5 = (bf16[8,64,1024]{2,1,0:T(8,128)(2,1)}, bf16[8,64,1024]{2,1,0:T(8,128)(2,1)}, u32[]{:S(2)}, u32[]{:S(2)}) collective-permute-start(bf16[8,64,1024]{2,1,0:T(8,128)(2,1)} %bitcast.214), channel_id=1, source_target_pairs={{32,0},{64,32},{96,64},{33,1},{65,33},{97,65},{34,2},{66,34},{98,6... | collective-permute-start | bytes 3145736 | tf_op jit(solution)/shard_map/ppermute | solution.py:20
  511.1 12.6 %collective-permute-start.6 = (bf16[32,8,1024]{2,1,0:T(8,128)(2,1)}, bf16[32,8,1024]{2,1,0:T(8,128)(2,1)S(1)}, u32[]{:S(2)}, u32[]{:S(2)}) collective-permute-start(bf16[32,8,1024]{2,1,0:T(8,128)(2,1)} %get-tuple-element.237), channel_id=1, source_target_pairs={{0,1},{1,2},{2,3},{3,4},{4,5},{5,6},{6,7},{7,8},{8,9},{9,10},{10,1... | collective-permute-start | bytes 1572872 | tf_op jit(solution)/shard_map/ppermute | solution.py:17
  511.1 13.8 %collective-permute-start.7 = (bf16[32,8,1024]{2,1,0:T(8,128)(2,1)S(1)}, bf16[32,8,1024]{2,1,0:T(8,128)(2,1)}, u32[]{:S(2)}, u32[]{:S(2)}) collective-permute-start(bf16[32,8,1024]{2,1,0:T(8,128)(2,1)S(1)} %get-tuple-element.238), channel_id=1, source_target_pairs={{1,0},{2,1},{3,2},{4,3},{5,4},{6,5},{7,6},{8,7},{9,8},{10,9},{11,1... | collective-permute-start | bytes 1572872 | tf_op jit(solution)/shard_map/ppermute | solution.py:20
  852.3 3.8 copy-start.1
where the time goes:
time: 869 us; the launch traced here: 856 us
  matrix products  402 us (46%)
  local copies, waits for them, and re-layouts  172 us (20%)
  other arithmetic  166 us (19%)
  waiting for transfers between devices  70.2 us (8%)
  starting transfers between devices  41.8 us (5%)
    dot_general x4, matrix products, attend(): jnp.einsum('nhabck,cnkhe->anbhe', weights, value_tiles, preferred_element...  209 us
    dot_general x4, matrix products, attend(): jnp.einsum('anbhe,cnkhe->nhabck', q_five, key_tiles, preferred_element_ty...  176 us
    reduce_sum x4, other arithmetic, attend(): jnp.sum(expo, axis=-1, keepdims=True)  101 us
    reshape x8, local copies, waits for them, and re-layouts, tiles_of(): return stacked.reshape(24, blocks_row, 24, HEADS, head_size)  99.7 us
    ppermute x4, waiting for transfers between devices, with_halo(): lax.ppermute(lax.slice_in_dim(block, 0, width, axis=dim), axis, backward)  37.6 us
    another operation x8, other arithmetic, tiles_of(): stacked = jnp.stack([tiles[:, j:j + blocks_row] for j in range(3)], axis=2)  19.5 us
  transfers between devices with their start and end apart: 10, of which 10 were waited for; matrix products, arithmetic and copies ran while one was open for 5% of the time, Pallas kernels for 0%

commit v1 on v0

v1 whole, which is shorter than its diff:
```python
import jax
import jax.numpy as jnp
from jax import lax
from jax.experimental import pallas as pl
from jax.experimental.pallas import tpu as pltpu
from jax.sharding import PartitionSpec as P

HEADS = 8
LAYERS = 2
D = 512
FIN = 256
DEVICES = 128
CAP = 16
ROWS = 40
OBS = 1024
CELLS = 1024
SLOTS = DEVICES * CAP
BLOCK = 64
BANDS = 2
SECTORS = 8
FRAME = SECTORS + 2
GROUP = 256
KEYS = 9 * BLOCK
NEG = -1e30
F32 = jnp.float32
BF16 = jnp.bfloat16

VMEM = pl.BlockSpec(memory_space=pltpu.VMEM)
SMEM = pl.BlockSpec(memory_space=pltpu.SMEM)
ANY = pl.BlockSpec(memory_space=pl.ANY)
PARAMS = pltpu.CompilerParams(vmem_limit_bytes=56 * 1024 * 1024)
NT = (((1,), (1,)), ((), ()))


def iota(shape, axis):
    return lax.broadcasted_iota(jnp.int32, shape, axis)


def dispatch_kernel(owner_ref, cell_ref, valid_ref, feat_ref, send_ref):
    owner = owner_ref[...]
    cell = cell_ref[...]
    valid = valid_ref[...]
    wide = 256
    earlier = (iota((wide, wide), 0) < iota((wide, wide), 1)).astype(F32).astype(BF16)
    carry = jnp.zeros((DEVICES, 1), F32)
    ranks = []
    chosen = []
    for at in range(0, OBS, wide):
        hot = (iota((DEVICES, wide), 0) == owner[:, at : at + wide]).astype(F32)
        before = jnp.dot(hot.astype(BF16), earlier, preferred_element_type=F32) + carry
        ranks.append(jnp.sum(hot * before, axis=0, keepdims=True))
        carry = carry + jnp.sum(hot, axis=1, keepdims=True)
        chosen.append(hot.astype(BF16))
    rank = jnp.concatenate(ranks, axis=1).astype(jnp.int32)
    hot_all = jnp.concatenate(chosen, axis=1)
    row = cell // 64
    col = cell % 64
    high = (row // 8) * SECTORS + col // 8 + 1
    low = (row % 8) * 8 + col % 8
    usable = valid == 1
    high = jnp.where(usable, high, 0)
    low = jnp.where(usable, low, 0)
    lane = iota((128, OBS), 0)
    part = jnp.where(lane < CAP, high, jnp.where(lane < 2 * CAP, low, 0))
    entry = jnp.where(lane % CAP == rank, part, 0).astype(F32).astype(BF16)
    tags = lax.dot_general(hot_all, entry, NT, preferred_element_type=F32)
    send_ref[:, 32:40, :] = jnp.broadcast_to(tags[:, None, :], (DEVICES, 8, 128)).astype(BF16)
    target = owner * CAP + rank
    feat = feat_ref[...]
    step = 256
    for at in range(0, SLOTS, step):
        pick = (iota((step, OBS), 0) + at == target).astype(F32).astype(BF16)
        rows = jnp.dot(pick, feat, preferred_element_type=F32).astype(BF16)
        first = at // CAP
        count = step // CAP
        send_ref[first : first + count, 0:16, :] = rows[:, :128].reshape(count, CAP, 128)
        send_ref[first : first + count, 16:32, :] = rows[:, 128:].reshape(count, CAP, 128)


def dispatch(owner, cell, valid, feat):
    return pl.pallas_call(
        dispatch_kernel,
        out_shape=jax.ShapeDtypeStruct((DEVICES, ROWS, 128), BF16),
        in_specs=[VMEM] * 4,
        out_specs=VMEM,
        compiler_params=PARAMS,
        name="dispatch",
    )(owner, cell, valid, feat)


def norm_rows(hidden, gain):
    scale = lax.rsqrt(jnp.mean(hidden * hidden, axis=-1, keepdims=True) + 1e-06)
    return (hidden * scale * gain).astype(BF16)


def combine_kernel(got_ref, embed_ref, grid_ref, gain_ref, hidden_ref, normed_ref, emb_ref, tag_ref):
    step = 512
    for at in range(0, SLOTS, step):
        first = at // CAP
        count = step // CAP
        left = got_ref[first : first + count, 0:16, :].reshape(step, 128)
        right = got_ref[first : first + count, 16:32, :].reshape(step, 128)
        raw = jnp.concatenate([left, right], axis=1)
        product = jnp.dot(raw, embed_ref[...], preferred_element_type=F32)
        emb_ref[at : at + step, :] = jax.nn.gelu(product).astype(BF16)
    tag_ref[...] = got_ref[:, 32:40, :].astype(F32).reshape(DEVICES * 8, 128)
    tags = tag_ref[pl.ds(0, DEVICES, stride=8), :]
    tags = jnp.transpose(tags)[: 2 * CAP].astype(BF16)
    spread = (iota((DEVICES, SLOTS), 1) // CAP == iota((DEVICES, SLOTS), 0)).astype(F32).astype(BF16)
    wide = jnp.dot(tags, spread, preferred_element_type=F32)
    own = iota((CAP, SLOTS), 1) % CAP == iota((CAP, SLOTS), 0)
    high = jnp.sum(jnp.where(own, wide[:CAP], 0.0), axis=0, keepdims=True)
    low = jnp.sum(jnp.where(own, wide[CAP:], 0.0), axis=0, keepdims=True)
    index = jnp.where(high > 0.5, (high - 1.0) * 64.0 + low, -1.0).astype(jnp.int32)
    size = 128
    for at in range(0, CELLS, size):
        hot = (iota((size, SLOTS), 0) + at == index).astype(F32)
        count = jnp.sum(hot, axis=1, keepdims=True)
        total = jnp.dot(hot.astype(BF16), emb_ref[...], preferred_element_type=F32)
        hidden_ref[at : at + size, :] = total / jnp.maximum(count, 1.0)
    for band in range(BANDS):
        for r in range(8):
            static = grid_ref[band * 8 + r].astype(F32)
            for sector in range(SECTORS):
                at = (band * SECTORS + sector) * BLOCK + r * 8
                hidden_ref[at : at + 8, :] += static[sector * 8 : sector * 8 + 8]
    gain = gain_ref[0:1, :]
    for at in range(0, CELLS, 128):
        normed_ref[at : at + 128, :] = norm_rows(hidden_ref[at : at + 128, :], gain)


def combine(got, w_embed, grid_feat, gains):
    return pl.pallas_call(
        combine_kernel,
        out_shape=(
            jax.ShapeDtypeStruct((CELLS, D), F32),
            jax.ShapeDtypeStruct((CELLS, D), BF16),
        ),
        in_specs=[VMEM] * 4,
        out_specs=(VMEM, VMEM),
        scratch_shapes=[pltpu.VMEM((SLOTS, D), BF16), pltpu.VMEM((DEVICES * 8, 128), F32)],
        compiler_params=PARAMS,
        name="combine",
    )(got, w_embed, grid_feat, gains)


def project_kernel(normed_ref, query_w, key_w, value_w, query_ref, key_ref, value_ref):
    flat = normed_ref[...]
    query = jnp.dot(flat, query_w[0], preferred_element_type=F32).astype(BF16)
    query_ref[...] = query * BF16(0.125)
    key_ref[...] = jnp.dot(flat, key_w[0], preferred_element_type=F32).astype(BF16)
    value_ref[...] = jnp.dot(flat, value_w[0], preferred_element_type=F32).astype(BF16)


def layer_spec(layer):
    return pl.BlockSpec((1, D, D), lambda i: (layer, 0, 0))


def project(normed, w_query, w_key, w_value, layer):
    whole = pl.BlockSpec((CELLS, D), lambda i: (0, 0))
    shape = jax.ShapeDtypeStruct((CELLS, D), BF16)
    return pl.pallas_call(
        project_kernel,
        grid=(1,),
        out_shape=(shape, shape, shape),
        in_specs=[whole] + [layer_spec(layer)] * 3,
        out_specs=(whole, whole, whole),
        compiler_params=PARAMS,
        name="project",
    )(normed, w_query, w_key, w_value)


def make_attend_kernel(last):
    def attend_kernel(
        lat_ref, query_ref, key_ref, value_ref, up_ref, down_ref, west_ref, east_ref,
        hidden_ref, gain_ref, key_w, value_w, out_w, *rest,
    ):
        if last:
            out_ref, key_f, value_f, att_ref, new_ref, sems = rest
        else:
            new_ref, normed_ref, key_f, value_f, att_ref, sems = rest
        copies = []
        for band in range(BANDS):
            for which, (source, frame) in enumerate(((key_ref, key_f), (value_ref, value_f))):
                copy = pltpu.make_async_copy(
                    source.at[pl.ds(band * SECTORS * BLOCK, SECTORS * BLOCK)],
                    frame.at[pl.ds(((band + 1) * FRAME + 1) * BLOCK, SECTORS * BLOCK)],
                    sems.at[band * 2 + which],
                )
                copy.start()
                copies.append(copy)
        for weight, frame in ((key_w, key_f), (value_w, value_f)):
            for source, row in ((up_ref, 0), (down_ref, BANDS + 1)):
                at = (row * FRAME + 1) * BLOCK
                frame[at : at + SECTORS * BLOCK, :] = jnp.dot(
                    source[...], weight[0], preferred_element_type=F32
                ).astype(BF16)
            for source, column in ((west_ref, 0), (east_ref, FRAME - 1)):
                done = jnp.dot(source[...], weight[0], preferred_element_type=F32).astype(BF16)
                for row in range(BANDS + 2):
                    at = (row * FRAME + column) * BLOCK
                    frame[at : at + BLOCK, :] = done[row * BLOCK : (row + 1) * BLOCK]
        for copy in copies:
            copy.wait()
        first = lat_ref[0] == 0
        final = lat_ref[0] == lat_ref[1] - 1
        lane_key = iota((1, KEYS), 1)

        def one_block(index, carry):
            band = index // SECTORS
            sector = index % SECTORS
            hide_top = jnp.where(first & (band == 0), 3 * BLOCK, 0)
            hide_low = jnp.where(final & (band == BANDS - 1), 6 * BLOCK, KEYS)
            bias = jnp.where((lane_key < hide_top) | (lane_key >= hide_low), NEG, 0.0).astype(F32)
            base = pl.multiple_of(index * BLOCK, BLOCK)
            corner = pl.multiple_of((band * FRAME + sector) * BLOCK, BLOCK)
            for group in range(2):
                lanes = slice(group * GROUP, (group + 1) * GROUP)
                query = query_ref[pl.ds(base, BLOCK), lanes]
                stacked = jnp.concatenate([query] * 4, axis=0)
                diagonal = iota((GROUP, GROUP), 0) // BLOCK == iota((GROUP, GROUP), 1) // BLOCK
                stacked = jnp.where(diagonal, stacked, jnp.zeros_like(stacked))
                keys = jnp.concatenate(
                    [key_f[pl.ds(corner + a * FRAME * BLOCK, 3 * BLOCK), lanes] for a in range(3)], axis=0
                )
                values = jnp.concatenate(
                    [value_f[pl.ds(corner + a * FRAME * BLOCK, 3 * BLOCK), lanes] for a in range(3)], axis=0
                )
                scores = lax.dot_general(stacked, keys, NT, preferred_element_type=F32) + bias
                highest = jnp.max(scores, axis=-1, keepdims=True)
                expo = jnp.exp(scores - highest)
                inverse = 1.0 / jnp.sum(expo, axis=-1, keepdims=True)
                weights = (expo * inverse).astype(BF16)
                mixed = jnp.dot(weights, values, preferred_element_type=F32)
                half = iota((BLOCK, 128), 1) < BLOCK
                for pair in range(2):
                    columns = slice(pair * 128, pair * 128 + 128)
                    low = mixed[pair * 128 : pair * 128 + BLOCK, columns]
                    high = mixed[pair * 128 + BLOCK : pair * 128 + 128, columns]
                    to = group * GROUP + pair * 128
                    att_ref[pl.ds(base, BLOCK), to : to + 128] = jnp.where(half, low, high).astype(BF16)
            return carry

        lax.fori_loop(0, BANDS * SECTORS, one_block, 0)
        gain = gain_ref[...]
        for at in range(0, CELLS, 256):
            update = jnp.dot(att_ref[at : at + 256, :], out_w[0], preferred_element_type=F32)
            hidden = hidden_ref[at : at + 256, :] + update
            new_ref[at : at + 256, :] = hidden
            if not last:
                normed_ref[at : at + 256, :] = norm_rows(hidden, gain)
        if last:
            for band in range(BANDS):
                for r in range(8):
                    pieces = []
                    for sector in range(SECTORS):
                        at = (band * SECTORS + sector) * BLOCK + r * 8
                        pieces.append(new_ref[at : at + 8, :])
                    out_ref[band * 8 + r] = jnp.concatenate(pieces, axis=0).astype(BF16)

    return attend_kernel


def attend(place, query, key, value, up, down, west, east, hidden, gain, w_key, w_value, w_out, layer):
    last = layer == LAYERS - 1

    def whole(shape):
        return pl.BlockSpec(shape, lambda i: (0,) * len(shape))

    cells = whole((CELLS, D))
    scratch = [
        pltpu.VMEM(((BANDS + 2) * FRAME * BLOCK, D), BF16),
        pltpu.VMEM(((BANDS + 2) * FRAME * BLOCK, D), BF16),
        pltpu.VMEM((CELLS, D), BF16),
    ]
    if last:
        scratch.append(pltpu.VMEM((CELLS, D), F32))
        out_shape = jax.ShapeDtypeStruct((16, 64, D), BF16)
        out_specs = whole((16, 64, D))
    else:
        out_shape = (jax.ShapeDtypeStruct((CELLS, D), F32), jax.ShapeDtypeStruct((CELLS, D), BF16))
        out_specs = (cells, cells)
    scratch.append(pltpu.SemaphoreType.DMA((4,)))
    halo = SECTORS * BLOCK
    side = (BANDS + 2) * BLOCK
    return pl.pallas_call(
        make_attend_kernel(last),
        grid=(1,),
        out_shape=out_shape,
        in_specs=[
            SMEM, cells, ANY, ANY,
            whole((halo, D)), whole((halo, D)), whole((side, D)), whole((side, D)),
            cells, whole((1, D)),
        ] + [layer_spec(layer)] * 3,
        out_specs=out_specs,
        scratch_shapes=scratch,
        compiler_params=PARAMS,
        name="attend",
    )(place, query, key, value, up, down, west, east, hidden, gain, w_key, w_value, w_out)


def neighbours(normed):
    lat_count = lax.axis_size("lat")
    lon_count = lax.axis_size("lon")
    halo = SECTORS * BLOCK
    rising = [(i, i + 1) for i in range(lat_count - 1)]
    falling = [(b, a) for a, b in rising]
    up = lax.ppermute(normed[halo:], "lat", rising)
    down = lax.ppermute(normed[:halo], "lat", falling)
    forward = [(i, (i + 1) % lon_count) for i in range(lon_count)]
    backward = [(b, a) for a, b in forward]
    edge = halo - BLOCK
    eastern = jnp.concatenate([up[edge:], normed[edge:halo], normed[halo + edge :], down[edge:]], axis=0)
    western = jnp.concatenate(
        [up[:BLOCK], normed[:BLOCK], normed[halo : halo + BLOCK], down[:BLOCK]], axis=0
    )
    west = lax.ppermute(eastern, "lon", forward)
    east = lax.ppermute(western, "lon", backward)
    return up, down, west, east


def local(
    obs_feat, obs_owner, obs_cell, obs_valid, grid_feat,
    w_embed, gains, w_query, w_key, w_value, w_out,
):
    send = dispatch(
        obs_owner.reshape(1, OBS), obs_cell.reshape(1, OBS), obs_valid.reshape(1, OBS), obs_feat
    )
    got = lax.all_to_all(send, ("lat", "lon"), split_axis=0, concat_axis=0, tiled=True)
    hidden, normed = combine(got, w_embed, grid_feat, gains)
    place = jnp.stack([lax.axis_index("lat"), jnp.int32(lax.axis_size("lat"))])
    for layer in range(LAYERS):
        up, down, west, east = neighbours(normed)
        query, key, value = project(normed, w_query, w_key, w_value, layer)
        following = min(layer + 1, LAYERS - 1)
        result = attend(
            place, query, key, value, up, down, west, east, hidden,
            gains[following : following + 1], w_key, w_value, w_out, layer,
        )
        if layer < LAYERS - 1:
            hidden, normed = result
    return result


def solution(mesh):
    placed = (
        P(("lat", "lon"), None),
        P(("lat", "lon"), None),
        P(("lat", "lon")),
        P(("lat", "lon")),
        P("lat", "lon", None),
        P(), P(), P(), P(), P(), P(),
    )
    return jax.shard_map(
        local, mesh=mesh, in_specs=placed, out_specs=P("lat", "lon", None), check_vma=False
    )
```

time: 869 us -> 158 us (0.18); the launches traced: 856 us -> 158 us
  matrix products: 402 us -> 0 us
  other arithmetic: 166 us -> 0.74 us
  local copies, waits for them, and re-layouts: 172 us -> 6.75 us
  Pallas kernels: 0 us -> 69.1 us
  waiting for transfers between devices: 70.2 us -> 19.8 us
  blocking collectives: 0 us -> 33.8 us
  starting transfers between devices: 41.8 us -> 27.2 us
    dot_general x17 -> x0, matrix products: 402 us -> none  [the longest x4 209 us: attend(): jnp.einsum('nhabck,cnkhe->anbhe', weights, value_tiles, preferred_element...]
    reshape x17 -> x0, local copies, waits for them, and re-layouts: 112 us -> none  [the longest x8 99.7 us: tiles_of(): return stacked.reshape(24, blocks_row, 24, HEADS, head_size)]
    reduce_sum x6 -> x0, other arithmetic: 102 us -> none  [the longest x4 101 us: attend(): jnp.sum(expo, axis=-1, keepdims=True)]
    pallas_call x0 -> x6, Pallas kernels: none -> 69.1 us  [the longest x2 48.2 us: attend(): pl.pallas_call(make_attend_kernel(last), grid=(1,), out_shape=out_shape,...]
    all_to_all x0 -> x1, blocking collectives: none -> 33.8 us  [local(): lax.all_to_all(send, ('lat', 'lon'), split_axis=0, concat_axis=0, tiled=T...]
    ppermute x8, waiting for transfers between devices: 52.4 us -> 19.8 us  [the longest x2 18.2 us: neighbours(): down = lax.ppermute(normed[:halo], 'lat', falling)]
    scatter-add x2 -> x0, other arithmetic: 26.8 us -> none  [the longest x1 14 us: local(): jax.ops.segment_sum(got_rows.astype(jnp.float32), safe_tags, num_segments...]
    all_to_all x2 -> x0, starting transfers between devices: 19.2 us -> none  [the longest x1 11.5 us: local(): lax.all_to_all(send_tags.reshape(devices, capacity), ('lat', 'lon'), spli...]
  transfers between devices with their start and end apart: 10 -> 8, of which waited for: 10 -> 3; matrix products, arithmetic and copies ran while one was open for 5% -> 2% of each run, Pallas kernels for 0% -> 6%
where the time goes in v1:
time: 158 us
  Pallas kernels  69.1 us (44%)
  blocking collectives  33.8 us (21%)
  starting transfers between devices  27.2 us (17%)
  waiting for transfers between devices  19.8 us (13%)
  local copies, waits for them, and re-layouts  6.75 us (4%)
    pallas_call x2, Pallas kernels, attend(): pl.pallas_call(make_attend_kernel(last), grid=(1,), out_shape=out_shape,...  48.2 us
    all_to_all x1, blocking collectives, local(): lax.all_to_all(send, ('lat', 'lon'), split_axis=0, concat_axis=0, tiled=T...  33.8 us
    ppermute x2, waiting for transfers between devices, neighbours(): down = lax.ppermute(normed[:halo], 'lat', falling)  18.2 us
    ppermute x2, starting transfers between devices, neighbours(): east = lax.ppermute(western, 'lon', backward)  11.6 us
    ppermute x2, starting transfers between devices, neighbours(): up = lax.ppermute(normed[halo:], 'lat', rising)  11.2 us
    pallas_call x2, Pallas kernels, project(): pl.pallas_call(project_kernel, grid=(1,), out_shape=(shape, shape, shape)...  8.91 us
    pallas_call x1, Pallas kernels, combine(): pl.pallas_call(combine_kernel, out_shape=(jax.ShapeDtypeStruct((CELLS, D)...  8.31 us
    ppermute x2, starting transfers between devices, neighbours(): down = lax.ppermute(normed[:halo], 'lat', falling)  4.23 us
  transfers between devices with their start and end apart: 8, of which 3 were waited for; matrix products, arithmetic and copies ran while one was open for 2% of the time, Pallas kernels for 6%

profile of v1, /device:TPU:1, one launch (start us, length us, event | category | flops | bytes accessed | tf_op | source)
XLA Modules:
  0.0 157.8 jit_solution(16311449005718947527)
XLA Ops:
  0.0 3.7 %dispatch.1 = bf16[128,40,128]{2,1,0:T(8,128)(2,1)} custom-call(s32[1,1024]{1,0:T(1,128)} %bitcast.4, s32[1,1024]{1,0:T(1,128)} %bitcast.5, s32[1,1024]{1,0:T(1,128)} %bitcast.6, bf16[1024,256]{1,0:T(8,128)(2,1)} %feat_ref.1), custom_call_target="tpu_custom_call" | custom-call | tf_op jit(solution)/shard_map/dispatch/pallas_call | solution.py:81
  3.7 33.8 %all_to_all.5.got_ref = bf16[128,40,128]{2,1,0:T(8,128)(2,1)} all-to-all(bf16[128,40,128]{2,1,0:T(8,128)(2,1)} %dispatch.1), channel_id=1, replica_groups=mesh['lat'=4,'lon'=32] {'lat','lon'}, dimensions={0} | all-to-all | bytes 2621440 | tf_op jit(solution)/shard_map/all_to_all | solution.py:329
  37.5 8.3 %combine.1 = (f32[1024,512]{1,0:T(8,128)}, bf16[1024,512]{1,0:T(8,128)(2,1)}) custom-call(bf16[128,40,128]{2,1,0:T(8,128)(2,1)} %all_to_all.5.got_ref, bf16[256,512]{1,0:T(8,128)(2,1)} %embed_ref.1, bf16[16,64,512]{2,1,0:T(8,128)(2,1)} %grid_ref.1, f32[2,512]{1,0:T(2,128)} %gain_ref.1), custom_call_target="tpu_custom_call" | custom-call | tf_op jit(solution)/shard_map/combine/pallas_call | solution.py:133
  45.8 0.0 copy-start.8
  45.8 1.3 fusion.3
  47.1 2.3 %collective-permute-start.1 = (bf16[512,512]{1,0:T(8,128)(2,1)S(1)}, bf16[512,512]{1,0:T(8,128)(2,1)S(1)}, u32[]{:S(2)}, u32[]{:S(2)}) collective-permute-start(bf16[512,512]{1,0:T(8,128)(2,1)S(1)} %get-tuple-element.35), channel_id=1, source_target_pairs={{32,0},{64,32},{96,64},{33,1},{65,33},{97,65},{34,2},{66,34},{98,6... | collective-permute-start | bytes 1572872 | tf_op jit(solution)/shard_map/ppermute | solution.py:309
  49.4 4.8 %collective-permute-start = (bf16[512,512]{1,0:T(8,128)(2,1)S(1)}, bf16[512,512]{1,0:T(8,128)(2,1)S(1)}, u32[]{:S(2)}, u32[]{:S(2)}) collective-permute-start(bf16[512,512]{1,0:T(8,128)(2,1)S(1)} %get-tuple-element.36), channel_id=1, source_target_pairs={{0,32},{32,64},{64,96},{1,33},{33,65},{65,97},{2,34},{34,66},{66,9... | collective-permute-start | bytes 1572872 | tf_op jit(solution)/shard_map/ppermute | solution.py:308
  54.2 1.0 fusion.2
  55.2 9.1 %collective-permute-done.1.down_ref = bf16[512,512]{1,0:T(8,128)(2,1)S(1)} collective-permute-done((bf16[512,512]{1,0:T(8,128)(2,1)S(1)}, bf16[512,512]{1,0:T(8,128)(2,1)S(1)}, u32[]{:S(2)}, u32[]{:S(2)}) %collective-permute-start.1) | collective-permute-done | bytes 524320 | tf_op jit(solution)/shard_map/ppermute | solution.py:309
  64.3 0.0 copy-start
  64.3 1.6 %collective-permute-done.up_ref = bf16[512,512]{1,0:T(8,128)(2,1)S(1)} collective-permute-done((bf16[512,512]{1,0:T(8,128)(2,1)S(1)}, bf16[512,512]{1,0:T(8,128)(2,1)S(1)}, u32[]{:S(2)}, u32[]{:S(2)}) %collective-permute-start) | collective-permute-done | bytes 524320 | tf_op jit(solution)/shard_map/ppermute | solution.py:308
  65.9 0.0 copy-start.1
  66.0 0.1 collective-permute-start.2
  66.1 5.9 %collective-permute-start.3 = (bf16[256,512]{1,0:T(8,128)(2,1)S(1)}, bf16[256,512]{1,0:T(8,128)(2,1)S(1)}, u32[]{:S(2)}, u32[]{:S(2)}) collective-permute-start(bf16[256,512]{1,0:T(8,128)(2,1)S(1)} %pad_maximum_fusion.1), channel_id=1, source_target_pairs={{1,0},{2,1},{3,2},{4,3},{5,4},{6,5},{7,6},{8,7},{9,8},{10,9},{11,1... | collective-permute-start | bytes 786440 | tf_op jit(solution)/shard_map/ppermute | solution.py:318
  72.0 0.0 copy-done.8
  72.0 0.6 slice.74.gain_ref
  72.6 0.7 pad_add_fusion.lat_ref
  73.2 4.4 %project.2 = (bf16[1024,512]{1,0:T(8,128)(2,1)}, bf16[1024,512]{1,0:T(8,128)(2,1)}, bf16[1024,512]{1,0:T(8,128)(2,1)}) custom-call(bf16[1024,512]{1,0:T(8,128)(2,1)} %get-tuple-element.15.normed_ref, bf16[2,512,512]{2,1,0:T(8,128)(2,1)} %query_w.3, bf16[2,512,512]{2,1,0:T(8,128)(2,1)} %key_w.7, bf16[2,512,512]{2,1,0:T(8,128)(2,1)} %value_w.7), custom_call_target="tpu_custom_call" | custom-call | tf_op jit(solution)/shard_map/project/pallas_call | solution.py:162
  77.7 0.0 copy-done
  77.7 0.0 copy-done.1
  77.7 0.0 collective-permute-done.2.west_ref
  77.7 0.0 copy-start.4
  77.7 0.0 collective-permute-done.3.east_ref
  77.7 0.0 copy-start.5
  77.7 0.7 copy-done.4
  78.4 0.1 copy-done.5
  78.6 24.4 %attend.2 = (f32[1024,512]{1,0:T(8,128)}, bf16[1024,512]{1,0:T(8,128)(2,1)}) custom-call(s32[2]{0:T(128)} %pad_add_fusion.lat_ref, bf16[1024,512]{1,0:T(8,128)(2,1)} %get-tuple-element.16.query_ref, bf16[1024,512]{1,0:T(8,128)(2,1)} %get-tuple-element.17.key_ref, bf16[1024,512]{1,0:T(8,128)(2,1)} %get-tuple-element.18.value_ref, bf16[512,512]{1,0:T(8,128)(2,1)} %copy-done.1, ...), custom_call_target="tpu_custom_call" | custom-call | tf_op jit(solution)/shard_map/attend/pallas_call | solution.py:286
  103.0 1.3 fusion.1
  104.3 1.9 %collective-permute-start.5 = (bf16[512,512]{1,0:T(8,128)(2,1)S(1)}, bf16[512,512]{1,0:T(8,128)(2,1)S(1)}, u32[]{:S(2)}, u32[]{:S(2)}) collective-permute-start(bf16[512,512]{1,0:T(8,128)(2,1)S(1)} %get-tuple-element.29), channel_id=1, source_target_pairs={{32,0},{64,32},{96,64},{33,1},{65,33},{97,65},{34,2},{66,34},{98,6... | collective-permute-start | bytes 1572872 | tf_op jit(solution)/shard_map/ppermute | solution.py:309
  106.2 6.5 %collective-permute-start.4 = (bf16[512,512]{1,0:T(8,128)(2,1)S(1)}, bf16[512,512]{1,0:T(8,128)(2,1)S(1)}, u32[]{:S(2)}, u32[]{:S(2)}) collective-permute-start(bf16[512,512]{1,0:T(8,128)(2,1)S(1)} %get-tuple-element.30), channel_id=1, source_target_pairs={{0,32},{32,64},{64,96},{1,33},{33,65},{65,97},{2,34},{34,66},{66,9... | collective-permute-start | bytes 1572872 | tf_op jit(solution)/shard_map/ppermute | solution.py:308
  112.7 1.0 fusion
  113.6 9.1 %collective-permute-done.5.down_ref = bf16[512,512]{1,0:T(8,128)(2,1)S(1)} collective-permute-done((bf16[512,512]{1,0:T(8,128)(2,1)S(1)}, bf16[512,512]{1,0:T(8,128)(2,1)S(1)}, u32[]{:S(2)}, u32[]{:S(2)}) %collective-permute-start.5) | collective-permute-done | bytes 524320 | tf_op jit(solution)/shard_map/ppermute | solution.py:309
  122.7 0.0 copy-start.2
  122.7 0.0 collective-permute-done.4.up_ref
  122.7 0.0 copy-start.3
  122.8 0.1 collective-permute-start.6
  122.9 5.7 %collective-permute-start.7 = (bf16[256,512]{1,0:T(8,128)(2,1)S(1)}, bf16[256,512]{1,0:T(8,128)(2,1)S(1)}, u32[]{:S(2)}, u32[]{:S(2)}) collective-permute-start(bf16[256,512]{1,0:T(8,128)(2,1)S(1)} %pad_maximum_fusion.3), channel_id=1, source_target_pairs={{1,0},{2,1},{3,2},{4,3},{5,4},{6,5},{7,6},{8,7},{9,8},{10,9},{11,1... | collective-permute-start | bytes 786440 | tf_op jit(solution)/shard_map/ppermute | solution.py:318
  128.6 4.5 %project.3 = (bf16[1024,512]{1,0:T(8,128)(2,1)}, bf16[1024,512]{1,0:T(8,128)(2,1)}, bf16[1024,512]{1,0:T(8,128)(2,1)}) custom-call(bf16[1024,512]{1,0:T(8,128)(2,1)} %get-tuple-element.20.normed_ref, bf16[2,512,512]{2,1,0:T(8,128)(2,1)} %query_w.3, bf16[2,512,512]{2,1,0:T(8,128)(2,1)} %key_w.7, bf16[2,512,512]{2,1,0:T(8,128)(2,1)} %value_w.7), custom_call_target="tpu_custom_call" | custom-call | tf_op jit(solution)/shard_map/project/pallas_call | solution.py:162
  133.1 0.0 copy-done.2
  133.1 0.0 copy-done.3
  133.1 0.0 collective-permute-done.6.west_ref
  133.1 0.0 copy-start.6
  133.1 0.0 collective-permute-done.7.east_ref
  133.1 0.0 copy-start.7
  133.1 0.7 copy-done.6
  133.8 0.1 copy-done.7
  133.9 23.7 %attend.3 = bf16[16,64,512]{2,1,0:T(8,128)(2,1)} custom-call(s32[2]{0:T(128)} %pad_add_fusion.lat_ref, bf16[1024,512]{1,0:T(8,128)(2,1)} %get-tuple-element.21.query_ref, bf16[1024,512]{1,0:T(8,128)(2,1)} %get-tuple-element.22.key_ref, bf16[1024,512]{1,0:T(8,128)(2,1)} %get-tuple-element.23.value_ref, bf16[512,512]{1,0:T(8,128)(2,1)} %copy-done.3, ...), custom_call_target="tpu_custom_call" | custom-call | tf_op jit(solution)/shard_map/attend/pallas_call | solution.py:286
  (8 shorter events, 0.1 us)
Async XLA Ops:
  45.8 26.2 %copy-start.8 = (f32[2,512]{1,0:T(2,128)S(1)}, f32[2,512]{1,0:T(2,128)}, u32[]{:S(2)}) copy-start(f32[2,512]{1,0:T(2,128)} %gain_ref.1) | copy-start | bytes 12292
  47.1 17.2 %collective-permute-start.1 = (bf16[512,512]{1,0:T(8,128)(2,1)S(1)}, bf16[512,512]{1,0:T(8,128)(2,1)S(1)}, u32[]{:S(2)}, u32[]{:S(2)}) collective-permute-start(bf16[512,512]{1,0:T(8,128)(2,1)S(1)} %get-tuple-element.35), channel_id=1, source_target_pairs={{32,0},{64,32},{96,64},{33,1},{65,33},{97,65},{34,2},{66,34},{98,6... | collective-permute-start | bytes 1572872 | tf_op jit(solution)/shard_map/ppermute | solution.py:309
  49.4 16.5 %collective-permute-start = (bf16[512,512]{1,0:T(8,128)(2,1)S(1)}, bf16[512,512]{1,0:T(8,128)(2,1)S(1)}, u32[]{:S(2)}, u32[]{:S(2)}) collective-permute-start(bf16[512,512]{1,0:T(8,128)(2,1)S(1)} %get-tuple-element.36), channel_id=1, source_target_pairs={{0,32},{32,64},{64,96},{1,33},{33,65},{65,97},{2,34},{34,66},{66,9... | collective-permute-start | bytes 1572872 | tf_op jit(solution)/shard_map/ppermute | solution.py:308
  64.3 13.4 %copy-start = (bf16[512,512]{1,0:T(8,128)(2,1)}, bf16[512,512]{1,0:T(8,128)(2,1)S(1)}, u32[]{:S(2)}) copy-start(bf16[512,512]{1,0:T(8,128)(2,1)S(1)} %collective-permute-done.1.down_ref) | copy-start | bytes 1572868
  65.9 11.8 %copy-start.1 = (bf16[512,512]{1,0:T(8,128)(2,1)}, bf16[512,512]{1,0:T(8,128)(2,1)S(1)}, u32[]{:S(2)}) copy-start(bf16[512,512]{1,0:T(8,128)(2,1)S(1)} %collective-permute-done.up_ref) | copy-start | bytes 1572868
  66.0 11.7 %collective-permute-start.2 = (bf16[256,512]{1,0:T(8,128)(2,1)S(1)}, bf16[256,512]{1,0:T(8,128)(2,1)S(1)}, u32[]{:S(2)}, u32[]{:S(2)}) collective-permute-start(bf16[256,512]{1,0:T(8,128)(2,1)S(1)} %pad_maximum_fusion), channel_id=1, source_target_pairs={{0,1},{1,2},{2,3},{3,4},{4,5},{5,6},{6,7},{7,8},{8,9},{9,10},{10,1... | collective-permute-start | bytes 786440 | tf_op jit(solution)/shard_map/ppermute | solution.py:317
  66.1 11.6 %collective-permute-start.3 = (bf16[256,512]{1,0:T(8,128)(2,1)S(1)}, bf16[256,512]{1,0:T(8,128)(2,1)S(1)}, u32[]{:S(2)}, u32[]{:S(2)}) collective-permute-start(bf16[256,512]{1,0:T(8,128)(2,1)S(1)} %pad_maximum_fusion.1), channel_id=1, source_target_pairs={{1,0},{2,1},{3,2},{4,3},{5,4},{6,5},{7,6},{8,7},{9,8},{10,9},{11,1... | collective-permute-start | bytes 786440 | tf_op jit(solution)/shard_map/ppermute | solution.py:318
  77.7 0.7 copy-start.4
  77.7 0.8 copy-start.5
  104.3 18.4 %collective-permute-start.5 = (bf16[512,512]{1,0:T(8,128)(2,1)S(1)}, bf16[512,512]{1,0:T(8,128)(2,1)S(1)}, u32[]{:S(2)}, u32[]{:S(2)}) collective-permute-start(bf16[512,512]{1,0:T(8,128)(2,1)S(1)} %get-tuple-element.29), channel_id=1, source_target_pairs={{32,0},{64,32},{96,64},{33,1},{65,33},{97,65},{34,2},{66,34},{98,6... | collective-permute-start | bytes 1572872 | tf_op jit(solution)/shard_map/ppermute | solution.py:309
  106.2 16.5 %collective-permute-start.4 = (bf16[512,512]{1,0:T(8,128)(2,1)S(1)}, bf16[512,512]{1,0:T(8,128)(2,1)S(1)}, u32[]{:S(2)}, u32[]{:S(2)}) collective-permute-start(bf16[512,512]{1,0:T(8,128)(2,1)S(1)} %get-tuple-element.30), channel_id=1, source_target_pairs={{0,32},{32,64},{64,96},{1,33},{33,65},{65,97},{2,34},{34,66},{66,9... | collective-permute-start | bytes 1572872 | tf_op jit(solution)/shard_map/ppermute | solution.py:308
  122.7 10.4 %copy-start.2 = (bf16[512,512]{1,0:T(8,128)(2,1)}, bf16[512,512]{1,0:T(8,128)(2,1)S(1)}, u32[]{:S(2)}) copy-start(bf16[512,512]{1,0:T(8,128)(2,1)S(1)} %collective-permute-done.5.down_ref) | copy-start | bytes 1572868
  122.7 10.4 %copy-start.3 = (bf16[512,512]{1,0:T(8,128)(2,1)}, bf16[512,512]{1,0:T(8,128)(2,1)S(1)}, u32[]{:S(2)}) copy-start(bf16[512,512]{1,0:T(8,128)(2,1)S(1)} %collective-permute-done.4.up_ref) | copy-start | bytes 1572868
  122.8 10.3 %collective-permute-start.6 = (bf16[256,512]{1,0:T(8,128)(2,1)S(1)}, bf16[256,512]{1,0:T(8,128)(2,1)S(1)}, u32[]{:S(2)}, u32[]{:S(2)}) collective-permute-start(bf16[256,512]{1,0:T(8,128)(2,1)S(1)} %pad_maximum_fusion.2), channel_id=1, source_target_pairs={{0,1},{1,2},{2,3},{3,4},{4,5},{5,6},{6,7},{7,8},{8,9},{9,10},{10,1... | collective-permute-start | bytes 786440 | tf_op jit(solution)/shard_map/ppermute | solution.py:317
  122.9 10.2 %collective-permute-start.7 = (bf16[256,512]{1,0:T(8,128)(2,1)S(1)}, bf16[256,512]{1,0:T(8,128)(2,1)S(1)}, u32[]{:S(2)}, u32[]{:S(2)}) collective-permute-start(bf16[256,512]{1,0:T(8,128)(2,1)S(1)} %pad_maximum_fusion.3), channel_id=1, source_target_pairs={{1,0},{2,1},{3,2},{4,3},{5,4},{6,5},{7,6},{8,7},{9,8},{10,9},{11,1... | collective-permute-start | bytes 786440 | tf_op jit(solution)/shard_map/ppermute | solution.py:318
  133.1 0.7 copy-start.6
  133.1 0.8 copy-start.7

commit v2 on v1

v2 whole, which is shorter than its diff:
```python
import jax
import jax.numpy as jnp
from jax import lax
from jax.experimental import pallas as pl
from jax.experimental.pallas import tpu as pltpu
from jax.sharding import PartitionSpec as P

HEADS = 8
LAYERS = 2
D = 512
FIN = 256
DEVICES = 128
CAP = 16
ROWS = 40
OBS = 1024
CELLS = 1024
SLOTS = DEVICES * CAP
BLOCK = 64
BANDS = 2
SECTORS = 8
FRAME = SECTORS + 2
PAIRS = HEADS // 2
COLUMN = BANDS * BLOCK
EARLY = 5
NEG = -1e30
F32 = jnp.float32
BF16 = jnp.bfloat16

VMEM = pl.BlockSpec(memory_space=pltpu.VMEM)
SMEM = pl.BlockSpec(memory_space=pltpu.SMEM)
HBM = pl.BlockSpec(memory_space=pl.ANY)
PARAMS = pltpu.CompilerParams(vmem_limit_bytes=40 * 1024 * 1024)
WIDE = FRAME * BLOCK
HALO = SECTORS * BLOCK
NT = (((1,), (1,)), ((), ()))
TN = (((0,), (0,)), ((), ()))


def iota(shape, axis):
    return lax.broadcasted_iota(jnp.int32, shape, axis)


def dispatch_kernel(owner_ref, cell_ref, valid_ref, feat_hbm, send_ref, feat_ref, sem):
    fetch = pltpu.make_async_copy(feat_hbm, feat_ref, sem)
    fetch.start()
    owner = owner_ref[...]
    cell = cell_ref[...]
    valid = valid_ref[...]
    wide = 256
    earlier = (iota((wide, wide), 0) < iota((wide, wide), 1)).astype(F32).astype(BF16)
    carry = jnp.zeros((DEVICES, 1), F32)
    ranks = []
    chosen = []
    for at in range(0, OBS, wide):
        hot = (iota((DEVICES, wide), 0) == owner[:, at : at + wide]).astype(F32)
        before = jnp.dot(hot.astype(BF16), earlier, preferred_element_type=F32) + carry
        ranks.append(jnp.sum(hot * before, axis=0, keepdims=True))
        carry = carry + jnp.sum(hot, axis=1, keepdims=True)
        chosen.append(hot.astype(BF16))
    rank = jnp.concatenate(ranks, axis=1).astype(jnp.int32)
    hot_all = jnp.concatenate(chosen, axis=1)
    row = cell // 64
    col = cell % 64
    high = (col // 8) * BANDS + row // 8 + 1
    low = (row % 8) * 8 + col % 8
    usable = valid == 1
    high = jnp.where(usable, high, 0)
    low = jnp.where(usable, low, 0)
    lane = iota((128, OBS), 0)
    part = jnp.where(lane < CAP, high, jnp.where(lane < 2 * CAP, low, 0))
    entry = jnp.where(lane % CAP == rank, part, 0).astype(F32).astype(BF16)
    tags = lax.dot_general(hot_all, entry, NT, preferred_element_type=F32)
    send_ref[:, 32:40, :] = jnp.broadcast_to(tags[:, None, :], (DEVICES, 8, 128)).astype(BF16)
    target = owner * CAP + rank
    fetch.wait()
    feat = feat_ref[...]
    step = 256
    for at in range(0, SLOTS, step):
        pick = (iota((step, OBS), 0) + at == target).astype(F32).astype(BF16)
        rows = jnp.dot(pick, feat, preferred_element_type=F32).astype(BF16)
        first = at // CAP
        count = step // CAP
        send_ref[first : first + count, 0:16, :] = rows[:, :128].reshape(count, CAP, 128)
        send_ref[first : first + count, 16:32, :] = rows[:, 128:].reshape(count, CAP, 128)


def dispatch(owner, cell, valid, feat):
    return pl.pallas_call(
        dispatch_kernel,
        out_shape=jax.ShapeDtypeStruct((DEVICES, ROWS, 128), BF16),
        in_specs=[VMEM] * 3 + [HBM],
        out_specs=VMEM,
        scratch_shapes=[pltpu.VMEM((OBS, FIN), BF16), pltpu.SemaphoreType.DMA],
        compiler_params=PARAMS,
        name="dispatch",
    )(owner, cell, valid, feat)


def on_chip(array):
    return pltpu.with_memory_space_constraint(array, pltpu.VMEM)


def off_chip(array):
    return pltpu.with_memory_space_constraint(array, pltpu.HBM)


def norm_rows(hidden, gain):
    scale = lax.rsqrt(jnp.mean(hidden * hidden, axis=-1, keepdims=True) + 1e-06)
    return (hidden * scale * gain).astype(BF16)


def store_normed(at, rows, normed_ref, west_ref, east_ref):
    size = rows.shape[0]
    normed_ref[at : at + size, :] = rows
    for edge_ref, start in ((west_ref, 0), (east_ref, CELLS - COLUMN)):
        low = max(at, start)
        high = min(at + size, start + COLUMN)
        if low < high:
            edge_ref[low - start : high - start, :] = rows[low - at : high - at]


NORMED_SHAPES = (
    pltpu.VMEM((CELLS, D), BF16),
    pltpu.VMEM((BANDS * BLOCK, D), BF16),
    pltpu.VMEM((BANDS * BLOCK, D), BF16),
)


def combine_kernel(
    got_ref, embed_hbm, grid_hbm, gain_ref, hidden_ref, normed_ref, west_ref, east_ref,
    emb_ref, tag_ref, hot_ref, embed_ref, grid_ref, sems,
):
    fetch_embed = pltpu.make_async_copy(embed_hbm, embed_ref, sems.at[0])
    fetch_grid = pltpu.make_async_copy(grid_hbm, grid_ref, sems.at[1])
    fetch_embed.start()
    fetch_grid.start()
    tag_ref[...] = got_ref[:, 32:40, :].astype(F32).reshape(DEVICES * 8, 128)
    tags = tag_ref[pl.ds(0, DEVICES, stride=8), :]
    tags = jnp.transpose(tags)[: 2 * CAP].astype(BF16)
    spread = (iota((DEVICES, SLOTS), 1) // CAP == iota((DEVICES, SLOTS), 0)).astype(F32).astype(BF16)
    wide = jnp.dot(tags, spread, preferred_element_type=F32)
    own = iota((CAP, SLOTS), 1) % CAP == iota((CAP, SLOTS), 0)
    high = jnp.sum(jnp.where(own, wide[:CAP], 0.0), axis=0, keepdims=True)
    low = jnp.sum(jnp.where(own, wide[CAP:], 0.0), axis=0, keepdims=True)
    low_hot = (iota((BLOCK, SLOTS), 0).astype(F32) == low).astype(F32).astype(BF16)
    high_hot = (iota((16, SLOTS), 0).astype(F32) + 1.0 == high).astype(F32).astype(BF16)
    counts = lax.dot_general(low_hot, high_hot, NT, preferred_element_type=F32)
    inverse = 1.0 / jnp.maximum(counts, 1.0)
    high16 = jnp.broadcast_to(high, (16, SLOTS))
    for block in range(BANDS * SECTORS):
        mask = (high16 == block + 1.0).astype(F32).astype(BF16)
        for part in range(BLOCK // 16):
            at = block * BLOCK + part * 16
            hot_ref[at : at + 16, :] = low_hot[part * 16 : part * 16 + 16] * mask
    fetch_embed.wait()
    step = 512
    for at in range(0, SLOTS, step):
        first = at // CAP
        count = step // CAP
        left = got_ref[first : first + count, 0:16, :].reshape(step, 128)
        right = got_ref[first : first + count, 16:32, :].reshape(step, 128)
        raw = jnp.concatenate([left, right], axis=1)
        product = jnp.dot(raw, embed_ref[...], preferred_element_type=F32)
        emb_ref[at : at + step, :] = jax.nn.gelu(product).astype(BF16)
    gain = gain_ref[0:1, :]
    fetch_grid.wait()
    chunk = 512
    for start in range(0, CELLS, chunk):
        total = jnp.dot(hot_ref[start : start + chunk, :], emb_ref[...], preferred_element_type=F32)
        for sub in range(chunk // BLOCK):
            block = start // BLOCK + sub
            sector = block // BANDS
            band = block % BANDS
            mean = total[sub * BLOCK : (sub + 1) * BLOCK] * inverse[:, block : block + 1]
            static = jnp.concatenate(
                [
                    grid_ref[band * 8 + r, sector * 8 : sector * 8 + 8, :].astype(F32)
                    for r in range(8)
                ],
                axis=0,
            )
            hidden = mean + static
            hidden_ref[block * BLOCK : (block + 1) * BLOCK, :] = hidden
            store_normed(block * BLOCK, norm_rows(hidden, gain), normed_ref, west_ref, east_ref)


def combine(got, w_embed, grid_feat, gains):
    return pl.pallas_call(
        combine_kernel,
        out_shape=(pltpu.VMEM((CELLS, D), F32),) + NORMED_SHAPES,
        in_specs=[VMEM, HBM, HBM, VMEM],
        out_specs=(VMEM,) * 4,
        scratch_shapes=[
            pltpu.VMEM((SLOTS, D), BF16),
            pltpu.VMEM((DEVICES * 8, 128), F32),
            pltpu.VMEM((CELLS, SLOTS), BF16),
            pltpu.VMEM((FIN, D), BF16),
            pltpu.VMEM((16, 64, D), BF16),
            pltpu.SemaphoreType.DMA((2,)),
        ],
        compiler_params=PARAMS,
        name="combine",
    )(got, w_embed, grid_feat, gains)


def head_pair(query):
    lane = iota(query.shape, 1) < BLOCK
    zero = jnp.zeros_like(query)
    return jnp.concatenate([jnp.where(lane, query, zero), jnp.where(lane, zero, query)], axis=0)


def fold(values, op):
    rows, width = values.shape
    part = op(values.reshape(rows // BLOCK, BLOCK, width), axis=0)
    part = op(part.reshape(8, 8, width), axis=0)
    return op(part, axis=0, keepdims=True)


def soft(scores):
    highest = fold(scores, jnp.max)
    expo = jnp.exp(scores - highest)
    return expo.astype(BF16), highest, fold(expo, jnp.sum)


def staged(units, stages):
    held = {}
    for turn in range(len(units) + len(stages) - 1):
        for number, stage in enumerate(stages):
            at = turn - number
            if 0 <= at < len(units):
                held[at] = stage(units[at], held.get(at))


def near_columns(columns, query_ref, mixed_ref, highest_ref, total_ref):
    units = [(sector, pair) for sector in columns for pair in range(PAIRS)]

    def scored(unit, _):
        sector, pair = unit
        feats = slice(pair * 128, pair * 128 + 128)
        query = head_pair(query_ref[sector * COLUMN : (sector + 1) * COLUMN, feats])
        return lax.dot_general(columns[sector][0](feats), query, NT, preferred_element_type=F32)

    def weighed(unit, scores):
        return soft(scores)

    def summed(unit, held):
        sector, pair = unit
        weights, highest, total = held
        feats = slice(pair * 128, pair * 128 + 128)
        mixed = jnp.dot(columns[sector][1](feats), weights, preferred_element_type=F32)
        at = slice(sector * COLUMN, (sector + 1) * COLUMN)
        for h in range(2):
            head = pair * 2 + h
            lanes = slice(h * COLUMN, (h + 1) * COLUMN)
            mixed_ref[head * BLOCK : (head + 1) * BLOCK, at] = mixed[h * BLOCK : (h + 1) * BLOCK, lanes]
            highest_ref[head : head + 1, at] = highest[:, lanes]
            total_ref[head : head + 1, at] = total[:, lanes]

    staged(units, (scored, weighed, summed))


def inner_column(sector, key_ref, value_ref):
    at = slice((sector - 1) * COLUMN, (sector + 2) * COLUMN)
    return (lambda feats: key_ref[at, feats], lambda feats: value_ref[feats, at])


NEAR_SHAPES = (
    pltpu.VMEM((D, CELLS), F32),
    pltpu.VMEM((HEADS, CELLS), F32),
    pltpu.VMEM((HEADS, CELLS), F32),
)


def project_kernel(
    normed_ref, query_w, key_w, value_w,
    query_ref, key_ref, value_ref, mixed_ref, highest_ref, total_ref,
):
    flat = normed_ref[...]
    query = jnp.dot(flat, query_w[...], preferred_element_type=F32).astype(BF16)
    query_ref[...] = query * BF16(0.125)
    key_ref[...] = jnp.dot(flat, key_w[...], preferred_element_type=F32).astype(BF16)
    value_ref[...] = lax.dot_general(value_w[...], flat, NT, preferred_element_type=F32).astype(BF16)
    columns = {sector: inner_column(sector, key_ref, value_ref) for sector in range(1, EARLY)}
    near_columns(columns, query_ref, mixed_ref, highest_ref, total_ref)


def project(normed, w_query, w_key, w_value):
    shape = pltpu.VMEM((CELLS, D), BF16)
    return pl.pallas_call(
        project_kernel,
        out_shape=(shape, shape, pltpu.VMEM((D, CELLS), BF16)) + NEAR_SHAPES,
        in_specs=[VMEM] * 4,
        out_specs=(VMEM,) * 6,
        compiler_params=PARAMS,
        cost_estimate=pl.CostEstimate(flops=6 * CELLS * D * D, transcendentals=0, bytes_accessed=5 << 20),
        name="project",
    )(normed, w_query, w_key, w_value)


def margins_kernel(normed_ref, west_ref, east_ref, top_ref, low_ref):
    for band, out in enumerate((top_ref, low_ref)):
        here = slice(band * BLOCK, (band + 1) * BLOCK)
        out[0:BLOCK, :] = west_ref[here, :]
        for sector in range(SECTORS):
            at = (sector * BANDS + band) * BLOCK
            out[(sector + 1) * BLOCK : (sector + 2) * BLOCK, :] = normed_ref[at : at + BLOCK, :]
        out[BLOCK + HALO : WIDE, :] = east_ref[here, :]


def margins(normed, west, east):
    shape = pltpu.VMEM((WIDE, D), BF16)
    return pl.pallas_call(
        margins_kernel,
        out_shape=(shape, shape),
        in_specs=[VMEM] * 3,
        out_specs=(VMEM,) * 2,
        compiler_params=PARAMS,
        name="margins",
    )(normed, west, east)


def near_kernel(
    query_ref, key_ref, value_ref, west_ref, east_ref, key_w, value_w, mixed_in, highest_in, total_in,
    mixed_ref, highest_ref, total_ref,
):
    del mixed_in, highest_in, total_in
    outs = (query_ref, mixed_ref, highest_ref, total_ref)
    sides = jnp.concatenate([west_ref[...], east_ref[...]], axis=0)
    side_keys = jnp.dot(sides, key_w[...], preferred_element_type=F32).astype(BF16)
    side_values = lax.dot_general(value_w[...], sides, NT, preferred_element_type=F32).astype(BF16)
    columns = {
        sector: inner_column(sector, key_ref, value_ref) for sector in range(EARLY, SECTORS - 1)
    }
    inner = 2 * COLUMN
    columns[0] = (
        lambda feats: jnp.concatenate([side_keys[:COLUMN, feats], key_ref[:inner, feats]], axis=0),
        lambda feats: jnp.concatenate(
            [side_values[feats, :COLUMN], value_ref[feats, :inner]], axis=1
        ),
    )
    columns[SECTORS - 1] = (
        lambda feats: jnp.concatenate(
            [key_ref[CELLS - inner :, feats], side_keys[COLUMN:, feats]], axis=0
        ),
        lambda feats: jnp.concatenate(
            [value_ref[feats, CELLS - inner :], side_values[feats, COLUMN:]], axis=1
        ),
    )
    near_columns(columns, *outs)


def near(query, key, value, west, east, w_key, w_value, parts):
    return pl.pallas_call(
        near_kernel,
        out_shape=NEAR_SHAPES,
        in_specs=[VMEM] * 10,
        out_specs=(VMEM,) * 3,
        input_output_aliases={7: 0, 8: 1, 9: 2},
        compiler_params=PARAMS,
        cost_estimate=pl.CostEstimate(flops=8 << 30, transcendentals=4 << 20, bytes_accessed=8 << 20),
        name="near",
    )(query, key, value, west, east, w_key, w_value, *parts)


def make_far_kernel(last):
    def far_kernel(
        lat_ref, query_ref, mixed_ref, highest_ref, total_ref, up_ref, down_ref,
        hidden_ref, gain_ref, key_w, value_w, out_w, *rest,
    ):
        if last:
            out_ref, key_f, value_f, att_ref, new_ref = rest
        else:
            new_ref, normed_ref, west_ref, east_ref, key_f, value_f, att_ref = rest
        for band, source in enumerate((up_ref, down_ref)):
            rows = source[...]
            key_f[band] = jnp.dot(rows, key_w[...], preferred_element_type=F32).astype(BF16)
            value_f[band] = lax.dot_general(
                value_w[...], rows, NT, preferred_element_type=F32
            ).astype(BF16)
        beyond = (lat_ref[0] == 0, lat_ref[0] == lat_ref[1] - 1)
        span = 4 * BLOCK

        def hide(scores):
            second = iota((BLOCK, 2 * COLUMN), 1) % COLUMN >= BLOCK
            return jnp.concatenate(
                [
                    jnp.where(second, NEG, scores[:BLOCK]),
                    scores[BLOCK : 3 * BLOCK],
                    jnp.where(second, scores[3 * BLOCK :], NEG),
                ],
                axis=0,
            )

        def scored(unit, _):
            step, pair, band = unit
            feats = slice(pair * 128, pair * 128 + 128)
            first = step * 2 * COLUMN + band * BLOCK
            query = jnp.concatenate(
                [
                    query_ref[first : first + BLOCK, feats],
                    query_ref[first + COLUMN : first + COLUMN + BLOCK, feats],
                ],
                axis=0,
            )
            keys = key_f[band, step * COLUMN : step * COLUMN + span, feats]
            return hide(lax.dot_general(keys, head_pair(query), NT, preferred_element_type=F32))

        def weighed(unit, scores):
            return soft(scores)

        def summed(unit, held):
            step, pair, band = unit
            weights, highest, total = held
            feats = slice(pair * 128, pair * 128 + 128)
            values = value_f[band, feats, step * COLUMN : step * COLUMN + span]
            mixed = jnp.dot(values, weights, preferred_element_type=F32)
            waiting[unit] = (mixed, jnp.where(beyond[band], NEG, highest), total)
            if band == 1:
                merge(step, pair, waiting.pop((step, pair, 0)), waiting.pop(unit))

        def merge(step, pair, upper, lower):
            for h in range(2):
                head = pair * 2 + h
                rows = slice(head * BLOCK, (head + 1) * BLOCK)
                lanes = slice(h * COLUMN, (h + 1) * COLUMN)
                here = slice(h * BLOCK, (h + 1) * BLOCK)
                for second in range(2):
                    moved = []
                    for which in range(3):
                        x = upper[which][here if which == 0 else slice(None), lanes]
                        y = lower[which][here if which == 0 else slice(None), lanes]
                        if second:
                            x = pltpu.roll(x, BLOCK, 1)
                        else:
                            y = pltpu.roll(y, BLOCK, 1)
                        moved.append(jnp.where(iota(x.shape, 1) < BLOCK, x, y))
                    mixed, highest, total = moved
                    cells = slice((step * 2 + second) * COLUMN, (step * 2 + second + 1) * COLUMN)
                    highest_near = highest_ref[head : head + 1, cells]
                    top = jnp.maximum(highest, highest_near)
                    near_part = jnp.exp(highest_near - top)
                    far_part = jnp.exp(highest - top)
                    weight = total_ref[head : head + 1, cells] * near_part + total * far_part
                    near_part = near_part / weight
                    far_part = far_part / weight
                    att_ref[rows, cells] = (
                        mixed_ref[rows, cells] * near_part + mixed * far_part
                    ).astype(BF16)

        waiting = {}
        staged(
            [
                (step, pair, band)
                for step in range(SECTORS // 2)
                for pair in range(PAIRS)
                for band in range(BANDS)
            ],
            (scored, weighed, summed),
        )
        gain = gain_ref[...]
        for at in range(0, CELLS, 256):
            update = lax.dot_general(
                att_ref[:, at : at + 256], out_w[...], TN, preferred_element_type=F32
            )
            hidden = hidden_ref[at : at + 256, :] + update
            new_ref[at : at + 256, :] = hidden
            if not last:
                store_normed(at, norm_rows(hidden, gain), normed_ref, west_ref, east_ref)
        if last:
            for band in range(BANDS):
                for r in range(8):
                    pieces = []
                    for sector in range(SECTORS):
                        at = (sector * BANDS + band) * BLOCK + r * 8
                        pieces.append(new_ref[at : at + 8, :])
                    out_ref[band * 8 + r] = jnp.concatenate(pieces, axis=0).astype(BF16)

    return far_kernel


def far(place, query, parts, up, down, hidden, gain, w_key, w_value, w_out, last):
    scratch = [
        pltpu.VMEM((BANDS, WIDE, D), BF16),
        pltpu.VMEM((BANDS, D, WIDE), BF16),
        pltpu.VMEM((D, CELLS), BF16),
    ]
    if last:
        scratch.append(pltpu.VMEM((CELLS, D), F32))
        out_shape = jax.ShapeDtypeStruct((16, 64, D), BF16)
        out_specs = VMEM
    else:
        out_shape = (pltpu.VMEM((CELLS, D), F32),) + NORMED_SHAPES
        out_specs = (VMEM,) * 4
    return pl.pallas_call(
        make_far_kernel(last),
        out_shape=out_shape,
        in_specs=[SMEM] + [VMEM] * 11,
        out_specs=out_specs,
        scratch_shapes=scratch,
        compiler_params=PARAMS,
        name="far",
    )(place, query, *parts, up, down, hidden, gain, w_key, w_value, w_out)


def local(
    obs_feat, obs_owner, obs_cell, obs_valid, grid_feat,
    w_embed, gains, w_query, w_key, w_value, w_out,
):
    send = dispatch(
        obs_owner.reshape(1, OBS), obs_cell.reshape(1, OBS), obs_valid.reshape(1, OBS), off_chip(obs_feat)
    )
    got = lax.all_to_all(send, ("lat", "lon"), split_axis=0, concat_axis=0, tiled=True)
    hidden, normed, western, eastern = combine(got, off_chip(w_embed), off_chip(grid_feat), gains)
    lat_count = lax.axis_size("lat")
    lon_count = lax.axis_size("lon")
    place = jnp.stack([lax.axis_index("lat"), jnp.int32(lat_count)])
    rising = [(i, i + 1) for i in range(lat_count - 1)]
    falling = [(b, a) for a, b in rising]
    forward = [(i, (i + 1) % lon_count) for i in range(lon_count)]
    backward = [(b, a) for a, b in forward]
    for layer in range(LAYERS):
        last = layer == LAYERS - 1
        key_w = on_chip(w_key[layer])
        value_w = on_chip(jnp.transpose(w_value[layer]))
        hidden = on_chip(hidden)
        normed = on_chip(normed)
        west = lax.ppermute(on_chip(eastern), "lon", forward)
        east = lax.ppermute(on_chip(western), "lon", backward)
        query, key, value, *parts = project(normed, on_chip(w_query[layer]), key_w, value_w)
        query = on_chip(query)
        top, low = margins(normed, west, east)
        up = lax.ppermute(on_chip(low), "lat", rising)
        down = lax.ppermute(on_chip(top), "lat", falling)
        parts = [on_chip(part) for part in parts]
        parts = near(query, on_chip(key), on_chip(value), west, east, key_w, value_w, parts)
        following = min(layer + 1, LAYERS - 1)
        result = far(
            place, query, [on_chip(part) for part in parts], up, down, hidden,
            gains[following : following + 1], key_w, value_w, on_chip(w_out[layer]), last,
        )
        if not last:
            hidden, normed, western, eastern = result
    return result


def solution(mesh):
    placed = (
        P(("lat", "lon"), None),
        P(("lat", "lon"), None),
        P(("lat", "lon")),
        P(("lat", "lon")),
        P("lat", "lon", None),
        P(), P(), P(), P(), P(), P(),
    )
    return jax.shard_map(
        local, mesh=mesh, in_specs=placed, out_specs=P("lat", "lon", None), check_vma=False
    )
```

time: 158 us -> 115 us (0.73)
  blocking collectives: 33.8 us -> 0 us
  Pallas kernels: 69.1 us -> 37.6 us
  waiting for transfers between devices: 19.8 us -> 36.2 us
  starting transfers between devices: 27.2 us -> 33.1 us
    all_to_all x1 -> x0, blocking collectives: 33.8 us -> none  [local(): lax.all_to_all(send, ('lat', 'lon'), split_axis=0, concat_axis=0, tiled=T...]
    pallas_call x5 -> x9, Pallas kernels: 65.4 us -> 33.9 us  [the longest x2 14.7 us: far(): pl.pallas_call(make_far_kernel(last), out_shape=out_shape, in_specs=[SMEM...]
    all_to_all x0 -> x1, waiting for transfers between devices: none -> 17 us  [local(): lax.all_to_all(send, ('lat', 'lon'), split_axis=0, concat_axis=0, tiled=T...]
    all_to_all x0 -> x1, starting transfers between devices: none -> 11.5 us  [local(): lax.all_to_all(send, ('lat', 'lon'), split_axis=0, concat_axis=0, tiled=T...]
    ppermute x8, starting transfers between devices: 27.2 us -> 21.6 us  [the longest x2 11.3 us: local(): east = lax.ppermute(on_chip(western), 'lon', backward)]
    slice x8 -> x1, local copies, waits for them, and re-layouts: 4.51 us -> 0.07 us  [local(): value_w = on_chip(jnp.transpose(w_value[layer]))]
    squeeze x0 -> x3, local copies, waits for them, and re-layouts: none -> 4.16 us  [the longest x1 2.22 us: local(): key_w = on_chip(w_key[layer])]
  transfers between devices with their start and end apart: 8 -> 9, of which waited for: 3 -> 5; matrix products, arithmetic and copies ran while one was open for 2% -> 4% of each run, Pallas kernels for 6% -> 12%
where the time goes in v2:
time: 115 us; the launch traced here: 114 us
  Pallas kernels  37.6 us (33%)
  waiting for transfers between devices  36.2 us (31%)
  starting transfers between devices  33.1 us (29%)
  local copies, waits for them, and re-layouts  7.12 us (6%)
    all_to_all x1, waiting for transfers between devices, local(): lax.all_to_all(send, ('lat', 'lon'), split_axis=0, concat_axis=0, tiled=T...  17 us
    pallas_call x2, Pallas kernels, far(): pl.pallas_call(make_far_kernel(last), out_shape=out_shape, in_specs=[SMEM...  14.7 us
    ppermute x2, waiting for transfers between devices, local(): down = lax.ppermute(on_chip(top), 'lat', falling)  13.7 us
    all_to_all x1, starting transfers between devices, local(): lax.all_to_all(send, ('lat', 'lon'), split_axis=0, concat_axis=0, tiled=T...  11.5 us
    ppermute x2, starting transfers between devices, local(): east = lax.ppermute(on_chip(western), 'lon', backward)  11.3 us
    pallas_call x2, Pallas kernels, project(): pl.pallas_call(project_kernel, out_shape=(shape, shape, pltpu.VMEM((D, CE...  8.8 us
    ppermute x2, starting transfers between devices, local(): up = lax.ppermute(on_chip(low), 'lat', rising)  5.83 us
    ppermute x2, waiting for transfers between devices, local(): up = lax.ppermute(on_chip(low), 'lat', rising)  5.42 us
  transfers between devices with their start and end apart: 9, of which 5 were waited for; matrix products, arithmetic and copies ran while one was open for 4% of the time, Pallas kernels for 12%

profile of v2, /device:TPU:1, one launch (start us, length us, event | category | flops | bytes accessed | tf_op | source)
XLA Modules:
  0.0 114.4 jit_solution(11316327169168648274)
XLA Ops:
  0.0 0.7 copy-done.5
  0.7 0.7 copy-done.6
  1.4 0.7 copy-done.7
  2.1 3.8 %dispatch.1 = bf16[128,40,128]{2,1,0:T(8,128)(2,1)} custom-call(s32[1,1024]{1,0:T(1,128)S(1)} %bitcast.28, s32[1,1024]{1,0:T(1,128)S(1)} %bitcast.29, s32[1,1024]{1,0:T(1,128)S(1)} %bitcast.30, bf16[1024,256]{1,0:T(8,128)(2,1)} %feat_hbm.1), custom_call_target="tpu_custom_call" | custom-call | tf_op jit(solution)/shard_map/dispatch/pallas_call | solution.py:88
  5.8 11.5 %all-to-all-start = ((bf16[128,40,128]{2,1,0:T(8,128)(2,1)}), bf16[128,40,128]{2,1,0:T(8,128)(2,1)S(1)}, u32[]{:S(2)}, u32[]{:S(2)}) async-start(bf16[128,40,128]{2,1,0:T(8,128)(2,1)} %dispatch.1), calls=%async_computation | async-start | bytes 2621440 | tf_op jit(solution)/shard_map/all_to_all | solution.py:512
  17.3 0.0 copy-start.4
  17.4 0.0 copy-done.8
  17.4 0.1 fusion
  17.4 0.2 copy.20
  17.7 0.4 copy-done.4
  18.0 0.2 copy.21
  18.3 0.0 copy-start.9
  18.3 0.1 pad_add_fusion.lat_ref
  18.3 2.2 %slice_bitcast_fusion.1 = (bf16[512,512]{1,0:T(8,128)(2,1)}, bf16[512,512]{1,0:T(8,128)(2,1)S(1)}) fusion(bf16[2,512,512]{2,1,0:T(8,128)(2,1)} %param.19), kind=kLoop, calls=%fused_computation.1 | loop fusion | bytes 2097152 | tf_op jit(solution)/shard_map/squeeze | solution.py:523
  20.6 0.0 copy-done.9
  20.6 1.0 slice_bitcast_fusion.2
  21.6 0.0 copy-done.10
  21.6 0.9 slice_bitcast_fusion
  22.5 17.0 %all-to-all-done.got_ref = bf16[128,40,128]{2,1,0:T(8,128)(2,1)S(1)} async-done(((bf16[128,40,128]{2,1,0:T(8,128)(2,1)}), bf16[128,40,128]{2,1,0:T(8,128)(2,1)S(1)}, u32[]{:S(2)}, u32[]{:S(2)}) %all-to-all-start) | async-done | bytes 1310752 | tf_op jit(solution)/shard_map/all_to_all | solution.py:512
  39.5 5.0 %combine.1 = (f32[1024,512]{1,0:T(8,128)S(1)}, bf16[1024,512]{1,0:T(8,128)(2,1)S(1)}, bf16[128,512]{1,0:T(8,128)(2,1)S(1)}, bf16[128,512]{1,0:T(8,128)(2,1)S(1)}) custom-call(bf16[128,40,128]{2,1,0:T(8,128)(2,1)S(1)} %all-to-all-done.got_ref, bf16[256,512]{1,0:T(8,128)(2,1)} %embed_hbm.1, bf16[16,64,512]{2,1,0:T(8,128)(2,1)} %grid_hbm.1, f32[2,512]{1,0:T(2,128)S(1)} %copy-done.4), custom_call_target="tpu_custom_call" | custom-call | tf_op jit(solution)/shard_map/combine/pallas_call | solution.py:188
  44.5 0.1 collective-permute-start
  44.6 5.7 %collective-permute-start.1 = (bf16[128,512]{1,0:T(8,128)(2,1)S(1)}, bf16[128,512]{1,0:T(8,128)(2,1)S(1)}, u32[]{:S(2)}, u32[]{:S(2)}) collective-permute-start(bf16[128,512]{1,0:T(8,128)(2,1)S(1)} %get-tuple-element.40), channel_id=1, source_target_pairs={{1,0},{2,1},{3,2},{4,3},{5,4},{6,5},{7,6},{8,7},{9,8},{10,9},{11,1... | collective-permute-start | bytes 393224 | tf_op jit(solution)/shard_map/ppermute | solution.py:528
  50.3 0.0 copy-done.3
  50.3 4.4 %project.2 = (bf16[1024,512]{1,0:T(8,128)(2,1)S(1)}, bf16[1024,512]{1,0:T(8,128)(2,1)S(1)}, bf16[512,1024]{1,0:T(8,128)(2,1)S(1)}, f32[512,1024]{1,0:T(8,128)S(1...) custom-call(bf16[1024,512]{1,0:T(8,128)(2,1)S(1)} %get-tuple-element.35.normed_ref, bf16[512,512]{1,0:T(8,128)(2,1)S(1)} %copy-done.3, ...), custom_call_target="tpu_custom_call" | custom-call | flops 1610612736 | bytes 5242880 | tf_op jit(solution)/shard_map/project/pallas_call | solution.py:289
  54.7 0.0 collective-permute-done.west_ref
  54.7 0.0 collective-permute-done.1.east_ref
  54.7 0.1 margins.2
  54.8 3.7 %collective-permute-start.2 = (bf16[640,512]{1,0:T(8,128)(2,1)S(1)}, bf16[640,512]{1,0:T(8,128)(2,1)S(1)}, u32[]{:S(2)}, u32[]{:S(2)}) collective-permute-start(bf16[640,512]{1,0:T(8,128)(2,1)S(1)} %get-tuple-element.47), channel_id=1, source_target_pairs={{0,32},{32,64},{64,96},{1,33},{33,65},{65,97},{2,34},{34,66},{66,9... | collective-permute-start | bytes 1966088 | tf_op jit(solution)/shard_map/ppermute | solution.py:532
  58.5 2.1 %collective-permute-start.3 = (bf16[640,512]{1,0:T(8,128)(2,1)S(1)}, bf16[640,512]{1,0:T(8,128)(2,1)S(1)}, u32[]{:S(2)}, u32[]{:S(2)}) collective-permute-start(bf16[640,512]{1,0:T(8,128)(2,1)S(1)} %get-tuple-element.48), channel_id=1, source_target_pairs={{32,0},{64,32},{96,64},{33,1},{65,33},{97,65},{34,2},{66,34},{98,6... | collective-permute-start | bytes 1966088 | tf_op jit(solution)/shard_map/ppermute | solution.py:533
  60.6 2.6 %near.2 = (f32[512,1024]{1,0:T(8,128)S(1)}, f32[8,1024]{1,0:T(8,128)S(1)}, f32[8,1024]{1,0:T(8,128)S(1)}) custom-call(bf16[1024,512]{1,0:T(8,128)(2,1)S(1)} %get-tuple-element.36.query_ref, bf16[1024,512]{1,0:T(8,128)(2,1)S(1)} %get-tuple-element.37.key_ref, ...), custom_call_target="tpu_custom_call", output_to_operand_aliasing={{0}: (7, {}), {1}: (8, {}), {2}: (9, {})} | custom-call | flops 8589934592 | bytes 8388608 | tf_op jit(solution)/shard_map/near/pallas_call | solution.py:353
  63.2 2.8 %collective-permute-done.2.up_ref = bf16[640,512]{1,0:T(8,128)(2,1)S(1)} collective-permute-done((bf16[640,512]{1,0:T(8,128)(2,1)S(1)}, bf16[640,512]{1,0:T(8,128)(2,1)S(1)}, u32[]{:S(2)}, u32[]{:S(2)}) %collective-permute-start.2) | collective-permute-done | bytes 655392 | tf_op jit(solution)/shard_map/ppermute | solution.py:532
  66.0 7.8 %collective-permute-done.3.down_ref = bf16[640,512]{1,0:T(8,128)(2,1)S(1)} collective-permute-done((bf16[640,512]{1,0:T(8,128)(2,1)S(1)}, bf16[640,512]{1,0:T(8,128)(2,1)S(1)}, u32[]{:S(2)}, u32[]{:S(2)}) %collective-permute-start.3) | collective-permute-done | bytes 655392 | tf_op jit(solution)/shard_map/ppermute | solution.py:533
  73.8 6.9 %far.2 = (f32[1024,512]{1,0:T(8,128)S(1)}, bf16[1024,512]{1,0:T(8,128)(2,1)S(1)}, bf16[128,512]{1,0:T(8,128)(2,1)S(1)}, bf16[128,512]{1,0:T(8,128)(2,1)S(1)}) custom-call(s32[2]{0:T(128)S(1)} %pad_add_fusion.lat_ref, bf16[1024,512]{1,0:T(8,128)(2,1)S(1)} %get-tuple-element.36.query_ref, f32[512,1024]{1,0:T(8,128)S(1)} %get-tuple-element.44.mixed_ref, ...), custom_call_target="tpu_custom_call" | custom-call | tf_op jit(solution)/shard_map/far/pallas_call | solution.py:494
  80.7 0.1 collective-permute-start.4
  80.8 5.7 %collective-permute-start.5 = (bf16[128,512]{1,0:T(8,128)(2,1)S(1)}, bf16[128,512]{1,0:T(8,128)(2,1)S(1)}, u32[]{:S(2)}, u32[]{:S(2)}) collective-permute-start(bf16[128,512]{1,0:T(8,128)(2,1)S(1)} %get-tuple-element.55), channel_id=1, source_target_pairs={{1,0},{2,1},{3,2},{4,3},{5,4},{6,5},{7,6},{8,7},{9,8},{10,9},{11,1... | collective-permute-start | bytes 393224 | tf_op jit(solution)/shard_map/ppermute | solution.py:528
  86.5 0.0 copy-done
  86.5 0.0 copy-done.2
  86.5 4.4 %project.3 = (bf16[1024,512]{1,0:T(8,128)(2,1)S(1)}, bf16[1024,512]{1,0:T(8,128)(2,1)S(1)}, bf16[512,1024]{1,0:T(8,128)(2,1)S(1)}, f32[512,1024]{1,0:T(8,128)S(1...) custom-call(bf16[1024,512]{1,0:T(8,128)(2,1)S(1)} %get-tuple-element.50.normed_ref, bf16[512,512]{1,0:T(8,128)(2,1)S(1)} %copy-done.2, ...), custom_call_target="tpu_custom_call" | custom-call | flops 1610612736 | bytes 5242880 | tf_op jit(solution)/shard_map/project/pallas_call | solution.py:289
  90.9 0.0 collective-permute-done.4.west_ref
  90.9 0.0 collective-permute-done.5.east_ref
  90.9 0.1 margins.3
  91.0 2.2 %collective-permute-start.6 = (bf16[640,512]{1,0:T(8,128)(2,1)S(1)}, bf16[640,512]{1,0:T(8,128)(2,1)S(1)}, u32[]{:S(2)}, u32[]{:S(2)}) collective-permute-start(bf16[640,512]{1,0:T(8,128)(2,1)S(1)} %get-tuple-element.62), channel_id=1, source_target_pairs={{0,32},{32,64},{64,96},{1,33},{33,65},{65,97},{2,34},{34,66},{66,9... | collective-permute-start | bytes 1966088 | tf_op jit(solution)/shard_map/ppermute | solution.py:532
  93.2 2.2 %collective-permute-start.7 = (bf16[640,512]{1,0:T(8,128)(2,1)S(1)}, bf16[640,512]{1,0:T(8,128)(2,1)S(1)}, u32[]{:S(2)}, u32[]{:S(2)}) collective-permute-start(bf16[640,512]{1,0:T(8,128)(2,1)S(1)} %get-tuple-element.63), channel_id=1, source_target_pairs={{32,0},{64,32},{96,64},{33,1},{65,33},{97,65},{34,2},{66,34},{98,6... | collective-permute-start | bytes 1966088 | tf_op jit(solution)/shard_map/ppermute | solution.py:533
  95.4 0.0 copy-start.1
  95.4 2.6 %near.3 = (f32[512,1024]{1,0:T(8,128)S(1)}, f32[8,1024]{1,0:T(8,128)S(1)}, f32[8,1024]{1,0:T(8,128)S(1)}) custom-call(bf16[1024,512]{1,0:T(8,128)(2,1)S(1)} %get-tuple-element.51.query_ref, bf16[1024,512]{1,0:T(8,128)(2,1)S(1)} %get-tuple-element.52.key_ref, ...), custom_call_target="tpu_custom_call", output_to_operand_aliasing={{0}: (7, {}), {1}: (8, {}), {2}: (9, {})} | custom-call | flops 8589934592 | bytes 8388608 | tf_op jit(solution)/shard_map/near/pallas_call | solution.py:353
  98.0 2.7 %collective-permute-done.6.up_ref = bf16[640,512]{1,0:T(8,128)(2,1)S(1)} collective-permute-done((bf16[640,512]{1,0:T(8,128)(2,1)S(1)}, bf16[640,512]{1,0:T(8,128)(2,1)S(1)}, u32[]{:S(2)}, u32[]{:S(2)}) %collective-permute-start.6) | collective-permute-done | bytes 655392 | tf_op jit(solution)/shard_map/ppermute | solution.py:532
  100.7 5.9 %collective-permute-done.7.down_ref = bf16[640,512]{1,0:T(8,128)(2,1)S(1)} collective-permute-done((bf16[640,512]{1,0:T(8,128)(2,1)S(1)}, bf16[640,512]{1,0:T(8,128)(2,1)S(1)}, u32[]{:S(2)}, u32[]{:S(2)}) %collective-permute-start.7) | collective-permute-done | bytes 655392 | tf_op jit(solution)/shard_map/ppermute | solution.py:533
  106.6 7.8 %far.3 = bf16[16,64,512]{2,1,0:T(8,128)(2,1)} custom-call(s32[2]{0:T(128)S(1)} %pad_add_fusion.lat_ref, bf16[1024,512]{1,0:T(8,128)(2,1)S(1)} %get-tuple-element.51.query_ref, f32[512,1024]{1,0:T(8,128)S(1)} %get-tuple-element.59.mixed_ref, f32[8,1024]{1,0:T(8,128)S(1)} %get-tuple-element.60.highest_ref, f32[8,1024]{1,0:T(8,128)S(1)} %get-tuple-element.61.total_ref, ...), custom_call_target="tpu_custom_call" | custom-call | tf_op jit(solution)/shard_map/far/pallas_call | solution.py:494
  (10 shorter events, 0.0 us)
Async XLA Ops:
  0.0 0.7 copy-start.5
  0.7 0.7 copy-start.6
  1.4 0.7 copy-start.7
  2.1 15.3 %copy-start.8 = (bf16[2,512,512]{2,1,0:T(8,128)(2,1)S(1)}, bf16[2,512,512]{2,1,0:T(8,128)(2,1)}, u32[]{:S(2)}) copy-start(bf16[2,512,512]{2,1,0:T(8,128)(2,1)} %param.20) | copy-start | bytes 3145732
  5.8 33.7 %all-to-all-start = ((bf16[128,40,128]{2,1,0:T(8,128)(2,1)}), bf16[128,40,128]{2,1,0:T(8,128)(2,1)S(1)}, u32[]{:S(2)}, u32[]{:S(2)}) async-start(bf16[128,40,128]{2,1,0:T(8,128)(2,1)} %dispatch.1), calls=%async_computation | async-start | bytes 2621440 | tf_op jit(solution)/shard_map/all_to_all | solution.py:512
  17.3 0.7 copy-start.4
  18.3 2.3 %copy-start.9 = (bf16[2,512,512]{2,1,0:T(8,128)(2,1)S(1)}, bf16[2,512,512]{2,1,0:T(8,128)(2,1)}, u32[]{:S(2)}) copy-start(bf16[2,512,512]{2,1,0:T(8,128)(2,1)} %param.18) | copy-start | bytes 3145732
  18.3 3.3 %copy-start.10 = (bf16[2,512,512]{2,1,0:T(8,128)(2,1)S(1)}, bf16[2,512,512]{2,1,0:T(8,128)(2,1)}, u32[]{:S(2)}) copy-start(bf16[2,512,512]{2,1,0:T(8,128)(2,1)} %param.21) | copy-start | bytes 3145732
  39.5 10.7 %copy-start.3 = (bf16[512,512]{1,0:T(8,128)(2,1)S(1)}, bf16[512,512]{1,0:T(8,128)(2,1)}, u32[]{:S(2)}) copy-start(bf16[512,512]{1,0:T(8,128)(2,1)} %get-tuple-element.72.query_w) | copy-start | bytes 1572868
  44.5 10.2 %collective-permute-start = (bf16[128,512]{1,0:T(8,128)(2,1)S(1)}, bf16[128,512]{1,0:T(8,128)(2,1)S(1)}, u32[]{:S(2)}, u32[]{:S(2)}) collective-permute-start(bf16[128,512]{1,0:T(8,128)(2,1)S(1)} %get-tuple-element.39), channel_id=1, source_target_pairs={{0,1},{1,2},{2,3},{3,4},{4,5},{5,6},{6,7},{7,8},{8,9},{9,10},{10,1... | collective-permute-start | bytes 393224 | tf_op jit(solution)/shard_map/ppermute | solution.py:527
  44.6 10.1 %collective-permute-start.1 = (bf16[128,512]{1,0:T(8,128)(2,1)S(1)}, bf16[128,512]{1,0:T(8,128)(2,1)S(1)}, u32[]{:S(2)}, u32[]{:S(2)}) collective-permute-start(bf16[128,512]{1,0:T(8,128)(2,1)S(1)} %get-tuple-element.40), channel_id=1, source_target_pairs={{1,0},{2,1},{3,2},{4,3},{5,4},{6,5},{7,6},{8,7},{9,8},{10,9},{11,1... | collective-permute-start | bytes 393224 | tf_op jit(solution)/shard_map/ppermute | solution.py:528
  54.8 11.2 %collective-permute-start.2 = (bf16[640,512]{1,0:T(8,128)(2,1)S(1)}, bf16[640,512]{1,0:T(8,128)(2,1)S(1)}, u32[]{:S(2)}, u32[]{:S(2)}) collective-permute-start(bf16[640,512]{1,0:T(8,128)(2,1)S(1)} %get-tuple-element.47), channel_id=1, source_target_pairs={{0,32},{32,64},{64,96},{1,33},{33,65},{65,97},{2,34},{34,66},{66,9... | collective-permute-start | bytes 1966088 | tf_op jit(solution)/shard_map/ppermute | solution.py:532
  58.5 15.3 %collective-permute-start.3 = (bf16[640,512]{1,0:T(8,128)(2,1)S(1)}, bf16[640,512]{1,0:T(8,128)(2,1)S(1)}, u32[]{:S(2)}, u32[]{:S(2)}) collective-permute-start(bf16[640,512]{1,0:T(8,128)(2,1)S(1)} %get-tuple-element.48), channel_id=1, source_target_pairs={{32,0},{64,32},{96,64},{33,1},{65,33},{97,65},{34,2},{66,34},{98,6... | collective-permute-start | bytes 1966088 | tf_op jit(solution)/shard_map/ppermute | solution.py:533
  73.8 12.7 %copy-start = (bf16[512,512]{1,0:T(8,128)(2,1)S(1)}, bf16[512,512]{1,0:T(8,128)(2,1)}, u32[]{:S(2)}) copy-start(bf16[512,512]{1,0:T(8,128)(2,1)} %get-tuple-element.69.key_w) | copy-start | bytes 1572868
  73.8 12.7 %copy-start.2 = (bf16[512,512]{1,0:T(8,128)(2,1)S(1)}, bf16[512,512]{1,0:T(8,128)(2,1)}, u32[]{:S(2)}) copy-start(bf16[512,512]{1,0:T(8,128)(2,1)} %get-tuple-element.71.query_w) | copy-start | bytes 1572868
  80.7 10.2 %collective-permute-start.4 = (bf16[128,512]{1,0:T(8,128)(2,1)S(1)}, bf16[128,512]{1,0:T(8,128)(2,1)S(1)}, u32[]{:S(2)}, u32[]{:S(2)}) collective-permute-start(bf16[128,512]{1,0:T(8,128)(2,1)S(1)} %get-tuple-element.54), channel_id=1, source_target_pairs={{0,1},{1,2},{2,3},{3,4},{4,5},{5,6},{6,7},{7,8},{8,9},{9,10},{10,1... | collective-permute-start | bytes 393224 | tf_op jit(solution)/shard_map/ppermute | solution.py:527
  80.8 10.1 %collective-permute-start.5 = (bf16[128,512]{1,0:T(8,128)(2,1)S(1)}, bf16[128,512]{1,0:T(8,128)(2,1)S(1)}, u32[]{:S(2)}, u32[]{:S(2)}) collective-permute-start(bf16[128,512]{1,0:T(8,128)(2,1)S(1)} %get-tuple-element.55), channel_id=1, source_target_pairs={{1,0},{2,1},{3,2},{4,3},{5,4},{6,5},{7,6},{8,7},{9,8},{10,9},{11,1... | collective-permute-start | bytes 393224 | tf_op jit(solution)/shard_map/ppermute | solution.py:528
  91.0 9.7 %collective-permute-start.6 = (bf16[640,512]{1,0:T(8,128)(2,1)S(1)}, bf16[640,512]{1,0:T(8,128)(2,1)S(1)}, u32[]{:S(2)}, u32[]{:S(2)}) collective-permute-start(bf16[640,512]{1,0:T(8,128)(2,1)S(1)} %get-tuple-element.62), channel_id=1, source_target_pairs={{0,32},{32,64},{64,96},{1,33},{33,65},{65,97},{2,34},{34,66},{66,9... | collective-permute-start | bytes 1966088 | tf_op jit(solution)/shard_map/ppermute | solution.py:532
  93.2 13.4 %collective-permute-start.7 = (bf16[640,512]{1,0:T(8,128)(2,1)S(1)}, bf16[640,512]{1,0:T(8,128)(2,1)S(1)}, u32[]{:S(2)}, u32[]{:S(2)}) collective-permute-start(bf16[640,512]{1,0:T(8,128)(2,1)S(1)} %get-tuple-element.63), channel_id=1, source_target_pairs={{32,0},{64,32},{96,64},{33,1},{65,33},{97,65},{34,2},{66,34},{98,6... | collective-permute-start | bytes 1966088 | tf_op jit(solution)/shard_map/ppermute | solution.py:533
  95.4 11.2 %copy-start.1 = (bf16[512,512]{1,0:T(8,128)(2,1)S(1)}, bf16[512,512]{1,0:T(8,128)(2,1)}, u32[]{:S(2)}) copy-start(bf16[512,512]{1,0:T(8,128)(2,1)} %get-tuple-element.65.out_w) | copy-start | bytes 1572868

commit v3 on v2

--- a/solution.py
+++ b/solution.py
@@ -21,7 +21,6 @@
 FRAME = SECTORS + 2
 PAIRS = HEADS // 2
 COLUMN = BANDS * BLOCK
-EARLY = 5
 NEG = -1e30
 F32 = jnp.float32
 BF16 = jnp.bfloat16
@@ -40,9 +39,15 @@
     return lax.broadcasted_iota(jnp.int32, shape, axis)
 
 
-def dispatch_kernel(owner_ref, cell_ref, valid_ref, feat_hbm, send_ref, feat_ref, sem):
-    fetch = pltpu.make_async_copy(feat_hbm, feat_ref, sem)
-    fetch.start()
+def dispatch_kernel(
+    owner_hbm, cell_hbm, valid_hbm, feat_hbm, send_ref, owner_ref, cell_ref, valid_ref, feat_ref, sems
+):
+    pairs = ((owner_hbm, owner_ref), (cell_hbm, cell_ref), (valid_hbm, valid_ref), (feat_hbm, feat_ref))
+    copies = [pltpu.make_async_copy(a, b, sems.at[i]) for i, (a, b) in enumerate(pairs)]
+    for copy in copies:
+        copy.start()
+    for copy in copies[:3]:
+        copy.wait()
     owner = owner_ref[...]
     cell = cell_ref[...]
     valid = valid_ref[...]
@@ -72,7 +77,7 @@
     tags = lax.dot_general(hot_all, entry, NT, preferred_element_type=F32)
     send_ref[:, 32:40, :] = jnp.broadcast_to(tags[:, None, :], (DEVICES, 8, 128)).astype(BF16)
     target = owner * CAP + rank
-    fetch.wait()
+    copies[3].wait()
     feat = feat_ref[...]
     step = 256
     for at in range(0, SLOTS, step):
@@ -88,9 +93,10 @@
     return pl.pallas_call(
         dispatch_kernel,
         out_shape=jax.ShapeDtypeStruct((DEVICES, ROWS, 128), BF16),
-        in_specs=[VMEM] * 3 + [HBM],
+        in_specs=[HBM] * 4,
         out_specs=VMEM,
-        scratch_shapes=[pltpu.VMEM((OBS, FIN), BF16), pltpu.SemaphoreType.DMA],
+        scratch_shapes=[pltpu.VMEM((1, OBS), jnp.int32)] * 3
+        + [pltpu.VMEM((OBS, FIN), BF16), pltpu.SemaphoreType.DMA((4,))],
         compiler_params=PARAMS,
         name="dispatch",
     )(owner, cell, valid, feat)
@@ -109,27 +115,48 @@
     return (hidden * scale * gain).astype(BF16)
 
 
-def store_normed(at, rows, normed_ref, west_ref, east_ref):
-    size = rows.shape[0]
-    normed_ref[at : at + size, :] = rows
-    for edge_ref, start in ((west_ref, 0), (east_ref, CELLS - COLUMN)):
-        low = max(at, start)
-        high = min(at + size, start + COLUMN)
-        if low < high:
-            edge_ref[low - start : high - start, :] = rows[low - at : high - at]
+def pick(choose, x, y):
+    return jnp.where(choose, x, y)
+
+
+def store_normed(sector, rows, refs, place_ref):
+    normed_ref, first_ref, second_ref, third_ref, fourth_ref = refs
+    here = slice(sector * BLOCK, (sector + 1) * BLOCK)
+    normed_ref[sector * COLUMN : (sector + 1) * COLUMN, :] = rows
+    even = place_ref[2] == 0
+    top = rows[:BLOCK]
+    low = rows[BLOCK:]
+    first_ref[here, :] = pick(even, low, top)
+    second_ref[here, :] = pick(even, top, low)
+    if sector == 0:
+        third_ref[...] = rows
+        fourth_ref[...] = rows
+    if sector == SECTORS - 1:
+        even = place_ref[3] == 0
+        third_ref[...] = pick(even, rows, third_ref[...])
+        fourth_ref[...] = pick(even, fourth_ref[...], rows)
 
 
 NORMED_SHAPES = (
     pltpu.VMEM((CELLS, D), BF16),
-    pltpu.VMEM((BANDS * BLOCK, D), BF16),
-    pltpu.VMEM((BANDS * BLOCK, D), BF16),
+    pltpu.VMEM((HALO, D), BF16),
+    pltpu.VMEM((HALO, D), BF16),
+    pltpu.VMEM((COLUMN, D), BF16),
+    pltpu.VMEM((COLUMN, D), BF16),
 )
 
 
+def gelu(x):
+    inner = x * (0.7978845608028654 + (0.7978845608028654 * 0.044715) * (x * x))
+    half = 0.5 * x
+    return half + half * jnp.tanh(inner)
+
+
 def combine_kernel(
-    got_ref, embed_hbm, grid_hbm, gain_ref, hidden_ref, normed_ref, west_ref, east_ref,
-    emb_ref, tag_ref, hot_ref, embed_ref, grid_ref, sems,
+    place_ref, got_ref, embed_hbm, grid_hbm, gain_ref, hidden_ref, *rest
 ):
+    refs = rest[:5]
+    emb_ref, tag_ref, hot_ref, embed_ref, grid_ref, sems = rest[5:]
     fetch_embed = pltpu.make_async_copy(embed_hbm, embed_ref, sems.at[0])
     fetch_grid = pltpu.make_async_copy(grid_hbm, grid_ref, sems.at[1])
     fetch_embed.start()
@@ -161,35 +188,38 @@
         right = got_ref[first : first + count, 16:32, :].reshape(step, 128)
         raw = jnp.concatenate([left, right], axis=1)
         product = jnp.dot(raw, embed_ref[...], preferred_element_type=F32)
-        emb_ref[at : at + step, :] = jax.nn.gelu(product).astype(BF16)
+        emb_ref[at : at + step, :] = gelu(product).astype(BF16)
     gain = gain_ref[0:1, :]
     fetch_grid.wait()
     chunk = 512
     for start in range(0, CELLS, chunk):
         total = jnp.dot(hot_ref[start : start + chunk, :], emb_ref[...], preferred_element_type=F32)
-        for sub in range(chunk // BLOCK):
-            block = start // BLOCK + sub
-            sector = block // BANDS
-            band = block % BANDS
-            mean = total[sub * BLOCK : (sub + 1) * BLOCK] * inverse[:, block : block + 1]
-            static = jnp.concatenate(
-                [
-                    grid_ref[band * 8 + r, sector * 8 : sector * 8 + 8, :].astype(F32)
-                    for r in range(8)
-                ],
-                axis=0,
-            )
-            hidden = mean + static
-            hidden_ref[block * BLOCK : (block + 1) * BLOCK, :] = hidden
-            store_normed(block * BLOCK, norm_rows(hidden, gain), normed_ref, west_ref, east_ref)
-
-
-def combine(got, w_embed, grid_feat, gains):
+        for sub in range(chunk // COLUMN):
+            sector = start // COLUMN + sub
+            pieces = []
+            for band in range(BANDS):
+                block = sector * BANDS + band
+                row = sub * COLUMN + band * BLOCK
+                mean = total[row : row + BLOCK] * inverse[:, block : block + 1]
+                static = jnp.concatenate(
+                    [
+                        grid_ref[band * 8 + r, sector * 8 : sector * 8 + 8, :].astype(F32)
+                        for r in range(8)
+                    ],
+                    axis=0,
+                )
+                pieces.append(mean + static)
+            hidden = jnp.concatenate(pieces, axis=0)
+            hidden_ref[sector * COLUMN : (sector + 1) * COLUMN, :] = hidden
+            store_normed(sector, norm_rows(hidden, gain), refs, place_ref)
+
+
+def combine(place, got, w_embed, grid_feat, gains):
     return pl.pallas_call(
         combine_kernel,
         out_shape=(pltpu.VMEM((CELLS, D), F32),) + NORMED_SHAPES,
-        in_specs=[VMEM, HBM, HBM, VMEM],
-        out_specs=(VMEM,) * 4,
+        in_specs=[SMEM, VMEM, HBM, HBM, VMEM],
+        out_specs=(VMEM,) * 6,
         scratch_shapes=[
             pltpu.VMEM((SLOTS, D), BF16),
             pltpu.VMEM((DEVICES * 8, 128), F32),
@@ -200,7 +230,7 @@
         ],
         compiler_params=PARAMS,
         name="combine",
-    )(got, w_embed, grid_feat, gains)
+    )(place, got, w_embed, grid_feat, gains)
 
 
 def head_pair(query):
@@ -280,7 +310,7 @@
     query_ref[...] = query * BF16(0.125)
     key_ref[...] = jnp.dot(flat, key_w[...], preferred_element_type=F32).astype(BF16)
     value_ref[...] = lax.dot_general(value_w[...], flat, NT, preferred_element_type=F32).astype(BF16)
-    columns = {sector: inner_column(sector, key_ref, value_ref) for sector in range(1, EARLY)}
+    columns = {sector: inner_column(sector, key_ref, value_ref) for sector in range(1, SECTORS - 1)}
     near_columns(columns, query_ref, mixed_ref, highest_ref, total_ref)
 
 
@@ -297,40 +327,51 @@
     )(normed, w_query, w_key, w_value)
 
 
-def margins_kernel(normed_ref, west_ref, east_ref, top_ref, low_ref):
-    for band, out in enumerate((top_ref, low_ref)):
-        here = slice(band * BLOCK, (band + 1) * BLOCK)
-        out[0:BLOCK, :] = west_ref[here, :]
-        for sector in range(SECTORS):
-            at = (sector * BANDS + band) * BLOCK
-            out[(sector + 1) * BLOCK : (sector + 2) * BLOCK, :] = normed_ref[at : at + BLOCK, :]
-        out[BLOCK + HALO : WIDE, :] = east_ref[here, :]
-
-
-def margins(normed, west, east):
-    shape = pltpu.VMEM((WIDE, D), BF16)
+def sides_of(place_ref, third_ref, fourth_ref):
+    even = place_ref[3] == 0
+    third = third_ref[...]
+    fourth = fourth_ref[...]
+    return pick(even, fourth, third), pick(even, third, fourth)
+
+
+def rows_of(place_ref, first_ref, second_ref):
+    even = place_ref[2] == 0
+    first = first_ref[...]
+    second = second_ref[...]
+    return pick(even, second, first), pick(even, first, second)
+
+
+def corners_kernel(place_ref, third_ref, fourth_ref, first_ref, second_ref):
+    west, east = sides_of(place_ref, third_ref, fourth_ref)
+    even = place_ref[2] == 0
+    top = jnp.concatenate([west[:BLOCK], east[:BLOCK]], axis=0)
+    low = jnp.concatenate([west[BLOCK:], east[BLOCK:]], axis=0)
+    first_ref[...] = pick(even, low, top)
+    second_ref[...] = pick(even, top, low)
+
+
+def corners(place, third, fourth):
+    shape = pltpu.VMEM((COLUMN, D), BF16)
     return pl.pallas_call(
-        margins_kernel,
+        corners_kernel,
         out_shape=(shape, shape),
-        in_specs=[VMEM] * 3,
+        in_specs=[SMEM] + [VMEM] * 2,
         out_specs=(VMEM,) * 2,
         compiler_params=PARAMS,
-        name="margins",
-    )(normed, west, east)
+        name="corners",
+    )(place, third, fourth)
 
 
 def near_kernel(
-    query_ref, key_ref, value_ref, west_ref, east_ref, key_w, value_w, mixed_in, highest_in, total_in,
+    place_ref, query_ref, key_ref, value_ref, third_ref, fourth_ref, key_w, value_w, mixed_in, highest_in, total_in,
     mixed_ref, highest_ref, total_ref,
 ):
     del mixed_in, highest_in, total_in
     outs = (query_ref, mixed_ref, highest_ref, total_ref)
-    sides = jnp.concatenate([west_ref[...], east_ref[...]], axis=0)
+    sides = jnp.concatenate(sides_of(place_ref, third_ref, fourth_ref), axis=0)
     side_keys = jnp.dot(sides, key_w[...], preferred_element_type=F32).astype(BF16)
     side_values = lax.dot_general(value_w[...], sides, NT, preferred_element_type=F32).astype(BF16)
-    columns = {
-        sector: inner_column(sector, key_ref, value_ref) for sector in range(EARLY, SECTORS - 1)
-    }
+    columns = {}
     inner = 2 * COLUMN
     columns[0] = (
         lambda feats: jnp.concatenate([side_keys[:COLUMN, feats], key_ref[:inner, feats]], axis=0),
@@ -349,35 +390,60 @@
     near_columns(columns, *outs)
 
 
-def near(query, key, value, west, east, w_key, w_value, parts):
+def near(place, query, key, value, third, fourth, w_key, w_value, parts):
     return pl.pallas_call(
         near_kernel,
         out_shape=NEAR_SHAPES,
-        in_specs=[VMEM] * 10,
+        in_specs=[SMEM] + [VMEM] * 10,
         out_specs=(VMEM,) * 3,
-        input_output_aliases={7: 0, 8: 1, 9: 2},
+        input_output_aliases={8: 0, 9: 1, 10: 2},
         compiler_params=PARAMS,
         cost_estimate=pl.CostEstimate(flops=8 << 30, transcendentals=4 << 20, bytes_accessed=8 << 20),
         name="near",
-    )(query, key, value, west, east, w_key, w_value, *parts)
+    )(place, query, key, value, third, fourth, w_key, w_value, *parts)
+
+
+def merge(tiles, head, cells, near_refs, store):
+    mixed_ref, highest_ref, total_ref = near_refs
+    mixed, highest, total = tiles
+    rows = slice(head * BLOCK, (head + 1) * BLOCK)
+    highest_near = highest_ref[head : head + 1, cells]
+    top = jnp.maximum(highest, highest_near)
+    near_part = jnp.exp(highest_near - top)
+    far_part = jnp.exp(highest - top)
+    weight = total_ref[head : head + 1, cells] * near_part + total * far_part
+    near_part = near_part / weight
+    far_part = far_part / weight
+    store(rows, (mixed_ref[rows, cells] * near_part + mixed * far_part).astype(BF16))
+
+
+def join(x, y, turn_x):
+    if turn_x:
+        x = pltpu.roll(x, BLOCK, 1)
+    else:
+        y = pltpu.roll(y, BLOCK, 1)
+    return jnp.where(iota(x.shape, 1) < BLOCK, x, y)
+
+
+def beyond_grid(place_ref):
+    return (place_ref[0] == 0, place_ref[0] == place_ref[1] - 1)
 
 
 def make_far_kernel(last):
     def far_kernel(
-        lat_ref, query_ref, mixed_ref, highest_ref, total_ref, up_ref, down_ref,
+        place_ref, query_ref, mixed_ref, highest_ref, total_ref, first_ref, second_ref,
         hidden_ref, gain_ref, key_w, value_w, out_w, *rest,
     ):
-        if last:
-            out_ref, key_f, value_f, att_ref, new_ref = rest
-        else:
-            new_ref, normed_ref, west_ref, east_ref, key_f, value_f, att_ref = rest
-        for band, source in enumerate((up_ref, down_ref)):
-            rows = source[...]
+        new_ref, key_f, value_f = rest[:3]
+        refs = rest[3:-1]
+        att_ref = rest[-1]
+        near_refs = (mixed_ref, highest_ref, total_ref)
+        for band, rows in enumerate(rows_of(place_ref, first_ref, second_ref)):
             key_f[band] = jnp.dot(rows, key_w[...], preferred_element_type=F32).astype(BF16)
             value_f[band] = lax.dot_general(
                 value_w[...], rows, NT, preferred_element_type=F32
             ).astype(BF16)
-        beyond = (lat_ref[0] == 0, lat_ref[0] == lat_ref[1] - 1)
+        beyond = beyond_grid(place_ref)
         span = 4 * BLOCK
 
         def hide(scores):
@@ -394,7 +460,7 @@
         def scored(unit, _):
             step, pair, band = unit
             feats = slice(pair * 128, pair * 128 + 128)
-            first = step * 2 * COLUMN + band * BLOCK
+            first = (step * 2 + 1) * COLUMN + band * BLOCK
             query = jnp.concatenate(
                 [
                     query_ref[first : first + BLOCK, feats],
@@ -415,91 +481,204 @@
             values = value_f[band, feats, step * COLUMN : step * COLUMN + span]
             mixed = jnp.dot(values, weights, preferred_element_type=F32)
             waiting[unit] = (mixed, jnp.where(beyond[band], NEG, highest), total)
-            if band == 1:
-                merge(step, pair, waiting.pop((step, pair, 0)), waiting.pop(unit))
-
-        def merge(step, pair, upper, lower):
+            if band == 0:
+                return
+            upper = waiting.pop((step, pair, 0))
+            lower = waiting.pop(unit)
             for h in range(2):
-                head = pair * 2 + h
-                rows = slice(head * BLOCK, (head + 1) * BLOCK)
                 lanes = slice(h * COLUMN, (h + 1) * COLUMN)
-                here = slice(h * BLOCK, (h + 1) * BLOCK)
+                here = (slice(h * BLOCK, (h + 1) * BLOCK), slice(None), slice(None))
                 for second in range(2):
-                    moved = []
-                    for which in range(3):
-                        x = upper[which][here if which == 0 else slice(None), lanes]
-                        y = lower[which][here if which == 0 else slice(None), lanes]
-                        if second:
-                            x = pltpu.roll(x, BLOCK, 1)
-                        else:
-                            y = pltpu.roll(y, BLOCK, 1)
-                        moved.append(jnp.where(iota(x.shape, 1) < BLOCK, x, y))
-                    mixed, highest, total = moved
-                    cells = slice((step * 2 + second) * COLUMN, (step * 2 + second + 1) * COLUMN)
-                    highest_near = highest_ref[head : head + 1, cells]
-                    top = jnp.maximum(highest, highest_near)
-                    near_part = jnp.exp(highest_near - top)
-                    far_part = jnp.exp(highest - top)
-                    weight = total_ref[head : head + 1, cells] * near_part + total * far_part
-                    near_part = near_part / weight
-                    far_part = far_part / weight
-                    att_ref[rows, cells] = (
-                        mixed_ref[rows, cells] * near_part + mixed * far_part
-                    ).astype(BF16)
+                    tiles = [
+                        join(x[part, lanes], y[part, lanes], second == 1)
+                        for x, y, part in zip(upper, lower, here)
+                    ]
+                    at = (step * 2 + 1 + second) * COLUMN
+                    cells = slice(at, at + COLUMN)
+
+                    def store(rows, value):
+                        att_ref[rows, cells] = value
+
+                    merge(tiles, pair * 2 + h, cells, near_refs, store)
 
         waiting = {}
         staged(
             [
                 (step, pair, band)
-                for step in range(SECTORS // 2)
+                for step in range(SECTORS // 2 - 1)
                 for pair in range(PAIRS)
                 for band in range(BANDS)
             ],
             (scored, weighed, summed),
         )
         gain = gain_ref[...]
-        for at in range(0, CELLS, 256):
+        for at in range(COLUMN, CELLS - COLUMN, 256):
             update = lax.dot_general(
                 att_ref[:, at : at + 256], out_w[...], TN, preferred_element_type=F32
             )
             hidden = hidden_ref[at : at + 256, :] + update
             new_ref[at : at + 256, :] = hidden
             if not last:
-                store_normed(at, norm_rows(hidden, gain), normed_ref, west_ref, east_ref)
+                normed = norm_rows(hidden, gain)
+                for sub in range(256 // COLUMN):
+                    store_normed(
+                        at // COLUMN + sub,
+                        normed[sub * COLUMN : (sub + 1) * COLUMN],
+                        refs + (None, None),
+                        place_ref,
+                    )
+
+    return far_kernel
+
+
+def far(place, query, parts, first, second, hidden, gain, w_key, w_value, w_out, last):
+    out_shape = (
+        pltpu.VMEM((CELLS, D), F32),
+        pltpu.VMEM((BANDS, HALO, D), BF16),
+        pltpu.VMEM((BANDS, D, HALO), BF16),
+    )
+    if not last:
+        out_shape = out_shape + NORMED_SHAPES[:3]
+    return pl.pallas_call(
+        make_far_kernel(last),
+        out_shape=out_shape,
+        in_specs=[SMEM] + [VMEM] * 11,
+        out_specs=(VMEM,) * len(out_shape),
+        scratch_shapes=[pltpu.VMEM((D, CELLS), BF16)],
+        compiler_params=PARAMS,
+        cost_estimate=pl.CostEstimate(flops=8 << 30, transcendentals=4 << 20, bytes_accessed=8 << 20),
+        name="far",
+    )(place, query, *parts, first, second, hidden, gain, w_key, w_value, w_out)
+
+
+def make_edge_kernel(last):
+    def edge_kernel(
+        place_ref, query_ref, mixed_ref, highest_ref, total_ref, first_ref, second_ref,
+        hidden_ref, gain_ref, key_w, value_w, out_w, key_f, value_f, *rest,
+    ):
+        near_refs = (mixed_ref, highest_ref, total_ref)
+        att_ref = rest[-1]
+        if last:
+            inner_ref, out_ref, edge_ref = rest[:3]
+        else:
+            new_ref = rest[4]
+            refs = rest[5:10]
+        rows = jnp.concatenate(rows_of(place_ref, first_ref, second_ref), axis=0)
+        corner_keys = jnp.dot(rows, key_w[...], preferred_element_type=F32).astype(BF16)
+        corner_values = lax.dot_general(
+            value_w[...], rows, NT, preferred_element_type=F32
+        ).astype(BF16)
+        beyond = beyond_grid(place_ref)
+        starts = (0, HALO - 2 * BLOCK)
+
+        def scored(unit, _):
+            side, pair, band = unit
+            feats = slice(pair * 128, pair * 128 + 128)
+            first = side * (SECTORS - 1) * COLUMN + band * BLOCK
+            corner = (band * 2 + side) * BLOCK
+            keys = jnp.concatenate(
+                [
+                    key_f[band, starts[side] : starts[side] + 2 * BLOCK, feats],
+                    corner_keys[corner : corner + BLOCK, feats],
+                ],
+                axis=0,
+            )
+            query = head_pair(query_ref[first : first + BLOCK, feats])
+            return lax.dot_general(keys, query, NT, preferred_element_type=F32)
+
+        def weighed(unit, scores):
+            return soft(scores)
+
+        def summed(unit, held):
+            side, pair, band = unit
+            weights, highest, total = held
+            feats = slice(pair * 128, pair * 128 + 128)
+            corner = (band * 2 + side) * BLOCK
+            values = jnp.concatenate(
+                [
+                    value_f[band, feats, starts[side] : starts[side] + 2 * BLOCK],
+                    corner_values[feats, corner : corner + BLOCK],
+                ],
+                axis=1,
+            )
+            mixed = jnp.dot(values, weights, preferred_element_type=F32)
+            waiting[unit] = (mixed, jnp.where(beyond[band], NEG, highest), total)
+            if band == 0:
+                return
+            upper = waiting.pop((side, pair, 0))
+            lower = waiting.pop(unit)
+            for h in range(2):
+                here = (slice(h * BLOCK, (h + 1) * BLOCK), slice(None), slice(None))
+                tiles = [join(x[part], y[part], h == 1) for x, y, part in zip(upper, lower, here)]
+                at = side * (SECTORS - 1) * COLUMN
+                lanes = slice(side * COLUMN, (side + 1) * COLUMN)
+
+                def store(rows, value):
+                    att_ref[rows, lanes] = value
+
+                merge(tiles, pair * 2 + h, slice(at, at + COLUMN), near_refs, store)
+
+        waiting = {}
+        staged(
+            [
+                (side, pair, band)
+                for side in range(2)
+                for pair in range(PAIRS)
+                for band in range(BANDS)
+            ],
+            (scored, weighed, summed),
+        )
+        update = lax.dot_general(att_ref[...], out_w[...], TN, preferred_element_type=F32)
+        gain = gain_ref[...]
+        for side in range(2):
+            at = side * (CELLS - COLUMN)
+            hidden = hidden_ref[at : at + COLUMN, :] + update[side * COLUMN : (side + 1) * COLUMN]
+            if last:
+                edge_ref[side * COLUMN : (side + 1) * COLUMN, :] = hidden
+                continue
+            new_ref[at : at + COLUMN, :] = hidden
+            normed = norm_rows(hidden, gain)
+            store_normed(at // COLUMN, normed, refs, place_ref)
         if last:
             for band in range(BANDS):
                 for r in range(8):
                     pieces = []
                     for sector in range(SECTORS):
                         at = (sector * BANDS + band) * BLOCK + r * 8
-                        pieces.append(new_ref[at : at + 8, :])
+                        if sector == 0:
+                            pieces.append(edge_ref[at : at + 8, :])
+                        elif sector == SECTORS - 1:
+                            at = at - CELLS + 2 * COLUMN
+                            pieces.append(edge_ref[at : at + 8, :])
+                        else:
+                            pieces.append(inner_ref[at : at + 8, :])
                     out_ref[band * 8 + r] = jnp.concatenate(pieces, axis=0).astype(BF16)
 
-    return far_kernel
-
-
-def far(place, query, parts, up, down, hidden, gain, w_key, w_value, w_out, last):
-    scratch = [
-        pltpu.VMEM((BANDS, WIDE, D), BF16),
-        pltpu.VMEM((BANDS, D, WIDE), BF16),
-        pltpu.VMEM((D, CELLS), BF16),
-    ]
+    return edge_kernel
+
+
+def edges(place, query, parts, first, second, hidden, gain, w_key, w_value, w_out, inner, last):
+    new, key_f, value_f, *normed = inner
+    scratch = [pltpu.VMEM((D, 2 * COLUMN), BF16)]
     if last:
-        scratch.append(pltpu.VMEM((CELLS, D), F32))
+        scratch = [pltpu.VMEM((2 * COLUMN, D), F32)] + scratch
         out_shape = jax.ShapeDtypeStruct((16, 64, D), BF16)
         out_specs = VMEM
+        aliases = {}
     else:
         out_shape = (pltpu.VMEM((CELLS, D), F32),) + NORMED_SHAPES
-        out_specs = (VMEM,) * 4
+        out_specs = (VMEM,) * 6
+        aliases = {14: 0, 15: 1, 16: 2, 17: 3}
     return pl.pallas_call(
-        make_far_kernel(last),
+        make_edge_kernel(last),
         out_shape=out_shape,
-        in_specs=[SMEM] + [VMEM] * 11,
+        in_specs=[SMEM] + [VMEM] * (14 + len(normed)),
         out_specs=out_specs,
         scratch_shapes=scratch,
+        input_output_aliases=aliases,
         compiler_params=PARAMS,
-        name="far",
-    )(place, query, *parts, up, down, hidden, gain, w_key, w_value, w_out)
+        name="edges",
+    )(place, query, *parts, first, second, hidden, gain, w_key, w_value, w_out, key_f, value_f, new, *normed)
 
 
 def local(
@@ -507,39 +686,54 @@
     w_embed, gains, w_query, w_key, w_value, w_out,
 ):
     send = dispatch(
-        obs_owner.reshape(1, OBS), obs_cell.reshape(1, OBS), obs_valid.reshape(1, OBS), off_chip(obs_feat)
+        off_chip(obs_owner.reshape(1, OBS)),
+        off_chip(obs_cell.reshape(1, OBS)),
+        off_chip(obs_valid.reshape(1, OBS)),
+        off_chip(obs_feat),
     )
     got = lax.all_to_all(send, ("lat", "lon"), split_axis=0, concat_axis=0, tiled=True)
-    hidden, normed, western, eastern = combine(got, off_chip(w_embed), off_chip(grid_feat), gains)
     lat_count = lax.axis_size("lat")
     lon_count = lax.axis_size("lon")
-    place = jnp.stack([lax.axis_index("lat"), jnp.int32(lat_count)])
-    rising = [(i, i + 1) for i in range(lat_count - 1)]
-    falling = [(b, a) for a, b in rising]
-    forward = [(i, (i + 1) % lon_count) for i in range(lon_count)]
-    backward = [(b, a) for a, b in forward]
+    lat = lax.axis_index("lat")
+    lon = lax.axis_index("lon")
+    place = jnp.stack([lat, jnp.int32(lat_count), lat % 2, lon % 2])
+    hidden, *normed = combine(place, got, off_chip(w_embed), off_chip(grid_feat), gains)
+    lat_first = [(i, i ^ 1) for i in range(lat_count)]
+    lat_second = [(0, 0), (lat_count - 1, lat_count - 1)]
+    for i in range(1, lat_count - 1, 2):
+        lat_second += [(i, i + 1), (i + 1, i)]
+    lon_first = [(i, i ^ 1) for i in range(lon_count)]
+    lon_second = [(i, (((i + 1) ^ 1) - 1) % lon_count) for i in range(lon_count)]
     for layer in range(LAYERS):
         last = layer == LAYERS - 1
         key_w = on_chip(w_key[layer])
         value_w = on_chip(jnp.transpose(w_value[layer]))
         hidden = on_chip(hidden)
-        normed = on_chip(normed)
-        west = lax.ppermute(on_chip(eastern), "lon", forward)
-        east = lax.ppermute(on_chip(western), "lon", backward)
-        query, key, value, *parts = project(normed, on_chip(w_query[layer]), key_w, value_w)
+        flat, *trades = [on_chip(item) for item in normed]
+        third = lax.ppermute(trades[2], "lon", lon_first)
+        fourth = lax.ppermute(trades[3], "lon", lon_second)
+        second = lax.ppermute(trades[1], "lat", lat_second)
+        first = lax.ppermute(trades[0], "lat", lat_first)
+        query, key, value, *parts = project(flat, on_chip(w_query[layer]), key_w, value_w)
         query = on_chip(query)
-        top, low = margins(normed, west, east)
-        up = lax.ppermute(on_chip(low), "lat", rising)
-        down = lax.ppermute(on_chip(top), "lat", falling)
+        corner = corners(place, third, fourth)
+        corner_second = lax.ppermute(on_chip(corner[1]), "lat", lat_second)
+        corner_first = lax.ppermute(on_chip(corner[0]), "lat", lat_first)
         parts = [on_chip(part) for part in parts]
-        parts = near(query, on_chip(key), on_chip(value), west, east, key_w, value_w, parts)
+        parts = near(
+            place, query, on_chip(key), on_chip(value), third, fourth, key_w, value_w, parts
+        )
+        parts = [on_chip(part) for part in parts]
         following = min(layer + 1, LAYERS - 1)
-        result = far(
-            place, query, [on_chip(part) for part in parts], up, down, hidden,
-            gains[following : following + 1], key_w, value_w, on_chip(w_out[layer]), last,
+        gain = gains[following : following + 1]
+        out_w = on_chip(w_out[layer])
+        inner = far(place, query, parts, first, second, hidden, gain, key_w, value_w, out_w, last)
+        inner = [on_chip(item) for item in inner]
+        result = edges(
+            place, query, parts, corner_first, corner_second, hidden, gain, key_w, value_w, out_w, inner, last
         )
         if not last:
-            hidden, normed, western, eastern = result
+            hidden, *normed = result
     return result
 
 

time: 115 us -> 98.9 us (0.86)
  waiting for transfers between devices: 36.2 us -> 17.4 us
  Pallas kernels: 37.6 us -> 41.9 us
  local copies, waits for them, and re-layouts: 7.12 us -> 4.67 us
    ppermute x8 -> x12, waiting for transfers between devices: 19.2 us -> 0.03 us  [the longest x2 0.01 us: local(): second = lax.ppermute(trades[1], 'lat', lat_second)]
    pallas_call x4 -> x6, Pallas kernels: 5.43 us -> 11 us  [the longest x2 5.51 us: edges(): pl.pallas_call(make_edge_kernel(last), out_shape=out_shape, in_specs=[SME...]
    pallas_call x2, Pallas kernels: 14.7 us -> 10.6 us  [far(): pl.pallas_call(make_far_kernel(last), out_shape=out_shape, in_specs=[SMEM...]
    unnamed x24 -> x18, local copies, waits for them, and re-layouts: 2.88 us -> 0.46 us
    pallas_call x2, Pallas kernels: 8.8 us -> 11.1 us  [project(): pl.pallas_call(project_kernel, out_shape=(shape, shape, pltpu.VMEM((D, CE...]
    squeeze x1, local copies, waits for them, and re-layouts: 2.22 us -> 0.87 us  [local(): key_w = on_chip(w_key[layer])]
    squeeze x1, local copies, waits for them, and re-layouts: 1.05 us -> 2.4 us  [local(): w_query[layer]]
    ppermute x8 -> x12, starting transfers between devices: 21.6 us -> 22.7 us  [the longest x2 8.81 us: local(): corner_second = lax.ppermute(on_chip(corner[1]), 'lat', lat_second)]
  transfers between devices with their start and end apart: 9 -> 13, of which waited for: 5 -> 1; matrix products, arithmetic and copies ran while one was open for 4% -> 5% of each run, Pallas kernels for 12% -> 28%
where the time goes in v3:
time: 98.9 us; the launch traced here: 98.6 us
  Pallas kernels  41.9 us (42%)
  starting transfers between devices  34.2 us (35%)
  waiting for transfers between devices  17.4 us (18%)
  local copies, waits for them, and re-layouts  4.67 us (5%)
    all_to_all x1, waiting for transfers between devices, local(): lax.all_to_all(send, ('lat', 'lon'), split_axis=0, concat_axis=0, tiled=T...  17.4 us
    all_to_all x1, starting transfers between devices, local(): lax.all_to_all(send, ('lat', 'lon'), split_axis=0, concat_axis=0, tiled=T...  11.5 us
    pallas_call x2, Pallas kernels, project(): pl.pallas_call(project_kernel, out_shape=(shape, shape, pltpu.VMEM((D, CE...  11.1 us
    pallas_call x2, Pallas kernels, far(): pl.pallas_call(make_far_kernel(last), out_shape=out_shape, in_specs=[SMEM...  10.6 us
    ppermute x2, starting transfers between devices, local(): corner_second = lax.ppermute(on_chip(corner[1]), 'lat', lat_second)  8.81 us
    ppermute x2, starting transfers between devices, local(): second = lax.ppermute(trades[1], 'lat', lat_second)  6.27 us
    ppermute x2, starting transfers between devices, local(): fourth = lax.ppermute(trades[3], 'lon', lon_second)  5.85 us
    pallas_call x2, Pallas kernels, edges(): pl.pallas_call(make_edge_kernel(last), out_shape=out_shape, in_specs=[SME...  5.51 us
  transfers between devices with their start and end apart: 13, of which 1 were waited for; matrix products, arithmetic and copies ran while one was open for 5% of the time, Pallas kernels for 28%

profile of v3, /device:TPU:1, one launch (start us, length us, event | category | flops | bytes accessed | tf_op | source)
XLA Modules:
  0.0 98.6 jit_solution(15601383632187249616)
XLA Ops:
  0.0 3.8 %dispatch.1 = bf16[128,40,128]{2,1,0:T(8,128)(2,1)} custom-call(s32[1,1024]{1,0:T(1,128)} %bitcast.32, s32[1,1024]{1,0:T(1,128)} %bitcast.33, s32[1,1024]{1,0:T(1,128)} %bitcast.34, bf16[1024,256]{1,0:T(8,128)(2,1)} %feat_hbm.1), custom_call_target="tpu_custom_call" | custom-call | tf_op jit(solution)/shard_map/dispatch/pallas_call | solution.py:93
  3.8 11.5 %all-to-all-start = ((bf16[128,40,128]{2,1,0:T(8,128)(2,1)}), bf16[128,40,128]{2,1,0:T(8,128)(2,1)S(1)}, u32[]{:S(2)}, u32[]{:S(2)}) async-start(bf16[128,40,128]{2,1,0:T(8,128)(2,1)} %dispatch.1), calls=%async_computation | async-start | bytes 2621440 | tf_op jit(solution)/shard_map/all_to_all | solution.py:694
  15.3 0.0 copy-done.4
  15.3 0.1 fusion
  15.4 0.2 copy.25
  15.6 0.2 copy.24
  15.9 0.0 copy-start.6
  15.9 0.1 pad_add_fusion.place_ref
  15.9 2.4 %slice_bitcast_fusion.2 = (bf16[512,512]{1,0:T(8,128)(2,1)}, bf16[512,512]{1,0:T(8,128)(2,1)}) fusion(bf16[2,512,512]{2,1,0:T(8,128)(2,1)} %param.18), kind=kLoop, calls=%fused_computation.2 | loop fusion | bytes 2097152 | tf_op jit(solution)/shard_map/squeeze | solution.py:717
  18.4 0.9 slice_bitcast_fusion.1
  19.2 0.9 slice_bitcast_fusion
  20.1 17.4 %all-to-all-done.got_ref = bf16[128,40,128]{2,1,0:T(8,128)(2,1)S(1)} async-done(((bf16[128,40,128]{2,1,0:T(8,128)(2,1)}), bf16[128,40,128]{2,1,0:T(8,128)(2,1)S(1)}, u32[]{:S(2)}, u32[]{:S(2)}) %all-to-all-start) | async-done | bytes 1310752 | tf_op jit(solution)/shard_map/all_to_all | solution.py:694
  37.5 5.4 %combine.1 = (f32[1024,512]{1,0:T(8,128)S(1)}, bf16[1024,512]{1,0:T(8,128)(2,1)S(1)}, bf16[512,512]{1,0:T(8,128)(2,1)S(1)}, bf16[512,512]{1,0:T(8,128)(2,1)S(1)}...) custom-call(s32[4]{0:T(128)S(1)} %pad_add_fusion.place_ref, bf16[128,40,128]{2,1,0:T(8,128)(2,1)S(1)} %all-to-all-done.got_ref, ...), custom_call_target="tpu_custom_call" | custom-call | tf_op jit(solution)/shard_map/combine/pallas_call | solution.py:218
  42.9 0.1 collective-permute-start
  43.0 1.7 %collective-permute-start.1 = (bf16[128,512]{1,0:T(8,128)(2,1)S(1)}, bf16[128,512]{1,0:T(8,128)(2,1)S(1)}, u32[]{:S(2)}, u32[]{:S(2)}) collective-permute-start(bf16[128,512]{1,0:T(8,128)(2,1)S(1)} %get-tuple-element.53), channel_id=1, source_target_pairs={{0,31},{1,2},{2,1},{3,4},{4,3},{5,6},{6,5},{7,8},{8,7},{9,10},{10,... | collective-permute-start | bytes 393224 | tf_op jit(solution)/shard_map/ppermute | solution.py:714
  44.8 1.4 %collective-permute-start.4 = (bf16[512,512]{1,0:T(8,128)(2,1)S(1)}, bf16[512,512]{1,0:T(8,128)(2,1)S(1)}, u32[]{:S(2)}, u32[]{:S(2)}) collective-permute-start(bf16[512,512]{1,0:T(8,128)(2,1)S(1)} %get-tuple-element.63), channel_id=1, source_target_pairs={{0,32},{32,0},{64,96},{96,64},{1,33},{33,1},{65,97},{97,65},{2,34}... | collective-permute-start | bytes 1572872 | tf_op jit(solution)/shard_map/ppermute | solution.py:716
  46.1 2.7 %collective-permute-start.5 = (bf16[512,512]{1,0:T(8,128)(2,1)S(1)}, bf16[512,512]{1,0:T(8,128)(2,1)S(1)}, u32[]{:S(2)}, u32[]{:S(2)}) collective-permute-start(bf16[512,512]{1,0:T(8,128)(2,1)S(1)} %get-tuple-element.64), channel_id=1, source_target_pairs={{0,0},{96,96},{32,64},{64,32},{1,1},{97,97},{33,65},{65,33},{2,2},... | collective-permute-start | bytes 1572872 | tf_op jit(solution)/shard_map/ppermute | solution.py:715
  48.9 5.5 %project.2 = (bf16[1024,512]{1,0:T(8,128)(2,1)S(1)}, bf16[1024,512]{1,0:T(8,128)(2,1)S(1)}, bf16[512,1024]{1,0:T(8,128)(2,1)S(1)}, f32[512,1024]{1,0:T(8,128)S(1...) custom-call(bf16[1024,512]{1,0:T(8,128)(2,1)S(1)} %get-tuple-element.48.normed_ref, bf16[512,512]{1,0:T(8,128)(2,1)S(1)} %copy-done.3, ...), custom_call_target="tpu_custom_call" | custom-call | flops 1610612736 | bytes 5242880 | tf_op jit(solution)/shard_map/project/pallas_call | solution.py:319
  54.4 0.0 collective-permute-done.third_ref
  54.4 0.0 collective-permute-done.1.fourth_ref
  54.4 0.6 corners.2
  55.0 0.1 collective-permute-start.2
  55.1 4.8 %collective-permute-start.3 = (bf16[128,512]{1,0:T(8,128)(2,1)S(1)}, bf16[128,512]{1,0:T(8,128)(2,1)S(1)}, u32[]{:S(2)}, u32[]{:S(2)}) collective-permute-start(bf16[128,512]{1,0:T(8,128)(2,1)S(1)} %get-tuple-element.61), channel_id=1, source_target_pairs={{0,0},{96,96},{32,64},{64,32},{1,1},{97,97},{33,65},{65,33},{2,2},... | collective-permute-start | bytes 393224 | tf_op jit(solution)/shard_map/ppermute | solution.py:720
  59.9 2.2 %near.2 = (f32[512,1024]{1,0:T(8,128)S(1)}, f32[8,1024]{1,0:T(8,128)S(1)}, f32[8,1024]{1,0:T(8,128)S(1)}) custom-call(s32[4]{0:T(128)S(1)} %pad_add_fusion.place_ref, bf16[1024,512]{1,0:T(8,128)(2,1)S(1)} %get-tuple-element.49.query_ref, ...), custom_call_target="tpu_custom_call", output_to_operand_aliasing={{0}: (8, {}), {1}: (9, {}), {2}: (10, {})} | custom-call | flops 8589934592 | bytes 8388608 | tf_op jit(solution)/shard_map/near/pallas_call | solution.py:394
  62.1 0.0 collective-permute-done.4.first_ref
  62.1 0.0 collective-permute-done.5.second_ref
  62.1 5.4 %far.2 = (f32[1024,512]{1,0:T(8,128)S(1)}, bf16[2,512,512]{2,1,0:T(8,128)(2,1)S(1)}, bf16[2,512,512]{2,1,0:T(8,128)(2,1)S(1)}, bf16[1024,512]{1,0:T(8,128)(2,1)S...) custom-call(s32[4]{0:T(128)S(1)} %pad_add_fusion.place_ref, ...), custom_call_target="tpu_custom_call" | custom-call | flops 8589934592 | bytes 8388608 | tf_op jit(solution)/shard_map/far/pallas_call | solution.py:542
  67.5 0.0 collective-permute-done.2.first_ref
  67.5 0.0 collective-permute-done.3.second_ref
  67.5 0.0 copy-start.2
  67.5 2.3 %edges.2 = (f32[1024,512]{1,0:T(8,128)S(1)}, bf16[1024,512]{1,0:T(8,128)(2,1)S(1)}, bf16[512,512]{1,0:T(8,128)(2,1)S(1)}, bf16[512,512]{1,0:T(8,128)(2,1)S(1)}, ...) custom-call(s32[4]{0:T(128)S(1)} %pad_add_fusion.place_ref, ...), custom_call_target="tpu_custom_call", output_to_operand_aliasing={{0}: (14, {}), {1}: (15, {}), {2}: (16, {}), {3}: (17, {})} | custom-call | tf_op jit(solution)/shard_map/edges/pallas_call | solution.py:672
  69.9 0.1 collective-permute-start.6
  70.0 4.1 %collective-permute-start.7 = (bf16[128,512]{1,0:T(8,128)(2,1)S(1)}, bf16[128,512]{1,0:T(8,128)(2,1)S(1)}, u32[]{:S(2)}, u32[]{:S(2)}) collective-permute-start(bf16[128,512]{1,0:T(8,128)(2,1)S(1)} %get-tuple-element.76), channel_id=1, source_target_pairs={{0,31},{1,2},{2,1},{3,4},{4,3},{5,6},{6,5},{7,8},{8,7},{9,10},{10,... | collective-permute-start | bytes 393224 | tf_op jit(solution)/shard_map/ppermute | solution.py:714
  74.1 0.0 collective-permute-start.10
  74.1 3.6 %collective-permute-start.11 = (bf16[512,512]{1,0:T(8,128)(2,1)S(1)}, bf16[512,512]{1,0:T(8,128)(2,1)S(1)}, u32[]{:S(2)}, u32[]{:S(2)}) collective-permute-start(bf16[512,512]{1,0:T(8,128)(2,1)S(1)} %get-tuple-element.87), channel_id=1, source_target_pairs={{0,0},{96,96},{32,64},{64,32},{1,1},{97,97},{33,65},{65,33},{2,2},... | collective-permute-start | bytes 1572872 | tf_op jit(solution)/shard_map/ppermute | solution.py:715
  77.7 5.5 %project.3 = (bf16[1024,512]{1,0:T(8,128)(2,1)S(1)}, bf16[1024,512]{1,0:T(8,128)(2,1)S(1)}, bf16[512,1024]{1,0:T(8,128)(2,1)S(1)}, f32[512,1024]{1,0:T(8,128)S(1...) custom-call(bf16[1024,512]{1,0:T(8,128)(2,1)S(1)} %get-tuple-element.71.normed_ref, bf16[512,512]{1,0:T(8,128)(2,1)S(1)} %copy-done.2, ...), custom_call_target="tpu_custom_call" | custom-call | flops 1610612736 | bytes 5242880 | tf_op jit(solution)/shard_map/project/pallas_call | solution.py:319
  83.2 0.0 collective-permute-done.6.third_ref
  83.2 0.0 collective-permute-done.7.fourth_ref
  83.2 0.6 corners.3
  83.8 0.1 collective-permute-start.8
  83.9 4.0 %collective-permute-start.9 = (bf16[128,512]{1,0:T(8,128)(2,1)S(1)}, bf16[128,512]{1,0:T(8,128)(2,1)S(1)}, u32[]{:S(2)}, u32[]{:S(2)}) collective-permute-start(bf16[128,512]{1,0:T(8,128)(2,1)S(1)} %get-tuple-element.84), channel_id=1, source_target_pairs={{0,0},{96,96},{32,64},{64,32},{1,1},{97,97},{33,65},{65,33},{2,2},... | collective-permute-start | bytes 393224 | tf_op jit(solution)/shard_map/ppermute | solution.py:720
  88.0 2.2 %near.3 = (f32[512,1024]{1,0:T(8,128)S(1)}, f32[8,1024]{1,0:T(8,128)S(1)}, f32[8,1024]{1,0:T(8,128)S(1)}) custom-call(s32[4]{0:T(128)S(1)} %pad_add_fusion.place_ref, bf16[1024,512]{1,0:T(8,128)(2,1)S(1)} %get-tuple-element.72.query_ref, ...), custom_call_target="tpu_custom_call", output_to_operand_aliasing={{0}: (8, {}), {1}: (9, {}), {2}: (10, {})} | custom-call | flops 8589934592 | bytes 8388608 | tf_op jit(solution)/shard_map/near/pallas_call | solution.py:394
  90.2 0.0 collective-permute-done.10.first_ref
  90.2 0.0 collective-permute-done.11.second_ref
  90.2 5.2 %far.3 = (f32[1024,512]{1,0:T(8,128)S(1)}, bf16[2,512,512]{2,1,0:T(8,128)(2,1)S(1)}, bf16[2,512,512]{2,1,0:T(8,128)(2,1)S(1)}) custom-call(s32[4]{0:T(128)S(1)} %pad_add_fusion.place_ref, bf16[1024,512]{1,0:T(8,128)(2,1)S(1)} %get-tuple-element.72.query_ref, f32[512,1024]{1,0:T(8,128)S(1)} %get-tuple-element.80.mixed_ref, ...), custom_call_target="tpu_custom_call" | custom-call | flops 8589934592 | bytes 8388608 | tf_op jit(solution)/shard_map/far/pallas_call | solution.py:542
  95.4 0.0 collective-permute-done.8.first_ref
  95.4 0.0 collective-permute-done.9.second_ref
  95.4 3.2 %edges.3 = bf16[16,64,512]{2,1,0:T(8,128)(2,1)} custom-call(s32[4]{0:T(128)S(1)} %pad_add_fusion.place_ref, bf16[1024,512]{1,0:T(8,128)(2,1)S(1)} %get-tuple-element.72.query_ref, f32[512,1024]{1,0:T(8,128)S(1)} %get-tuple-element.80.mixed_ref, f32[8,1024]{1,0:T(8,128)S(1)} %get-tuple-element.81.highest_ref, f32[8,1024]{1,0:T(8,128)S(1)} %get-tuple-element.82.total_ref, ...), custom_call_target="tpu_custom_call" | custom-call | tf_op jit(solution)/shard_map/edges/pallas_call | solution.py:672
  (14 shorter events, 0.0 us)
Async XLA Ops:
  0.0 15.3 %copy-start.4 = (f32[2,512]{1,0:T(2,128)S(1)}, f32[2,512]{1,0:T(2,128)}, u32[]{:S(2)}) copy-start(f32[2,512]{1,0:T(2,128)} %gain_ref.1) | copy-start | bytes 12292
  0.0 15.3 %copy-start.5 = (bf16[2,512,512]{2,1,0:T(8,128)(2,1)S(1)}, bf16[2,512,512]{2,1,0:T(8,128)(2,1)}, u32[]{:S(2)}) copy-start(bf16[2,512,512]{2,1,0:T(8,128)(2,1)} %param.20) | copy-start | bytes 3145732
  3.8 33.7 %all-to-all-start = ((bf16[128,40,128]{2,1,0:T(8,128)(2,1)}), bf16[128,40,128]{2,1,0:T(8,128)(2,1)S(1)}, u32[]{:S(2)}, u32[]{:S(2)}) async-start(bf16[128,40,128]{2,1,0:T(8,128)(2,1)} %dispatch.1), calls=%async_computation | async-start | bytes 2621440 | tf_op jit(solution)/shard_map/all_to_all | solution.py:694
  15.9 2.5 %copy-start.6 = (bf16[2,512,512]{2,1,0:T(8,128)(2,1)S(1)}, bf16[2,512,512]{2,1,0:T(8,128)(2,1)}, u32[]{:S(2)}) copy-start(bf16[2,512,512]{2,1,0:T(8,128)(2,1)} %param.19) | copy-start | bytes 3145732
  15.9 3.3 %copy-start.7 = (bf16[2,512,512]{2,1,0:T(8,128)(2,1)S(1)}, bf16[2,512,512]{2,1,0:T(8,128)(2,1)}, u32[]{:S(2)}) copy-start(bf16[2,512,512]{2,1,0:T(8,128)(2,1)} %param.21) | copy-start | bytes 3145732
  37.5 11.4 %copy-start.3 = (bf16[512,512]{1,0:T(8,128)(2,1)S(1)}, bf16[512,512]{1,0:T(8,128)(2,1)}, u32[]{:S(2)}) copy-start(bf16[512,512]{1,0:T(8,128)(2,1)} %get-tuple-element.98.query_w) | copy-start | bytes 1572868
  42.9 11.5 %collective-permute-start = (bf16[128,512]{1,0:T(8,128)(2,1)S(1)}, bf16[128,512]{1,0:T(8,128)(2,1)S(1)}, u32[]{:S(2)}, u32[]{:S(2)}) collective-permute-start(bf16[128,512]{1,0:T(8,128)(2,1)S(1)} %get-tuple-element.52), channel_id=1, source_target_pairs={{0,1},{1,0},{2,3},{3,2},{4,5},{5,4},{6,7},{7,6},{8,9},{9,8},{10,11... | collective-permute-start | bytes 393224 | tf_op jit(solution)/shard_map/ppermute | solution.py:713
  43.0 11.4 %collective-permute-start.1 = (bf16[128,512]{1,0:T(8,128)(2,1)S(1)}, bf16[128,512]{1,0:T(8,128)(2,1)S(1)}, u32[]{:S(2)}, u32[]{:S(2)}) collective-permute-start(bf16[128,512]{1,0:T(8,128)(2,1)S(1)} %get-tuple-element.53), channel_id=1, source_target_pairs={{0,31},{1,2},{2,1},{3,4},{4,3},{5,6},{6,5},{7,8},{8,7},{9,10},{10,... | collective-permute-start | bytes 393224 | tf_op jit(solution)/shard_map/ppermute | solution.py:714
  44.8 17.3 %collective-permute-start.4 = (bf16[512,512]{1,0:T(8,128)(2,1)S(1)}, bf16[512,512]{1,0:T(8,128)(2,1)S(1)}, u32[]{:S(2)}, u32[]{:S(2)}) collective-permute-start(bf16[512,512]{1,0:T(8,128)(2,1)S(1)} %get-tuple-element.63), channel_id=1, source_target_pairs={{0,32},{32,0},{64,96},{96,64},{1,33},{33,1},{65,97},{97,65},{2,34}... | collective-permute-start | bytes 1572872 | tf_op jit(solution)/shard_map/ppermute | solution.py:716
  46.1 15.9 %collective-permute-start.5 = (bf16[512,512]{1,0:T(8,128)(2,1)S(1)}, bf16[512,512]{1,0:T(8,128)(2,1)S(1)}, u32[]{:S(2)}, u32[]{:S(2)}) collective-permute-start(bf16[512,512]{1,0:T(8,128)(2,1)S(1)} %get-tuple-element.64), channel_id=1, source_target_pairs={{0,0},{96,96},{32,64},{64,32},{1,1},{97,97},{33,65},{65,33},{2,2},... | collective-permute-start | bytes 1572872 | tf_op jit(solution)/shard_map/ppermute | solution.py:715
  55.0 12.5 %collective-permute-start.2 = (bf16[128,512]{1,0:T(8,128)(2,1)S(1)}, bf16[128,512]{1,0:T(8,128)(2,1)S(1)}, u32[]{:S(2)}, u32[]{:S(2)}) collective-permute-start(bf16[128,512]{1,0:T(8,128)(2,1)S(1)} %get-tuple-element.60), channel_id=1, source_target_pairs={{0,32},{32,0},{64,96},{96,64},{1,33},{33,1},{65,97},{97,65},{2,34}... | collective-permute-start | bytes 393224 | tf_op jit(solution)/shard_map/ppermute | solution.py:721
  55.1 12.4 %collective-permute-start.3 = (bf16[128,512]{1,0:T(8,128)(2,1)S(1)}, bf16[128,512]{1,0:T(8,128)(2,1)S(1)}, u32[]{:S(2)}, u32[]{:S(2)}) collective-permute-start(bf16[128,512]{1,0:T(8,128)(2,1)S(1)} %get-tuple-element.61), channel_id=1, source_target_pairs={{0,0},{96,96},{32,64},{64,32},{1,1},{97,97},{33,65},{65,33},{2,2},... | collective-permute-start | bytes 393224 | tf_op jit(solution)/shard_map/ppermute | solution.py:720
  67.5 10.1 %copy-start = (bf16[512,512]{1,0:T(8,128)(2,1)S(1)}, bf16[512,512]{1,0:T(8,128)(2,1)}, u32[]{:S(2)}) copy-start(bf16[512,512]{1,0:T(8,128)(2,1)} %get-tuple-element.95.key_w) | copy-start | bytes 1572868
  67.5 10.1 %copy-start.2 = (bf16[512,512]{1,0:T(8,128)(2,1)S(1)}, bf16[512,512]{1,0:T(8,128)(2,1)}, u32[]{:S(2)}) copy-start(bf16[512,512]{1,0:T(8,128)(2,1)} %get-tuple-element.97.query_w) | copy-start | bytes 1572868
  69.9 13.4 %collective-permute-start.6 = (bf16[128,512]{1,0:T(8,128)(2,1)S(1)}, bf16[128,512]{1,0:T(8,128)(2,1)S(1)}, u32[]{:S(2)}, u32[]{:S(2)}) collective-permute-start(bf16[128,512]{1,0:T(8,128)(2,1)S(1)} %get-tuple-element.75), channel_id=1, source_target_pairs={{0,1},{1,0},{2,3},{3,2},{4,5},{5,4},{6,7},{7,6},{8,9},{9,8},{10,11... | collective-permute-start | bytes 393224 | tf_op jit(solution)/shard_map/ppermute | solution.py:713
  70.0 13.3 %collective-permute-start.7 = (bf16[128,512]{1,0:T(8,128)(2,1)S(1)}, bf16[128,512]{1,0:T(8,128)(2,1)S(1)}, u32[]{:S(2)}, u32[]{:S(2)}) collective-permute-start(bf16[128,512]{1,0:T(8,128)(2,1)S(1)} %get-tuple-element.76), channel_id=1, source_target_pairs={{0,31},{1,2},{2,1},{3,4},{4,3},{5,6},{6,5},{7,8},{8,7},{9,10},{10,... | collective-permute-start | bytes 393224 | tf_op jit(solution)/shard_map/ppermute | solution.py:714
  74.1 16.1 %collective-permute-start.10 = (bf16[512,512]{1,0:T(8,128)(2,1)S(1)}, bf16[512,512]{1,0:T(8,128)(2,1)S(1)}, u32[]{:S(2)}, u32[]{:S(2)}) collective-permute-start(bf16[512,512]{1,0:T(8,128)(2,1)S(1)} %get-tuple-element.86), channel_id=1, source_target_pairs={{0,32},{32,0},{64,96},{96,64},{1,33},{33,1},{65,97},{97,65},{2,34}... | collective-permute-start | bytes 1572872 | tf_op jit(solution)/shard_map/ppermute | solution.py:716
  74.1 16.1 %collective-permute-start.11 = (bf16[512,512]{1,0:T(8,128)(2,1)S(1)}, bf16[512,512]{1,0:T(8,128)(2,1)S(1)}, u32[]{:S(2)}, u32[]{:S(2)}) collective-permute-start(bf16[512,512]{1,0:T(8,128)(2,1)S(1)} %get-tuple-element.87), channel_id=1, source_target_pairs={{0,0},{96,96},{32,64},{64,32},{1,1},{97,97},{33,65},{65,33},{2,2},... | collective-permute-start | bytes 1572872 | tf_op jit(solution)/shard_map/ppermute | solution.py:715
  83.8 11.6 %collective-permute-start.8 = (bf16[128,512]{1,0:T(8,128)(2,1)S(1)}, bf16[128,512]{1,0:T(8,128)(2,1)S(1)}, u32[]{:S(2)}, u32[]{:S(2)}) collective-permute-start(bf16[128,512]{1,0:T(8,128)(2,1)S(1)} %get-tuple-element.83), channel_id=1, source_target_pairs={{0,32},{32,0},{64,96},{96,64},{1,33},{33,1},{65,97},{97,65},{2,34}... | collective-permute-start | bytes 393224 | tf_op jit(solution)/shard_map/ppermute | solution.py:721
  83.9 11.5 %collective-permute-start.9 = (bf16[128,512]{1,0:T(8,128)(2,1)S(1)}, bf16[128,512]{1,0:T(8,128)(2,1)S(1)}, u32[]{:S(2)}, u32[]{:S(2)}) collective-permute-start(bf16[128,512]{1,0:T(8,128)(2,1)S(1)} %get-tuple-element.84), channel_id=1, source_target_pairs={{0,0},{96,96},{32,64},{64,32},{1,1},{97,97},{33,65},{65,33},{2,2},... | collective-permute-start | bytes 393224 | tf_op jit(solution)/shard_map/ppermute | solution.py:720
  88.0 2.2 %copy-start.1 = (bf16[512,512]{1,0:T(8,128)(2,1)S(1)}, bf16[512,512]{1,0:T(8,128)(2,1)}, u32[]{:S(2)}) copy-start(bf16[512,512]{1,0:T(8,128)(2,1)} %get-tuple-element.91.out_w) | copy-start | bytes 1572868

commit v4 on v3

--- a/solution.py
+++ b/solution.py
@@ -26,7 +26,6 @@
 BF16 = jnp.bfloat16
 
 VMEM = pl.BlockSpec(memory_space=pltpu.VMEM)
-SMEM = pl.BlockSpec(memory_space=pltpu.SMEM)
 HBM = pl.BlockSpec(memory_space=pl.ANY)
 PARAMS = pltpu.CompilerParams(vmem_limit_bytes=40 * 1024 * 1024)
 WIDE = FRAME * BLOCK
@@ -92,7 +91,7 @@
 def dispatch(owner, cell, valid, feat):
     return pl.pallas_call(
         dispatch_kernel,
-        out_shape=jax.ShapeDtypeStruct((DEVICES, ROWS, 128), BF16),
+        out_shape=pltpu.VMEM((DEVICES, ROWS, 128), BF16),
         in_specs=[HBM] * 4,
         out_specs=VMEM,
         scratch_shapes=[pltpu.VMEM((1, OBS), jnp.int32)] * 3
@@ -119,11 +118,11 @@
     return jnp.where(choose, x, y)
 
 
-def store_normed(sector, rows, refs, place_ref):
+def store_normed(sector, rows, refs):
     normed_ref, first_ref, second_ref, third_ref, fourth_ref = refs
     here = slice(sector * BLOCK, (sector + 1) * BLOCK)
     normed_ref[sector * COLUMN : (sector + 1) * COLUMN, :] = rows
-    even = place_ref[2] == 0
+    even = lax.axis_index("lat") % 2 == 0
     top = rows[:BLOCK]
     low = rows[BLOCK:]
     first_ref[here, :] = pick(even, low, top)
@@ -132,7 +131,7 @@
         third_ref[...] = rows
         fourth_ref[...] = rows
     if sector == SECTORS - 1:
-        even = place_ref[3] == 0
+        even = lax.axis_index("lon") % 2 == 0
         third_ref[...] = pick(even, rows, third_ref[...])
         fourth_ref[...] = pick(even, fourth_ref[...], rows)
 
@@ -153,7 +152,7 @@
 
 
 def combine_kernel(
-    place_ref, got_ref, embed_hbm, grid_hbm, gain_ref, hidden_ref, *rest
+    got_ref, embed_hbm, grid_hbm, gain_ref, hidden_ref, *rest
 ):
     refs = rest[:5]
     emb_ref, tag_ref, hot_ref, embed_ref, grid_ref, sems = rest[5:]
@@ -211,14 +210,14 @@
                 pieces.append(mean + static)
             hidden = jnp.concatenate(pieces, axis=0)
             hidden_ref[sector * COLUMN : (sector + 1) * COLUMN, :] = hidden
-            store_normed(sector, norm_rows(hidden, gain), refs, place_ref)
-
-
-def combine(place, got, w_embed, grid_feat, gains):
+            store_normed(sector, norm_rows(hidden, gain), refs)
+
+
+def combine(got, w_embed, grid_feat, gains):
     return pl.pallas_call(
         combine_kernel,
         out_shape=(pltpu.VMEM((CELLS, D), F32),) + NORMED_SHAPES,
-        in_specs=[SMEM, VMEM, HBM, HBM, VMEM],
+        in_specs=[VMEM, HBM, HBM, VMEM],
         out_specs=(VMEM,) * 6,
         scratch_shapes=[
             pltpu.VMEM((SLOTS, D), BF16),
@@ -230,7 +229,7 @@
         ],
         compiler_params=PARAMS,
         name="combine",
-    )(place, got, w_embed, grid_feat, gains)
+    )(got, w_embed, grid_feat, gains)
 
 
 def head_pair(query):
@@ -252,11 +251,14 @@
     return expo.astype(BF16), highest, fold(expo, jnp.sum)
 
 
+LAGS = (0, 2, 3)
+
+
 def staged(units, stages):
     held = {}
-    for turn in range(len(units) + len(stages) - 1):
-        for number, stage in enumerate(stages):
-            at = turn - number
+    for turn in range(len(units) + LAGS[-1]):
+        for lag, stage in zip(LAGS, stages):
+            at = turn - lag
             if 0 <= at < len(units):
                 held[at] = stage(units[at], held.get(at))
 
@@ -327,48 +329,48 @@
     )(normed, w_query, w_key, w_value)
 
 
-def sides_of(place_ref, third_ref, fourth_ref):
-    even = place_ref[3] == 0
+def sides_of(third_ref, fourth_ref):
+    even = lax.axis_index("lon") % 2 == 0
     third = third_ref[...]
     fourth = fourth_ref[...]
     return pick(even, fourth, third), pick(even, third, fourth)
 
 
-def rows_of(place_ref, first_ref, second_ref):
-    even = place_ref[2] == 0
+def rows_of(first_ref, second_ref):
+    even = lax.axis_index("lat") % 2 == 0
     first = first_ref[...]
     second = second_ref[...]
     return pick(even, second, first), pick(even, first, second)
 
 
-def corners_kernel(place_ref, third_ref, fourth_ref, first_ref, second_ref):
-    west, east = sides_of(place_ref, third_ref, fourth_ref)
-    even = place_ref[2] == 0
+def corners_kernel(third_ref, fourth_ref, first_ref, second_ref):
+    west, east = sides_of(third_ref, fourth_ref)
+    even = lax.axis_index("lat") % 2 == 0
     top = jnp.concatenate([west[:BLOCK], east[:BLOCK]], axis=0)
     low = jnp.concatenate([west[BLOCK:], east[BLOCK:]], axis=0)
     first_ref[...] = pick(even, low, top)
     second_ref[...] = pick(even, top, low)
 
 
-def corners(place, third, fourth):
+def corners(third, fourth):
     shape = pltpu.VMEM((COLUMN, D), BF16)
     return pl.pallas_call(
         corners_kernel,
         out_shape=(shape, shape),
-        in_specs=[SMEM] + [VMEM] * 2,
+        in_specs=[VMEM] * 2,
         out_specs=(VMEM,) * 2,
         compiler_params=PARAMS,
         name="corners",
-    )(place, third, fourth)
+    )(third, fourth)
 
 
 def near_kernel(
-    place_ref, query_ref, key_ref, value_ref, third_ref, fourth_ref, key_w, value_w, mixed_in, highest_in, total_in,
+    query_ref, key_ref, value_ref, third_ref, fourth_ref, key_w, value_w, mixed_in, highest_in, total_in,
     mixed_ref, highest_ref, total_ref,
 ):
     del mixed_in, highest_in, total_in
     outs = (query_ref, mixed_ref, highest_ref, total_ref)
-    sides = jnp.concatenate(sides_of(place_ref, third_ref, fourth_ref), axis=0)
+    sides = jnp.concatenate(sides_of(third_ref, fourth_ref), axis=0)
     side_keys = jnp.dot(sides, key_w[...], preferred_element_type=F32).astype(BF16)
     side_values = lax.dot_general(value_w[...], sides, NT, preferred_element_type=F32).astype(BF16)
     columns = {}
@@ -390,17 +392,17 @@
     near_columns(columns, *outs)
 
 
-def near(place, query, key, value, third, fourth, w_key, w_value, parts):
+def near(query, key, value, third, fourth, w_key, w_value, parts):
     return pl.pallas_call(
         near_kernel,
         out_shape=NEAR_SHAPES,
-        in_specs=[SMEM] + [VMEM] * 10,
+        in_specs=[VMEM] * 10,
         out_specs=(VMEM,) * 3,
-        input_output_aliases={8: 0, 9: 1, 10: 2},
+        input_output_aliases={7: 0, 8: 1, 9: 2},
         compiler_params=PARAMS,
         cost_estimate=pl.CostEstimate(flops=8 << 30, transcendentals=4 << 20, bytes_accessed=8 << 20),
         name="near",
-    )(place, query, key, value, third, fourth, w_key, w_value, *parts)
+    )(query, key, value, third, fourth, w_key, w_value, *parts)
 
 
 def merge(tiles, head, cells, near_refs, store):
@@ -425,25 +427,26 @@
     return jnp.where(iota(x.shape, 1) < BLOCK, x, y)
 
 
-def beyond_grid(place_ref):
-    return (place_ref[0] == 0, place_ref[0] == place_ref[1] - 1)
+def beyond_grid():
+    lat = lax.axis_index("lat")
+    return (lat == 0, lat == lax.axis_size("lat") - 1)
 
 
 def make_far_kernel(last):
     def far_kernel(
-        place_ref, query_ref, mixed_ref, highest_ref, total_ref, first_ref, second_ref,
+        query_ref, mixed_ref, highest_ref, total_ref, first_ref, second_ref,
         hidden_ref, gain_ref, key_w, value_w, out_w, *rest,
     ):
         new_ref, key_f, value_f = rest[:3]
         refs = rest[3:-1]
         att_ref = rest[-1]
         near_refs = (mixed_ref, highest_ref, total_ref)
-        for band, rows in enumerate(rows_of(place_ref, first_ref, second_ref)):
+        for band, rows in enumerate(rows_of(first_ref, second_ref)):
             key_f[band] = jnp.dot(rows, key_w[...], preferred_element_type=F32).astype(BF16)
             value_f[band] = lax.dot_general(
                 value_w[...], rows, NT, preferred_element_type=F32
             ).astype(BF16)
-        beyond = beyond_grid(place_ref)
+        beyond = beyond_grid()
         span = 4 * BLOCK
 
         def hide(scores):
@@ -525,13 +528,12 @@
                         at // COLUMN + sub,
                         normed[sub * COLUMN : (sub + 1) * COLUMN],
                         refs + (None, None),
-                        place_ref,
                     )
 
     return far_kernel
 
 
-def far(place, query, parts, first, second, hidden, gain, w_key, w_value, w_out, last):
+def far(query, parts, first, second, hidden, gain, w_key, w_value, w_out, last):
     out_shape = (
         pltpu.VMEM((CELLS, D), F32),
         pltpu.VMEM((BANDS, HALO, D), BF16),
@@ -542,18 +544,18 @@
     return pl.pallas_call(
         make_far_kernel(last),
         out_shape=out_shape,
-        in_specs=[SMEM] + [VMEM] * 11,
+        in_specs=[VMEM] * 11,
         out_specs=(VMEM,) * len(out_shape),
         scratch_shapes=[pltpu.VMEM((D, CELLS), BF16)],
         compiler_params=PARAMS,
         cost_estimate=pl.CostEstimate(flops=8 << 30, transcendentals=4 << 20, bytes_accessed=8 << 20),
         name="far",
-    )(place, query, *parts, first, second, hidden, gain, w_key, w_value, w_out)
+    )(query, *parts, first, second, hidden, gain, w_key, w_value, w_out)
 
 
 def make_edge_kernel(last):
     def edge_kernel(
-        place_ref, query_ref, mixed_ref, highest_ref, total_ref, first_ref, second_ref,
+        query_ref, mixed_ref, highest_ref, total_ref, first_ref, second_ref,
         hidden_ref, gain_ref, key_w, value_w, out_w, key_f, value_f, *rest,
     ):
         near_refs = (mixed_ref, highest_ref, total_ref)
@@ -563,12 +565,12 @@
         else:
             new_ref = rest[4]
             refs = rest[5:10]
-        rows = jnp.concatenate(rows_of(place_ref, first_ref, second_ref), axis=0)
+        rows = jnp.concatenate(rows_of(first_ref, second_ref), axis=0)
         corner_keys = jnp.dot(rows, key_w[...], preferred_element_type=F32).astype(BF16)
         corner_values = lax.dot_general(
             value_w[...], rows, NT, preferred_element_type=F32
         ).astype(BF16)
-        beyond = beyond_grid(place_ref)
+        beyond = beyond_grid()
         starts = (0, HALO - 2 * BLOCK)
 
         def scored(unit, _):
@@ -638,7 +640,7 @@
                 continue
             new_ref[at : at + COLUMN, :] = hidden
             normed = norm_rows(hidden, gain)
-            store_normed(at // COLUMN, normed, refs, place_ref)
+            store_normed(at // COLUMN, normed, refs)
         if last:
             for band in range(BANDS):
                 for r in range(8):
@@ -657,7 +659,7 @@
     return edge_kernel
 
 
-def edges(place, query, parts, first, second, hidden, gain, w_key, w_value, w_out, inner, last):
+def edges(query, parts, first, second, hidden, gain, w_key, w_value, w_out, inner, last):
     new, key_f, value_f, *normed = inner
     scratch = [pltpu.VMEM((D, 2 * COLUMN), BF16)]
     if last:
@@ -668,17 +670,17 @@
     else:
         out_shape = (pltpu.VMEM((CELLS, D), F32),) + NORMED_SHAPES
         out_specs = (VMEM,) * 6
-        aliases = {14: 0, 15: 1, 16: 2, 17: 3}
+        aliases = {13: 0, 14: 1, 15: 2, 16: 3}
     return pl.pallas_call(
         make_edge_kernel(last),
         out_shape=out_shape,
-        in_specs=[SMEM] + [VMEM] * (14 + len(normed)),
+        in_specs=[VMEM] * (14 + len(normed)),
         out_specs=out_specs,
         scratch_shapes=scratch,
         input_output_aliases=aliases,
         compiler_params=PARAMS,
         name="edges",
-    )(place, query, *parts, first, second, hidden, gain, w_key, w_value, w_out, key_f, value_f, new, *normed)
+    )(query, *parts, first, second, hidden, gain, w_key, w_value, w_out, key_f, value_f, new, *normed)
 
 
 def local(
@@ -691,17 +693,15 @@
         off_chip(obs_valid.reshape(1, OBS)),
         off_chip(obs_feat),
     )
-    got = lax.all_to_all(send, ("lat", "lon"), split_axis=0, concat_axis=0, tiled=True)
+    got = lax.all_to_all(on_chip(send), ("lat", "lon"), split_axis=0, concat_axis=0, tiled=True)
     lat_count = lax.axis_size("lat")
     lon_count = lax.axis_size("lon")
-    lat = lax.axis_index("lat")
-    lon = lax.axis_index("lon")
-    place = jnp.stack([lat, jnp.int32(lat_count), lat % 2, lon % 2])
-    hidden, *normed = combine(place, got, off_chip(w_embed), off_chip(grid_feat), gains)
+    hidden, *normed = combine(got, off_chip(w_embed), off_chip(grid_feat), gains)
     lat_first = [(i, i ^ 1) for i in range(lat_count)]
     lat_second = [(0, 0), (lat_count - 1, lat_count - 1)]
     for i in range(1, lat_count - 1, 2):
         lat_second += [(i, i + 1), (i + 1, i)]
+    lat_round = [(i, (((i + 1) ^ 1) - 1) % lat_count) for i in range(lat_count)]
     lon_first = [(i, i ^ 1) for i in range(lon_count)]
     lon_second = [(i, (((i + 1) ^ 1) - 1) % lon_count) for i in range(lon_count)]
     for layer in range(LAYERS):
@@ -716,21 +716,21 @@
         first = lax.ppermute(trades[0], "lat", lat_first)
         query, key, value, *parts = project(flat, on_chip(w_query[layer]), key_w, value_w)
         query = on_chip(query)
-        corner = corners(place, third, fourth)
-        corner_second = lax.ppermute(on_chip(corner[1]), "lat", lat_second)
+        corner = corners(third, fourth)
+        corner_second = lax.ppermute(on_chip(corner[1]), "lat", lat_round)
         corner_first = lax.ppermute(on_chip(corner[0]), "lat", lat_first)
         parts = [on_chip(part) for part in parts]
         parts = near(
-            place, query, on_chip(key), on_chip(value), third, fourth, key_w, value_w, parts
+            query, on_chip(key), on_chip(value), third, fourth, key_w, value_w, parts
         )
         parts = [on_chip(part) for part in parts]
         following = min(layer + 1, LAYERS - 1)
         gain = gains[following : following + 1]
         out_w = on_chip(w_out[layer])
-        inner = far(place, query, parts, first, second, hidden, gain, key_w, value_w, out_w, last)
+        inner = far(query, parts, first, second, hidden, gain, key_w, value_w, out_w, last)
         inner = [on_chip(item) for item in inner]
         result = edges(
-            place, query, parts, corner_first, corner_second, hidden, gain, key_w, value_w, out_w, inner, last
+            query, parts, corner_first, corner_second, hidden, gain, key_w, value_w, out_w, inner, last
         )
         if not last:
             hidden, *normed = result

time: 98.9 us -> 88.3 us (0.89)
  Pallas kernels: 41.9 us -> 34.7 us
  starting transfers between devices: 34.2 us -> 30.6 us
  local copies, waits for them, and re-layouts: 4.67 us -> 5.88 us
    pallas_call x9, Pallas kernels: 25.4 us -> 20.1 us  [the longest x2 8.82 us: far(): pl.pallas_call(make_far_kernel(last), out_shape=out_shape, in_specs=[VMEM...]
    ppermute x2, starting transfers between devices: 8.81 us -> 5.17 us  [local(): corner_second = lax.ppermute(on_chip(corner[1]), 'lat', lat_round)]
    ppermute x2, starting transfers between devices: 0.17 us -> 2.67 us  [local(): third = lax.ppermute(trades[2], 'lon', lon_first)]
    ppermute x2, starting transfers between devices: 5.85 us -> 3.86 us  [local(): fourth = lax.ppermute(trades[3], 'lon', lon_second)]
    pallas_call x2, Pallas kernels: 11.1 us -> 9.67 us  [project(): pl.pallas_call(project_kernel, out_shape=(shape, shape, pltpu.VMEM((D, CE...]
    slice x1, local copies, waits for them, and re-layouts: 0.07 us -> 1.27 us  [local(): value_w = on_chip(jnp.transpose(w_value[layer]))]
    all_to_all x1, waiting for transfers between devices: 17.4 us -> 16.3 us  [local(): lax.all_to_all(on_chip(send), ('lat', 'lon'), split_axis=0, concat_axis=0...]
  transfers between devices with their start and end apart: 13 -> 13, of which waited for: 1 -> 2; matrix products, arithmetic and copies ran while one was open for 5% -> 7% of each run, Pallas kernels for 28% -> 25%
where the time goes in v4:
time: 88.3 us; the launch traced here: 88 us
  Pallas kernels  34.7 us (39%)
  starting transfers between devices  30.6 us (35%)
  waiting for transfers between devices  16.5 us (19%)
  local copies, waits for them, and re-layouts  5.88 us (7%)
    all_to_all x1, waiting for transfers between devices, local(): lax.all_to_all(on_chip(send), ('lat', 'lon'), split_axis=0, concat_axis=0...  16.3 us
    all_to_all x1, starting transfers between devices, local(): lax.all_to_all(on_chip(send), ('lat', 'lon'), split_axis=0, concat_axis=0...  11.5 us
    pallas_call x2, Pallas kernels, project(): pl.pallas_call(project_kernel, out_shape=(shape, shape, pltpu.VMEM((D, CE...  9.67 us
    pallas_call x2, Pallas kernels, far(): pl.pallas_call(make_far_kernel(last), out_shape=out_shape, in_specs=[VMEM...  8.82 us
    ppermute x2, starting transfers between devices, local(): second = lax.ppermute(trades[1], 'lat', lat_second)  5.46 us
    ppermute x2, starting transfers between devices, local(): corner_second = lax.ppermute(on_chip(corner[1]), 'lat', lat_round)  5.17 us
    pallas_call x1, Pallas kernels, combine(): pl.pallas_call(combine_kernel, out_shape=(pltpu.VMEM((CELLS, D), F32),) +...  4.96 us
    pallas_call x2, Pallas kernels, edges(): pl.pallas_call(make_edge_kernel(last), out_shape=out_shape, in_specs=[VME...  4.33 us
  transfers between devices with their start and end apart: 13, of which 2 were waited for; matrix products, arithmetic and copies ran while one was open for 7% of the time, Pallas kernels for 25%

profile of v4, /device:TPU:1, one launch (start us, length us, event | category | flops | bytes accessed | tf_op | source)
XLA Modules:
  0.0 88.0 jit_solution(9718281124307900335)
XLA Ops:
  0.0 3.7 %dispatch.1 = bf16[128,40,128]{2,1,0:T(8,128)(2,1)} custom-call(s32[1,1024]{1,0:T(1,128)} %bitcast.29, s32[1,1024]{1,0:T(1,128)} %bitcast.30, s32[1,1024]{1,0:T(1,128)} %bitcast.31, bf16[1024,256]{1,0:T(8,128)(2,1)} %feat_hbm.1), custom_call_target="tpu_custom_call" | custom-call | tf_op jit(solution)/shard_map/dispatch/pallas_call | solution.py:92
  3.7 11.5 %all-to-all-start = ((bf16[128,40,128]{2,1,0:T(8,128)(2,1)}), bf16[128,40,128]{2,1,0:T(8,128)(2,1)S(1)}, u32[]{:S(2)}, u32[]{:S(2)}) async-start(bf16[128,40,128]{2,1,0:T(8,128)(2,1)} %dispatch.1), calls=%async_computation | async-start | bytes 2621440 | tf_op jit(solution)/shard_map/all_to_all | solution.py:696
  15.2 1.3 %fusion = (bf16[1,512,512]{2,1,0:T(8,128)(2,1)S(1)}, bf16[1,512,512]{2,1,0:T(8,128)(2,1)S(1)}) fusion(bf16[2,512,512]{2,1,0:T(8,128)(2,1)} %param.20), kind=kLoop, calls=%fused_computation.6 | loop fusion | bytes 2097152 | tf_op jit(solution)/shard_map/slice | solution.py:710
  16.5 0.2 copy.25
  16.7 0.2 copy.24
  16.9 0.0 copy-start.5
  17.0 0.0 copy-start.6
  17.0 2.4 %slice_bitcast_fusion.2 = (bf16[512,512]{1,0:T(8,128)(2,1)}, bf16[512,512]{1,0:T(8,128)(2,1)}) fusion(bf16[2,512,512]{2,1,0:T(8,128)(2,1)} %param.18), kind=kLoop, calls=%fused_computation.2 | loop fusion | bytes 2097152 | tf_op jit(solution)/shard_map/squeeze | solution.py:717
  19.4 0.0 copy-done.5
  19.4 0.9 slice_bitcast_fusion.1
  20.2 0.9 slice_bitcast_fusion
  21.1 16.3 %all-to-all-done.got_ref = bf16[128,40,128]{2,1,0:T(8,128)(2,1)S(1)} async-done(((bf16[128,40,128]{2,1,0:T(8,128)(2,1)}), bf16[128,40,128]{2,1,0:T(8,128)(2,1)S(1)}, u32[]{:S(2)}, u32[]{:S(2)}) %all-to-all-start) | async-done | bytes 1310752 | tf_op jit(solution)/shard_map/all_to_all | solution.py:696
  37.4 5.0 %combine.1 = (f32[1024,512]{1,0:T(8,128)S(1)}, bf16[1024,512]{1,0:T(8,128)(2,1)S(1)}, bf16[512,512]{1,0:T(8,128)(2,1)S(1)}, bf16[512,512]{1,0:T(8,128)(2,1)S(1)}...) custom-call(bf16[128,40,128]{2,1,0:T(8,128)(2,1)S(1)} %all-to-all-done.got_ref, bf16[256,512]{1,0:T(8,128)(2,1)} %embed_hbm.1, ...), custom_call_target="tpu_custom_call" | custom-call | tf_op jit(solution)/shard_map/combine/pallas_call | solution.py:217
  42.4 0.1 collective-permute-start
  42.5 1.8 %collective-permute-start.1 = (bf16[128,512]{1,0:T(8,128)(2,1)S(1)}, bf16[128,512]{1,0:T(8,128)(2,1)S(1)}, u32[]{:S(2)}, u32[]{:S(2)}) collective-permute-start(bf16[128,512]{1,0:T(8,128)(2,1)S(1)} %get-tuple-element.53), channel_id=1, source_target_pairs={{0,31},{1,2},{2,1},{3,4},{4,3},{5,6},{6,5},{7,8},{8,7},{9,10},{10,... | collective-permute-start | bytes 393224 | tf_op jit(solution)/shard_map/ppermute | solution.py:714
  44.2 1.4 %collective-permute-start.4 = (bf16[512,512]{1,0:T(8,128)(2,1)S(1)}, bf16[512,512]{1,0:T(8,128)(2,1)S(1)}, u32[]{:S(2)}, u32[]{:S(2)}) collective-permute-start(bf16[512,512]{1,0:T(8,128)(2,1)S(1)} %get-tuple-element.63), channel_id=1, source_target_pairs={{0,32},{32,0},{64,96},{96,64},{1,33},{33,1},{65,97},{97,65},{2,34}... | collective-permute-start | bytes 1572872 | tf_op jit(solution)/shard_map/ppermute | solution.py:716
  45.6 2.7 %collective-permute-start.5 = (bf16[512,512]{1,0:T(8,128)(2,1)S(1)}, bf16[512,512]{1,0:T(8,128)(2,1)S(1)}, u32[]{:S(2)}, u32[]{:S(2)}) collective-permute-start(bf16[512,512]{1,0:T(8,128)(2,1)S(1)} %get-tuple-element.64), channel_id=1, source_target_pairs={{0,0},{96,96},{32,64},{64,32},{1,1},{97,97},{33,65},{65,33},{2,2},... | collective-permute-start | bytes 1572872 | tf_op jit(solution)/shard_map/ppermute | solution.py:715
  48.4 4.8 %project.2 = (bf16[1024,512]{1,0:T(8,128)(2,1)S(1)}, bf16[1024,512]{1,0:T(8,128)(2,1)S(1)}, bf16[512,1024]{1,0:T(8,128)(2,1)S(1)}, f32[512,1024]{1,0:T(8,128)S(1...) custom-call(bf16[1024,512]{1,0:T(8,128)(2,1)S(1)} %get-tuple-element.48.normed_ref, bf16[512,512]{1,0:T(8,128)(2,1)S(1)} %copy-done.3, ...), custom_call_target="tpu_custom_call" | custom-call | flops 1610612736 | bytes 5242880 | tf_op jit(solution)/shard_map/project/pallas_call | solution.py:321
  53.2 0.0 collective-permute-done.third_ref
  53.2 0.0 collective-permute-done.1.fourth_ref
  53.2 0.1 corners.2
  53.3 0.1 collective-permute-start.2
  53.4 2.7 %collective-permute-start.3 = (bf16[128,512]{1,0:T(8,128)(2,1)S(1)}, bf16[128,512]{1,0:T(8,128)(2,1)S(1)}, u32[]{:S(2)}, u32[]{:S(2)}) collective-permute-start(bf16[128,512]{1,0:T(8,128)(2,1)S(1)} %get-tuple-element.61), channel_id=1, source_target_pairs={{0,96},{32,64},{64,32},{96,0},{1,97},{33,65},{65,33},{97,1},{2,98}... | collective-permute-start | bytes 393224 | tf_op jit(solution)/shard_map/ppermute | solution.py:720
  56.1 1.6 %near.2 = (f32[512,1024]{1,0:T(8,128)S(1)}, f32[8,1024]{1,0:T(8,128)S(1)}, f32[8,1024]{1,0:T(8,128)S(1)}) custom-call(bf16[1024,512]{1,0:T(8,128)(2,1)S(1)} %get-tuple-element.49.query_ref, bf16[1024,512]{1,0:T(8,128)(2,1)S(1)} %get-tuple-element.50.key_ref, ...), custom_call_target="tpu_custom_call", output_to_operand_aliasing={{0}: (7, {}), {1}: (8, {}), {2}: (9, {})} | custom-call | flops 8589934592 | bytes 8388608 | tf_op jit(solution)/shard_map/near/pallas_call | solution.py:396
  57.7 0.0 collective-permute-done.4.first_ref
  57.7 0.0 collective-permute-done.5.second_ref
  57.7 4.5 %far.2 = (f32[1024,512]{1,0:T(8,128)S(1)}, bf16[2,512,512]{2,1,0:T(8,128)(2,1)S(1)}, bf16[2,512,512]{2,1,0:T(8,128)(2,1)S(1)}, bf16[1024,512]{1,0:T(8,128)(2,1)S...) custom-call(bf16[1024,512]{1,0:T(8,128)(2,1)S(1)} %get-tuple-element.49.query_ref, ...), custom_call_target="tpu_custom_call" | custom-call | flops 8589934592 | bytes 8388608 | tf_op jit(solution)/shard_map/far/pallas_call | solution.py:544
  62.2 0.0 collective-permute-done.2.first_ref
  62.2 0.0 collective-permute-done.3.second_ref
  62.2 0.0 copy-start.2
  62.3 1.7 %edges.2 = (f32[1024,512]{1,0:T(8,128)S(1)}, bf16[1024,512]{1,0:T(8,128)(2,1)S(1)}, bf16[512,512]{1,0:T(8,128)(2,1)S(1)}, bf16[512,512]{1,0:T(8,128)(2,1)S(1)}, ...) custom-call(bf16[1024,512]{1,0:T(8,128)(2,1)S(1)} %get-tuple-element, ...), custom_call_target="tpu_custom_call", output_to_operand_aliasing={{0}: (13, {}), {1}: (14, {}), {2}: (15, {}), {3}: (16, {})} | custom-call | tf_op jit(solution)/shard_map/edges/pallas_call | solution.py:674
  64.0 2.6 %collective-permute-start.6 = (bf16[128,512]{1,0:T(8,128)(2,1)S(1)}, bf16[128,512]{1,0:T(8,128)(2,1)S(1)}, u32[]{:S(2)}, u32[]{:S(2)}) collective-permute-start(bf16[128,512]{1,0:T(8,128)(2,1)S(1)} %get-tuple-element.75), channel_id=1, source_target_pairs={{0,1},{1,0},{2,3},{3,2},{4,5},{5,4},{6,7},{7,6},{8,9},{9,8},{10,11... | collective-permute-start | bytes 393224 | tf_op jit(solution)/shard_map/ppermute | solution.py:713
  66.6 2.1 %collective-permute-start.7 = (bf16[128,512]{1,0:T(8,128)(2,1)S(1)}, bf16[128,512]{1,0:T(8,128)(2,1)S(1)}, u32[]{:S(2)}, u32[]{:S(2)}) collective-permute-start(bf16[128,512]{1,0:T(8,128)(2,1)S(1)} %get-tuple-element.76), channel_id=1, source_target_pairs={{0,31},{1,2},{2,1},{3,4},{4,3},{5,6},{6,5},{7,8},{8,7},{9,10},{10,... | collective-permute-start | bytes 393224 | tf_op jit(solution)/shard_map/ppermute | solution.py:714
  68.7 0.4 collective-permute-start.10
  69.1 2.8 %collective-permute-start.11 = (bf16[512,512]{1,0:T(8,128)(2,1)S(1)}, bf16[512,512]{1,0:T(8,128)(2,1)S(1)}, u32[]{:S(2)}, u32[]{:S(2)}) collective-permute-start(bf16[512,512]{1,0:T(8,128)(2,1)S(1)} %get-tuple-element.87), channel_id=1, source_target_pairs={{0,0},{96,96},{32,64},{64,32},{1,1},{97,97},{33,65},{65,33},{2,2},... | collective-permute-start | bytes 1572872 | tf_op jit(solution)/shard_map/ppermute | solution.py:715
  71.9 4.8 %project.3 = (bf16[1024,512]{1,0:T(8,128)(2,1)S(1)}, bf16[1024,512]{1,0:T(8,128)(2,1)S(1)}, bf16[512,1024]{1,0:T(8,128)(2,1)S(1)}, f32[512,1024]{1,0:T(8,128)S(1...) custom-call(bf16[1024,512]{1,0:T(8,128)(2,1)S(1)} %get-tuple-element.71.normed_ref, bf16[512,512]{1,0:T(8,128)(2,1)S(1)} %copy-done.2, ...), custom_call_target="tpu_custom_call" | custom-call | flops 1610612736 | bytes 5242880 | tf_op jit(solution)/shard_map/project/pallas_call | solution.py:321
  76.7 0.0 collective-permute-done.6.third_ref
  76.7 0.0 collective-permute-done.7.fourth_ref
  76.8 0.1 corners.3
  76.8 0.1 collective-permute-start.8
  76.9 2.5 %collective-permute-start.9 = (bf16[128,512]{1,0:T(8,128)(2,1)S(1)}, bf16[128,512]{1,0:T(8,128)(2,1)S(1)}, u32[]{:S(2)}, u32[]{:S(2)}) collective-permute-start(bf16[128,512]{1,0:T(8,128)(2,1)S(1)} %get-tuple-element.84), channel_id=1, source_target_pairs={{0,96},{32,64},{64,32},{96,0},{1,97},{33,65},{65,33},{97,1},{2,98}... | collective-permute-start | bytes 393224 | tf_op jit(solution)/shard_map/ppermute | solution.py:720
  79.4 1.6 %near.3 = (f32[512,1024]{1,0:T(8,128)S(1)}, f32[8,1024]{1,0:T(8,128)S(1)}, f32[8,1024]{1,0:T(8,128)S(1)}) custom-call(bf16[1024,512]{1,0:T(8,128)(2,1)S(1)} %get-tuple-element.72.query_ref, bf16[1024,512]{1,0:T(8,128)(2,1)S(1)} %get-tuple-element.73.key_ref, ...), custom_call_target="tpu_custom_call", output_to_operand_aliasing={{0}: (7, {}), {1}: (8, {}), {2}: (9, {})} | custom-call | flops 8589934592 | bytes 8388608 | tf_op jit(solution)/shard_map/near/pallas_call | solution.py:396
  81.0 0.0 collective-permute-done.10.first_ref
  81.0 0.1 collective-permute-done.11.second_ref
  81.1 4.3 %far.3 = (f32[1024,512]{1,0:T(8,128)S(1)}, bf16[2,512,512]{2,1,0:T(8,128)(2,1)S(1)}, bf16[2,512,512]{2,1,0:T(8,128)(2,1)S(1)}) custom-call(bf16[1024,512]{1,0:T(8,128)(2,1)S(1)} %get-tuple-element.72.query_ref, f32[512,1024]{1,0:T(8,128)S(1)} %get-tuple-element.80.mixed_ref, f32[8,1024]{1,0:T(8,128)S(1)} %get-tuple-element.81.highest_ref, ...), custom_call_target="tpu_custom_call" | custom-call | flops 8589934592 | bytes 8388608 | tf_op jit(solution)/shard_map/far/pallas_call | solution.py:544
  85.4 0.0 collective-permute-done.8.first_ref
  85.4 0.0 collective-permute-done.9.second_ref
  85.4 2.6 %edges.3 = bf16[16,64,512]{2,1,0:T(8,128)(2,1)} custom-call(bf16[1024,512]{1,0:T(8,128)(2,1)S(1)} %get-tuple-element.72.query_ref, f32[512,1024]{1,0:T(8,128)S(1)} %get-tuple-element.80.mixed_ref, f32[8,1024]{1,0:T(8,128)S(1)} %get-tuple-element.81.highest_ref, f32[8,1024]{1,0:T(8,128)S(1)} %get-tuple-element.82.total_ref, ...), custom_call_target="tpu_custom_call" | custom-call | tf_op jit(solution)/shard_map/edges/pallas_call | solution.py:674
  (11 shorter events, 0.0 us)
Async XLA Ops:
  0.0 15.2 %copy-start.4 = (f32[2,512]{1,0:T(2,128)S(1)}, f32[2,512]{1,0:T(2,128)}, u32[]{:S(2)}) copy-start(f32[2,512]{1,0:T(2,128)} %gain_ref.1) | copy-start | bytes 12292
  3.7 33.7 %all-to-all-start = ((bf16[128,40,128]{2,1,0:T(8,128)(2,1)}), bf16[128,40,128]{2,1,0:T(8,128)(2,1)S(1)}, u32[]{:S(2)}, u32[]{:S(2)}) async-start(bf16[128,40,128]{2,1,0:T(8,128)(2,1)} %dispatch.1), calls=%async_computation | async-start | bytes 2621440 | tf_op jit(solution)/shard_map/all_to_all | solution.py:696
  16.9 2.4 %copy-start.5 = (bf16[2,512,512]{2,1,0:T(8,128)(2,1)S(1)}, bf16[2,512,512]{2,1,0:T(8,128)(2,1)}, u32[]{:S(2)}) copy-start(bf16[2,512,512]{2,1,0:T(8,128)(2,1)} %param.19) | copy-start | bytes 3145732
  17.0 3.3 %copy-start.6 = (bf16[2,512,512]{2,1,0:T(8,128)(2,1)S(1)}, bf16[2,512,512]{2,1,0:T(8,128)(2,1)}, u32[]{:S(2)}) copy-start(bf16[2,512,512]{2,1,0:T(8,128)(2,1)} %param.21) | copy-start | bytes 3145732
  37.4 10.9 %copy-start = (bf16[512,512]{1,0:T(8,128)(2,1)S(1)}, bf16[512,512]{1,0:T(8,128)(2,1)}, u32[]{:S(2)}) copy-start(bf16[512,512]{1,0:T(8,128)(2,1)} %get-tuple-element.96.key_w) | copy-start | bytes 1572868
  37.4 10.9 %copy-start.3 = (bf16[512,512]{1,0:T(8,128)(2,1)S(1)}, bf16[512,512]{1,0:T(8,128)(2,1)}, u32[]{:S(2)}) copy-start(bf16[512,512]{1,0:T(8,128)(2,1)} %get-tuple-element.98.query_w) | copy-start | bytes 1572868
  42.4 10.8 %collective-permute-start = (bf16[128,512]{1,0:T(8,128)(2,1)S(1)}, bf16[128,512]{1,0:T(8,128)(2,1)S(1)}, u32[]{:S(2)}, u32[]{:S(2)}) collective-permute-start(bf16[128,512]{1,0:T(8,128)(2,1)S(1)} %get-tuple-element.52), channel_id=1, source_target_pairs={{0,1},{1,0},{2,3},{3,2},{4,5},{5,4},{6,7},{7,6},{8,9},{9,8},{10,11... | collective-permute-start | bytes 393224 | tf_op jit(solution)/shard_map/ppermute | solution.py:713
  42.5 10.7 %collective-permute-start.1 = (bf16[128,512]{1,0:T(8,128)(2,1)S(1)}, bf16[128,512]{1,0:T(8,128)(2,1)S(1)}, u32[]{:S(2)}, u32[]{:S(2)}) collective-permute-start(bf16[128,512]{1,0:T(8,128)(2,1)S(1)} %get-tuple-element.53), channel_id=1, source_target_pairs={{0,31},{1,2},{2,1},{3,4},{4,3},{5,6},{6,5},{7,8},{8,7},{9,10},{10,... | collective-permute-start | bytes 393224 | tf_op jit(solution)/shard_map/ppermute | solution.py:714
  44.2 13.4 %collective-permute-start.4 = (bf16[512,512]{1,0:T(8,128)(2,1)S(1)}, bf16[512,512]{1,0:T(8,128)(2,1)S(1)}, u32[]{:S(2)}, u32[]{:S(2)}) collective-permute-start(bf16[512,512]{1,0:T(8,128)(2,1)S(1)} %get-tuple-element.63), channel_id=1, source_target_pairs={{0,32},{32,0},{64,96},{96,64},{1,33},{33,1},{65,97},{97,65},{2,34}... | collective-permute-start | bytes 1572872 | tf_op jit(solution)/shard_map/ppermute | solution.py:716
  45.6 12.0 %collective-permute-start.5 = (bf16[512,512]{1,0:T(8,128)(2,1)S(1)}, bf16[512,512]{1,0:T(8,128)(2,1)S(1)}, u32[]{:S(2)}, u32[]{:S(2)}) collective-permute-start(bf16[512,512]{1,0:T(8,128)(2,1)S(1)} %get-tuple-element.64), channel_id=1, source_target_pairs={{0,0},{96,96},{32,64},{64,32},{1,1},{97,97},{33,65},{65,33},{2,2},... | collective-permute-start | bytes 1572872 | tf_op jit(solution)/shard_map/ppermute | solution.py:715
  53.3 8.9 %collective-permute-start.2 = (bf16[128,512]{1,0:T(8,128)(2,1)S(1)}, bf16[128,512]{1,0:T(8,128)(2,1)S(1)}, u32[]{:S(2)}, u32[]{:S(2)}) collective-permute-start(bf16[128,512]{1,0:T(8,128)(2,1)S(1)} %get-tuple-element.60), channel_id=1, source_target_pairs={{0,32},{32,0},{64,96},{96,64},{1,33},{33,1},{65,97},{97,65},{2,34}... | collective-permute-start | bytes 393224 | tf_op jit(solution)/shard_map/ppermute | solution.py:721
  53.4 8.9 %collective-permute-start.3 = (bf16[128,512]{1,0:T(8,128)(2,1)S(1)}, bf16[128,512]{1,0:T(8,128)(2,1)S(1)}, u32[]{:S(2)}, u32[]{:S(2)}) collective-permute-start(bf16[128,512]{1,0:T(8,128)(2,1)S(1)} %get-tuple-element.61), channel_id=1, source_target_pairs={{0,96},{32,64},{64,32},{96,0},{1,97},{33,65},{65,33},{97,1},{2,98}... | collective-permute-start | bytes 393224 | tf_op jit(solution)/shard_map/ppermute | solution.py:720
  56.1 1.6 %copy-start.1 = (bf16[512,512]{1,0:T(8,128)(2,1)S(1)}, bf16[512,512]{1,0:T(8,128)(2,1)}, u32[]{:S(2)}) copy-start(bf16[512,512]{1,0:T(8,128)(2,1)} %get-tuple-element.92.out_w) | copy-start | bytes 1572868
  62.2 9.6 %copy-start.2 = (bf16[512,512]{1,0:T(8,128)(2,1)S(1)}, bf16[512,512]{1,0:T(8,128)(2,1)}, u32[]{:S(2)}) copy-start(bf16[512,512]{1,0:T(8,128)(2,1)} %get-tuple-element.97.query_w) | copy-start | bytes 1572868
  64.0 12.7 %collective-permute-start.6 = (bf16[128,512]{1,0:T(8,128)(2,1)S(1)}, bf16[128,512]{1,0:T(8,128)(2,1)S(1)}, u32[]{:S(2)}, u32[]{:S(2)}) collective-permute-start(bf16[128,512]{1,0:T(8,128)(2,1)S(1)} %get-tuple-element.75), channel_id=1, source_target_pairs={{0,1},{1,0},{2,3},{3,2},{4,5},{5,4},{6,7},{7,6},{8,9},{9,8},{10,11... | collective-permute-start | bytes 393224 | tf_op jit(solution)/shard_map/ppermute | solution.py:713
  66.6 10.2 %collective-permute-start.7 = (bf16[128,512]{1,0:T(8,128)(2,1)S(1)}, bf16[128,512]{1,0:T(8,128)(2,1)S(1)}, u32[]{:S(2)}, u32[]{:S(2)}) collective-permute-start(bf16[128,512]{1,0:T(8,128)(2,1)S(1)} %get-tuple-element.76), channel_id=1, source_target_pairs={{0,31},{1,2},{2,1},{3,4},{4,3},{5,6},{6,5},{7,8},{8,7},{9,10},{10,... | collective-permute-start | bytes 393224 | tf_op jit(solution)/shard_map/ppermute | solution.py:714
  68.7 12.3 %collective-permute-start.10 = (bf16[512,512]{1,0:T(8,128)(2,1)S(1)}, bf16[512,512]{1,0:T(8,128)(2,1)S(1)}, u32[]{:S(2)}, u32[]{:S(2)}) collective-permute-start(bf16[512,512]{1,0:T(8,128)(2,1)S(1)} %get-tuple-element.86), channel_id=1, source_target_pairs={{0,32},{32,0},{64,96},{96,64},{1,33},{33,1},{65,97},{97,65},{2,34}... | collective-permute-start | bytes 1572872 | tf_op jit(solution)/shard_map/ppermute | solution.py:716
  69.1 12.0 %collective-permute-start.11 = (bf16[512,512]{1,0:T(8,128)(2,1)S(1)}, bf16[512,512]{1,0:T(8,128)(2,1)S(1)}, u32[]{:S(2)}, u32[]{:S(2)}) collective-permute-start(bf16[512,512]{1,0:T(8,128)(2,1)S(1)} %get-tuple-element.87), channel_id=1, source_target_pairs={{0,0},{96,96},{32,64},{64,32},{1,1},{97,97},{33,65},{65,33},{2,2},... | collective-permute-start | bytes 1572872 | tf_op jit(solution)/shard_map/ppermute | solution.py:715
  76.8 8.6 %collective-permute-start.8 = (bf16[128,512]{1,0:T(8,128)(2,1)S(1)}, bf16[128,512]{1,0:T(8,128)(2,1)S(1)}, u32[]{:S(2)}, u32[]{:S(2)}) collective-permute-start(bf16[128,512]{1,0:T(8,128)(2,1)S(1)} %get-tuple-element.83), channel_id=1, source_target_pairs={{0,32},{32,0},{64,96},{96,64},{1,33},{33,1},{65,97},{97,65},{2,34}... | collective-permute-start | bytes 393224 | tf_op jit(solution)/shard_map/ppermute | solution.py:721
  76.9 8.5 %collective-permute-start.9 = (bf16[128,512]{1,0:T(8,128)(2,1)S(1)}, bf16[128,512]{1,0:T(8,128)(2,1)S(1)}, u32[]{:S(2)}, u32[]{:S(2)}) collective-permute-start(bf16[128,512]{1,0:T(8,128)(2,1)S(1)} %get-tuple-element.84), channel_id=1, source_target_pairs={{0,96},{32,64},{64,32},{96,0},{1,97},{33,65},{65,33},{97,1},{2,98}... | collective-permute-start | bytes 393224 | tf_op jit(solution)/shard_map/ppermute | solution.py:720

commit v5 on v4

--- a/solution.py
+++ b/solution.py
@@ -251,7 +251,7 @@
     return expo.astype(BF16), highest, fold(expo, jnp.sum)
 
 
-LAGS = (0, 2, 3)
+LAGS = (0, 3, 4)
 
 
 def staged(units, stages):
@@ -561,7 +561,20 @@
         near_refs = (mixed_ref, highest_ref, total_ref)
         att_ref = rest[-1]
         if last:
-            inner_ref, out_ref, edge_ref = rest[:3]
+            inner_ref, out_ref, edge_ref, stage_ref, side_ref, sems = rest[:6]
+            for band in range(BANDS):
+                for r in range(8):
+                    pieces = []
+                    for sector in range(1, SECTORS - 1):
+                        at = (sector * BANDS + band) * BLOCK + r * 8
+                        pieces.append(inner_ref[at : at + 8, :])
+                    stage_ref[band * 8 + r] = jnp.concatenate(pieces, axis=0).astype(BF16)
+            copies = [
+                pltpu.make_async_copy(stage_ref, out_ref.at[:, pl.ds(8, 48), :], sems.at[0]),
+                pltpu.make_async_copy(side_ref.at[0], out_ref.at[:, pl.ds(0, 8), :], sems.at[1]),
+                pltpu.make_async_copy(side_ref.at[1], out_ref.at[:, pl.ds(56, 8), :], sems.at[2]),
+            ]
+            copies[0].start()
         else:
             new_ref = rest[4]
             refs = rest[5:10]
@@ -642,19 +655,14 @@
             normed = norm_rows(hidden, gain)
             store_normed(at // COLUMN, normed, refs)
         if last:
-            for band in range(BANDS):
-                for r in range(8):
-                    pieces = []
-                    for sector in range(SECTORS):
-                        at = (sector * BANDS + band) * BLOCK + r * 8
-                        if sector == 0:
-                            pieces.append(edge_ref[at : at + 8, :])
-                        elif sector == SECTORS - 1:
-                            at = at - CELLS + 2 * COLUMN
-                            pieces.append(edge_ref[at : at + 8, :])
-                        else:
-                            pieces.append(inner_ref[at : at + 8, :])
-                    out_ref[band * 8 + r] = jnp.concatenate(pieces, axis=0).astype(BF16)
+            for side in range(2):
+                for band in range(BANDS):
+                    for r in range(8):
+                        at = side * COLUMN + band * BLOCK + r * 8
+                        side_ref[side, band * 8 + r] = edge_ref[at : at + 8, :].astype(BF16)
+                copies[1 + side].start()
+            for copy in copies:
+                copy.wait()
 
     return edge_kernel
 
@@ -663,9 +671,14 @@
     new, key_f, value_f, *normed = inner
     scratch = [pltpu.VMEM((D, 2 * COLUMN), BF16)]
     if last:
-        scratch = [pltpu.VMEM((2 * COLUMN, D), F32)] + scratch
+        scratch = [
+            pltpu.VMEM((2 * COLUMN, D), F32),
+            pltpu.VMEM((16, 48, D), BF16),
+            pltpu.VMEM((2, 16, 8, D), BF16),
+            pltpu.SemaphoreType.DMA((3,)),
+        ] + scratch
         out_shape = jax.ShapeDtypeStruct((16, 64, D), BF16)
-        out_specs = VMEM
+        out_specs = HBM
         aliases = {}
     else:
         out_shape = (pltpu.VMEM((CELLS, D), F32),) + NORMED_SHAPES

time: 88.3 us -> 88.3 us (level)
  transfers between devices with their start and end apart: 13 -> 13, of which waited for: 2 -> 1; matrix products, arithmetic and copies ran while one was open for 7% -> 7% of each run, Pallas kernels for 25% -> 25%
where the time goes in v5:
time: 88.3 us; the launch traced here: 88.1 us
  Pallas kernels  34.9 us (40%)
  starting transfers between devices  30.4 us (34%)
  waiting for transfers between devices  16.4 us (19%)
  local copies, waits for them, and re-layouts  5.88 us (7%)
    all_to_all x1, waiting for transfers between devices, local(): lax.all_to_all(on_chip(send), ('lat', 'lon'), split_axis=0, concat_axis=0...  16.3 us
    all_to_all x1, starting transfers between devices, local(): lax.all_to_all(on_chip(send), ('lat', 'lon'), split_axis=0, concat_axis=0...  11.5 us
    pallas_call x2, Pallas kernels, project(): pl.pallas_call(project_kernel, out_shape=(shape, shape, pltpu.VMEM((D, CE...  9.83 us
    pallas_call x2, Pallas kernels, far(): pl.pallas_call(make_far_kernel(last), out_shape=out_shape, in_specs=[VMEM...  8.94 us
    ppermute x2, starting transfers between devices, local(): second = lax.ppermute(trades[1], 'lat', lat_second)  5.46 us
    ppermute x2, starting transfers between devices, local(): corner_second = lax.ppermute(on_chip(corner[1]), 'lat', lat_round)  5.17 us
    pallas_call x1, Pallas kernels, combine(): pl.pallas_call(combine_kernel, out_shape=(pltpu.VMEM((CELLS, D), F32),) +...  4.96 us
    pallas_call x2, Pallas kernels, edges(): pl.pallas_call(make_edge_kernel(last), out_shape=out_shape, in_specs=[VME...  4.2 us
  transfers between devices with their start and end apart: 13, of which 1 were waited for; matrix products, arithmetic and copies ran while one was open for 7% of the time, Pallas kernels for 25%

profile of v5, /device:TPU:1, one launch (start us, length us, event | category | flops | bytes accessed | tf_op | source)
XLA Modules:
  0.0 88.1 jit_solution(10073666189313322804)
XLA Ops:
  0.0 3.7 %dispatch.1 = bf16[128,40,128]{2,1,0:T(8,128)(2,1)} custom-call(s32[1,1024]{1,0:T(1,128)} %bitcast.29, s32[1,1024]{1,0:T(1,128)} %bitcast.30, s32[1,1024]{1,0:T(1,128)} %bitcast.31, bf16[1024,256]{1,0:T(8,128)(2,1)} %feat_hbm.1), custom_call_target="tpu_custom_call" | custom-call | tf_op jit(solution)/shard_map/dispatch/pallas_call | solution.py:92
  3.7 11.5 %all-to-all-start = ((bf16[128,40,128]{2,1,0:T(8,128)(2,1)}), bf16[128,40,128]{2,1,0:T(8,128)(2,1)S(1)}, u32[]{:S(2)}, u32[]{:S(2)}) async-start(bf16[128,40,128]{2,1,0:T(8,128)(2,1)} %dispatch.1), calls=%async_computation | async-start | bytes 2621440 | tf_op jit(solution)/shard_map/all_to_all | solution.py:709
  15.2 1.3 %fusion = (bf16[1,512,512]{2,1,0:T(8,128)(2,1)S(1)}, bf16[1,512,512]{2,1,0:T(8,128)(2,1)S(1)}) fusion(bf16[2,512,512]{2,1,0:T(8,128)(2,1)} %param.20), kind=kLoop, calls=%fused_computation.6 | loop fusion | bytes 2097152 | tf_op jit(solution)/shard_map/slice | solution.py:723
  16.5 0.2 copy.25
  16.7 0.2 copy.24
  16.9 0.0 copy-start.5
  17.0 0.0 copy-start.6
  17.0 2.4 %slice_bitcast_fusion.2 = (bf16[512,512]{1,0:T(8,128)(2,1)}, bf16[512,512]{1,0:T(8,128)(2,1)}) fusion(bf16[2,512,512]{2,1,0:T(8,128)(2,1)} %param.18), kind=kLoop, calls=%fused_computation.2 | loop fusion | bytes 2097152 | tf_op jit(solution)/shard_map/squeeze | solution.py:730
  19.4 0.9 slice_bitcast_fusion.1
  20.2 0.0 copy-done.6
  20.2 0.9 slice_bitcast_fusion
  21.1 16.3 %all-to-all-done.got_ref = bf16[128,40,128]{2,1,0:T(8,128)(2,1)S(1)} async-done(((bf16[128,40,128]{2,1,0:T(8,128)(2,1)}), bf16[128,40,128]{2,1,0:T(8,128)(2,1)S(1)}, u32[]{:S(2)}, u32[]{:S(2)}) %all-to-all-start) | async-done | bytes 1310752 | tf_op jit(solution)/shard_map/all_to_all | solution.py:709
  37.4 5.0 %combine.1 = (f32[1024,512]{1,0:T(8,128)S(1)}, bf16[1024,512]{1,0:T(8,128)(2,1)S(1)}, bf16[512,512]{1,0:T(8,128)(2,1)S(1)}, bf16[512,512]{1,0:T(8,128)(2,1)S(1)}...) custom-call(bf16[128,40,128]{2,1,0:T(8,128)(2,1)S(1)} %all-to-all-done.got_ref, bf16[256,512]{1,0:T(8,128)(2,1)} %embed_hbm.1, ...), custom_call_target="tpu_custom_call" | custom-call | tf_op jit(solution)/shard_map/combine/pallas_call | solution.py:217
  42.4 0.1 collective-permute-start
  42.5 1.8 %collective-permute-start.1 = (bf16[128,512]{1,0:T(8,128)(2,1)S(1)}, bf16[128,512]{1,0:T(8,128)(2,1)S(1)}, u32[]{:S(2)}, u32[]{:S(2)}) collective-permute-start(bf16[128,512]{1,0:T(8,128)(2,1)S(1)} %get-tuple-element.53), channel_id=1, source_target_pairs={{0,31},{1,2},{2,1},{3,4},{4,3},{5,6},{6,5},{7,8},{8,7},{9,10},{10,... | collective-permute-start | bytes 393224 | tf_op jit(solution)/shard_map/ppermute | solution.py:727
  44.2 1.4 %collective-permute-start.4 = (bf16[512,512]{1,0:T(8,128)(2,1)S(1)}, bf16[512,512]{1,0:T(8,128)(2,1)S(1)}, u32[]{:S(2)}, u32[]{:S(2)}) collective-permute-start(bf16[512,512]{1,0:T(8,128)(2,1)S(1)} %get-tuple-element.63), channel_id=1, source_target_pairs={{0,32},{32,0},{64,96},{96,64},{1,33},{33,1},{65,97},{97,65},{2,34}... | collective-permute-start | bytes 1572872 | tf_op jit(solution)/shard_map/ppermute | solution.py:729
  45.6 2.7 %collective-permute-start.5 = (bf16[512,512]{1,0:T(8,128)(2,1)S(1)}, bf16[512,512]{1,0:T(8,128)(2,1)S(1)}, u32[]{:S(2)}, u32[]{:S(2)}) collective-permute-start(bf16[512,512]{1,0:T(8,128)(2,1)S(1)} %get-tuple-element.64), channel_id=1, source_target_pairs={{0,0},{96,96},{32,64},{64,32},{1,1},{97,97},{33,65},{65,33},{2,2},... | collective-permute-start | bytes 1572872 | tf_op jit(solution)/shard_map/ppermute | solution.py:728
  48.4 4.9 %project.2 = (bf16[1024,512]{1,0:T(8,128)(2,1)S(1)}, bf16[1024,512]{1,0:T(8,128)(2,1)S(1)}, bf16[512,1024]{1,0:T(8,128)(2,1)S(1)}, f32[512,1024]{1,0:T(8,128)S(1...) custom-call(bf16[1024,512]{1,0:T(8,128)(2,1)S(1)} %get-tuple-element.48.normed_ref, bf16[512,512]{1,0:T(8,128)(2,1)S(1)} %copy-done.3, ...), custom_call_target="tpu_custom_call" | custom-call | flops 1610612736 | bytes 5242880 | tf_op jit(solution)/shard_map/project/pallas_call | solution.py:321
  53.3 0.0 collective-permute-done.third_ref
  53.3 0.0 collective-permute-done.1.fourth_ref
  53.3 0.1 corners.2
  53.4 0.1 collective-permute-start.2
  53.5 2.7 %collective-permute-start.3 = (bf16[128,512]{1,0:T(8,128)(2,1)S(1)}, bf16[128,512]{1,0:T(8,128)(2,1)S(1)}, u32[]{:S(2)}, u32[]{:S(2)}) collective-permute-start(bf16[128,512]{1,0:T(8,128)(2,1)S(1)} %get-tuple-element.61), channel_id=1, source_target_pairs={{0,96},{32,64},{64,32},{96,0},{1,97},{33,65},{65,33},{97,1},{2,98}... | collective-permute-start | bytes 393224 | tf_op jit(solution)/shard_map/ppermute | solution.py:733
  56.2 1.6 %near.2 = (f32[512,1024]{1,0:T(8,128)S(1)}, f32[8,1024]{1,0:T(8,128)S(1)}, f32[8,1024]{1,0:T(8,128)S(1)}) custom-call(bf16[1024,512]{1,0:T(8,128)(2,1)S(1)} %get-tuple-element.49.query_ref, bf16[1024,512]{1,0:T(8,128)(2,1)S(1)} %get-tuple-element.50.key_ref, ...), custom_call_target="tpu_custom_call", output_to_operand_aliasing={{0}: (7, {}), {1}: (8, {}), {2}: (9, {})} | custom-call | flops 8589934592 | bytes 8388608 | tf_op jit(solution)/shard_map/near/pallas_call | solution.py:396
  57.8 0.0 collective-permute-done.4.first_ref
  57.8 0.0 collective-permute-done.5.second_ref
  57.8 4.6 %far.2 = (f32[1024,512]{1,0:T(8,128)S(1)}, bf16[2,512,512]{2,1,0:T(8,128)(2,1)S(1)}, bf16[2,512,512]{2,1,0:T(8,128)(2,1)S(1)}, bf16[1024,512]{1,0:T(8,128)(2,1)S...) custom-call(bf16[1024,512]{1,0:T(8,128)(2,1)S(1)} %get-tuple-element.49.query_ref, ...), custom_call_target="tpu_custom_call" | custom-call | flops 8589934592 | bytes 8388608 | tf_op jit(solution)/shard_map/far/pallas_call | solution.py:544
  62.4 0.0 collective-permute-done.2.first_ref
  62.4 0.0 collective-permute-done.3.second_ref
  62.4 0.0 copy-start.2
  62.4 1.7 %edges.2 = (f32[1024,512]{1,0:T(8,128)S(1)}, bf16[1024,512]{1,0:T(8,128)(2,1)S(1)}, bf16[512,512]{1,0:T(8,128)(2,1)S(1)}, bf16[512,512]{1,0:T(8,128)(2,1)S(1)}, ...) custom-call(bf16[1024,512]{1,0:T(8,128)(2,1)S(1)} %get-tuple-element, ...), custom_call_target="tpu_custom_call", output_to_operand_aliasing={{0}: (13, {}), {1}: (14, {}), {2}: (15, {}), {3}: (16, {})} | custom-call | tf_op jit(solution)/shard_map/edges/pallas_call | solution.py:687
  64.1 2.4 %collective-permute-start.6 = (bf16[128,512]{1,0:T(8,128)(2,1)S(1)}, bf16[128,512]{1,0:T(8,128)(2,1)S(1)}, u32[]{:S(2)}, u32[]{:S(2)}) collective-permute-start(bf16[128,512]{1,0:T(8,128)(2,1)S(1)} %get-tuple-element.75), channel_id=1, source_target_pairs={{0,1},{1,0},{2,3},{3,2},{4,5},{5,4},{6,7},{7,6},{8,9},{9,8},{10,11... | collective-permute-start | bytes 393224 | tf_op jit(solution)/shard_map/ppermute | solution.py:726
  66.5 1.8 %collective-permute-start.7 = (bf16[128,512]{1,0:T(8,128)(2,1)S(1)}, bf16[128,512]{1,0:T(8,128)(2,1)S(1)}, u32[]{:S(2)}, u32[]{:S(2)}) collective-permute-start(bf16[128,512]{1,0:T(8,128)(2,1)S(1)} %get-tuple-element.76), channel_id=1, source_target_pairs={{0,31},{1,2},{2,1},{3,4},{4,3},{5,6},{6,5},{7,8},{8,7},{9,10},{10,... | collective-permute-start | bytes 393224 | tf_op jit(solution)/shard_map/ppermute | solution.py:727
  68.3 0.7 collective-permute-start.10
  69.0 2.8 %collective-permute-start.11 = (bf16[512,512]{1,0:T(8,128)(2,1)S(1)}, bf16[512,512]{1,0:T(8,128)(2,1)S(1)}, u32[]{:S(2)}, u32[]{:S(2)}) collective-permute-start(bf16[512,512]{1,0:T(8,128)(2,1)S(1)} %get-tuple-element.87), channel_id=1, source_target_pairs={{0,0},{96,96},{32,64},{64,32},{1,1},{97,97},{33,65},{65,33},{2,2},... | collective-permute-start | bytes 1572872 | tf_op jit(solution)/shard_map/ppermute | solution.py:728
  71.8 4.9 %project.3 = (bf16[1024,512]{1,0:T(8,128)(2,1)S(1)}, bf16[1024,512]{1,0:T(8,128)(2,1)S(1)}, bf16[512,1024]{1,0:T(8,128)(2,1)S(1)}, f32[512,1024]{1,0:T(8,128)S(1...) custom-call(bf16[1024,512]{1,0:T(8,128)(2,1)S(1)} %get-tuple-element.71.normed_ref, bf16[512,512]{1,0:T(8,128)(2,1)S(1)} %copy-done.2, ...), custom_call_target="tpu_custom_call" | custom-call | flops 1610612736 | bytes 5242880 | tf_op jit(solution)/shard_map/project/pallas_call | solution.py:321
  76.7 0.0 collective-permute-done.6.third_ref
  76.7 0.0 collective-permute-done.7.fourth_ref
  76.8 0.1 corners.3
  76.8 0.1 collective-permute-start.8
  76.9 2.5 %collective-permute-start.9 = (bf16[128,512]{1,0:T(8,128)(2,1)S(1)}, bf16[128,512]{1,0:T(8,128)(2,1)S(1)}, u32[]{:S(2)}, u32[]{:S(2)}) collective-permute-start(bf16[128,512]{1,0:T(8,128)(2,1)S(1)} %get-tuple-element.84), channel_id=1, source_target_pairs={{0,96},{32,64},{64,32},{96,0},{1,97},{33,65},{65,33},{97,1},{2,98}... | collective-permute-start | bytes 393224 | tf_op jit(solution)/shard_map/ppermute | solution.py:733
  79.4 1.6 %near.3 = (f32[512,1024]{1,0:T(8,128)S(1)}, f32[8,1024]{1,0:T(8,128)S(1)}, f32[8,1024]{1,0:T(8,128)S(1)}) custom-call(bf16[1024,512]{1,0:T(8,128)(2,1)S(1)} %get-tuple-element.72.query_ref, bf16[1024,512]{1,0:T(8,128)(2,1)S(1)} %get-tuple-element.73.key_ref, ...), custom_call_target="tpu_custom_call", output_to_operand_aliasing={{0}: (7, {}), {1}: (8, {}), {2}: (9, {})} | custom-call | flops 8589934592 | bytes 8388608 | tf_op jit(solution)/shard_map/near/pallas_call | solution.py:396
  81.0 0.0 collective-permute-done.10.first_ref
  81.0 0.0 collective-permute-done.11.second_ref
  81.0 4.3 %far.3 = (f32[1024,512]{1,0:T(8,128)S(1)}, bf16[2,512,512]{2,1,0:T(8,128)(2,1)S(1)}, bf16[2,512,512]{2,1,0:T(8,128)(2,1)S(1)}) custom-call(bf16[1024,512]{1,0:T(8,128)(2,1)S(1)} %get-tuple-element.72.query_ref, f32[512,1024]{1,0:T(8,128)S(1)} %get-tuple-element.80.mixed_ref, f32[8,1024]{1,0:T(8,128)S(1)} %get-tuple-element.81.highest_ref, ...), custom_call_target="tpu_custom_call" | custom-call | flops 8589934592 | bytes 8388608 | tf_op jit(solution)/shard_map/far/pallas_call | solution.py:544
  85.4 0.0 collective-permute-done.8.first_ref
  85.4 0.0 collective-permute-done.9.second_ref
  85.4 2.5 %edges.3 = bf16[16,64,512]{2,1,0:T(8,128)(2,1)} custom-call(bf16[1024,512]{1,0:T(8,128)(2,1)S(1)} %get-tuple-element.72.query_ref, f32[512,1024]{1,0:T(8,128)S(1)} %get-tuple-element.80.mixed_ref, f32[8,1024]{1,0:T(8,128)S(1)} %get-tuple-element.81.highest_ref, f32[8,1024]{1,0:T(8,128)S(1)} %get-tuple-element.82.total_ref, ...), custom_call_target="tpu_custom_call" | custom-call | tf_op jit(solution)/shard_map/edges/pallas_call | solution.py:687
  (11 shorter events, 0.0 us)
Async XLA Ops:
  0.0 15.2 %copy-start.4 = (f32[2,512]{1,0:T(2,128)S(1)}, f32[2,512]{1,0:T(2,128)}, u32[]{:S(2)}) copy-start(f32[2,512]{1,0:T(2,128)} %gain_ref.1) | copy-start | bytes 12292
  3.7 33.7 %all-to-all-start = ((bf16[128,40,128]{2,1,0:T(8,128)(2,1)}), bf16[128,40,128]{2,1,0:T(8,128)(2,1)S(1)}, u32[]{:S(2)}, u32[]{:S(2)}) async-start(bf16[128,40,128]{2,1,0:T(8,128)(2,1)} %dispatch.1), calls=%async_computation | async-start | bytes 2621440 | tf_op jit(solution)/shard_map/all_to_all | solution.py:709
  16.9 2.4 %copy-start.5 = (bf16[2,512,512]{2,1,0:T(8,128)(2,1)S(1)}, bf16[2,512,512]{2,1,0:T(8,128)(2,1)}, u32[]{:S(2)}) copy-start(bf16[2,512,512]{2,1,0:T(8,128)(2,1)} %param.19) | copy-start | bytes 3145732
  17.0 3.3 %copy-start.6 = (bf16[2,512,512]{2,1,0:T(8,128)(2,1)S(1)}, bf16[2,512,512]{2,1,0:T(8,128)(2,1)}, u32[]{:S(2)}) copy-start(bf16[2,512,512]{2,1,0:T(8,128)(2,1)} %param.21) | copy-start | bytes 3145732
  37.4 10.9 %copy-start = (bf16[512,512]{1,0:T(8,128)(2,1)S(1)}, bf16[512,512]{1,0:T(8,128)(2,1)}, u32[]{:S(2)}) copy-start(bf16[512,512]{1,0:T(8,128)(2,1)} %get-tuple-element.96.key_w) | copy-start | bytes 1572868
  37.4 10.9 %copy-start.3 = (bf16[512,512]{1,0:T(8,128)(2,1)S(1)}, bf16[512,512]{1,0:T(8,128)(2,1)}, u32[]{:S(2)}) copy-start(bf16[512,512]{1,0:T(8,128)(2,1)} %get-tuple-element.98.query_w) | copy-start | bytes 1572868
  42.4 10.9 %collective-permute-start = (bf16[128,512]{1,0:T(8,128)(2,1)S(1)}, bf16[128,512]{1,0:T(8,128)(2,1)S(1)}, u32[]{:S(2)}, u32[]{:S(2)}) collective-permute-start(bf16[128,512]{1,0:T(8,128)(2,1)S(1)} %get-tuple-element.52), channel_id=1, source_target_pairs={{0,1},{1,0},{2,3},{3,2},{4,5},{5,4},{6,7},{7,6},{8,9},{9,8},{10,11... | collective-permute-start | bytes 393224 | tf_op jit(solution)/shard_map/ppermute | solution.py:726
  42.5 10.8 %collective-permute-start.1 = (bf16[128,512]{1,0:T(8,128)(2,1)S(1)}, bf16[128,512]{1,0:T(8,128)(2,1)S(1)}, u32[]{:S(2)}, u32[]{:S(2)}) collective-permute-start(bf16[128,512]{1,0:T(8,128)(2,1)S(1)} %get-tuple-element.53), channel_id=1, source_target_pairs={{0,31},{1,2},{2,1},{3,4},{4,3},{5,6},{6,5},{7,8},{8,7},{9,10},{10,... | collective-permute-start | bytes 393224 | tf_op jit(solution)/shard_map/ppermute | solution.py:727
  44.2 13.5 %collective-permute-start.4 = (bf16[512,512]{1,0:T(8,128)(2,1)S(1)}, bf16[512,512]{1,0:T(8,128)(2,1)S(1)}, u32[]{:S(2)}, u32[]{:S(2)}) collective-permute-start(bf16[512,512]{1,0:T(8,128)(2,1)S(1)} %get-tuple-element.63), channel_id=1, source_target_pairs={{0,32},{32,0},{64,96},{96,64},{1,33},{33,1},{65,97},{97,65},{2,34}... | collective-permute-start | bytes 1572872 | tf_op jit(solution)/shard_map/ppermute | solution.py:729
  45.6 12.1 %collective-permute-start.5 = (bf16[512,512]{1,0:T(8,128)(2,1)S(1)}, bf16[512,512]{1,0:T(8,128)(2,1)S(1)}, u32[]{:S(2)}, u32[]{:S(2)}) collective-permute-start(bf16[512,512]{1,0:T(8,128)(2,1)S(1)} %get-tuple-element.64), channel_id=1, source_target_pairs={{0,0},{96,96},{32,64},{64,32},{1,1},{97,97},{33,65},{65,33},{2,2},... | collective-permute-start | bytes 1572872 | tf_op jit(solution)/shard_map/ppermute | solution.py:728
  53.4 9.0 %collective-permute-start.2 = (bf16[128,512]{1,0:T(8,128)(2,1)S(1)}, bf16[128,512]{1,0:T(8,128)(2,1)S(1)}, u32[]{:S(2)}, u32[]{:S(2)}) collective-permute-start(bf16[128,512]{1,0:T(8,128)(2,1)S(1)} %get-tuple-element.60), channel_id=1, source_target_pairs={{0,32},{32,0},{64,96},{96,64},{1,33},{33,1},{65,97},{97,65},{2,34}... | collective-permute-start | bytes 393224 | tf_op jit(solution)/shard_map/ppermute | solution.py:734
  53.5 9.0 %collective-permute-start.3 = (bf16[128,512]{1,0:T(8,128)(2,1)S(1)}, bf16[128,512]{1,0:T(8,128)(2,1)S(1)}, u32[]{:S(2)}, u32[]{:S(2)}) collective-permute-start(bf16[128,512]{1,0:T(8,128)(2,1)S(1)} %get-tuple-element.61), channel_id=1, source_target_pairs={{0,96},{32,64},{64,32},{96,0},{1,97},{33,65},{65,33},{97,1},{2,98}... | collective-permute-start | bytes 393224 | tf_op jit(solution)/shard_map/ppermute | solution.py:733
  56.2 1.6 %copy-start.1 = (bf16[512,512]{1,0:T(8,128)(2,1)S(1)}, bf16[512,512]{1,0:T(8,128)(2,1)}, u32[]{:S(2)}) copy-start(bf16[512,512]{1,0:T(8,128)(2,1)} %get-tuple-element.92.out_w) | copy-start | bytes 1572868
  62.4 9.4 %copy-start.2 = (bf16[512,512]{1,0:T(8,128)(2,1)S(1)}, bf16[512,512]{1,0:T(8,128)(2,1)}, u32[]{:S(2)}) copy-start(bf16[512,512]{1,0:T(8,128)(2,1)} %get-tuple-element.97.query_w) | copy-start | bytes 1572868
  64.1 12.6 %collective-permute-start.6 = (bf16[128,512]{1,0:T(8,128)(2,1)S(1)}, bf16[128,512]{1,0:T(8,128)(2,1)S(1)}, u32[]{:S(2)}, u32[]{:S(2)}) collective-permute-start(bf16[128,512]{1,0:T(8,128)(2,1)S(1)} %get-tuple-element.75), channel_id=1, source_target_pairs={{0,1},{1,0},{2,3},{3,2},{4,5},{5,4},{6,7},{7,6},{8,9},{9,8},{10,11... | collective-permute-start | bytes 393224 | tf_op jit(solution)/shard_map/ppermute | solution.py:726
  66.5 10.2 %collective-permute-start.7 = (bf16[128,512]{1,0:T(8,128)(2,1)S(1)}, bf16[128,512]{1,0:T(8,128)(2,1)S(1)}, u32[]{:S(2)}, u32[]{:S(2)}) collective-permute-start(bf16[128,512]{1,0:T(8,128)(2,1)S(1)} %get-tuple-element.76), channel_id=1, source_target_pairs={{0,31},{1,2},{2,1},{3,4},{4,3},{5,6},{6,5},{7,8},{8,7},{9,10},{10,... | collective-permute-start | bytes 393224 | tf_op jit(solution)/shard_map/ppermute | solution.py:727
  68.3 12.7 %collective-permute-start.10 = (bf16[512,512]{1,0:T(8,128)(2,1)S(1)}, bf16[512,512]{1,0:T(8,128)(2,1)S(1)}, u32[]{:S(2)}, u32[]{:S(2)}) collective-permute-start(bf16[512,512]{1,0:T(8,128)(2,1)S(1)} %get-tuple-element.86), channel_id=1, source_target_pairs={{0,32},{32,0},{64,96},{96,64},{1,33},{33,1},{65,97},{97,65},{2,34}... | collective-permute-start | bytes 1572872 | tf_op jit(solution)/shard_map/ppermute | solution.py:729
  69.0 12.0 %collective-permute-start.11 = (bf16[512,512]{1,0:T(8,128)(2,1)S(1)}, bf16[512,512]{1,0:T(8,128)(2,1)S(1)}, u32[]{:S(2)}, u32[]{:S(2)}) collective-permute-start(bf16[512,512]{1,0:T(8,128)(2,1)S(1)} %get-tuple-element.87), channel_id=1, source_target_pairs={{0,0},{96,96},{32,64},{64,32},{1,1},{97,97},{33,65},{65,33},{2,2},... | collective-permute-start | bytes 1572872 | tf_op jit(solution)/shard_map/ppermute | solution.py:728
  76.8 8.5 %collective-permute-start.8 = (bf16[128,512]{1,0:T(8,128)(2,1)S(1)}, bf16[128,512]{1,0:T(8,128)(2,1)S(1)}, u32[]{:S(2)}, u32[]{:S(2)}) collective-permute-start(bf16[128,512]{1,0:T(8,128)(2,1)S(1)} %get-tuple-element.83), channel_id=1, source_target_pairs={{0,32},{32,0},{64,96},{96,64},{1,33},{33,1},{65,97},{97,65},{2,34}... | collective-permute-start | bytes 393224 | tf_op jit(solution)/shard_map/ppermute | solution.py:734
  76.9 8.5 %collective-permute-start.9 = (bf16[128,512]{1,0:T(8,128)(2,1)S(1)}, bf16[128,512]{1,0:T(8,128)(2,1)S(1)}, u32[]{:S(2)}, u32[]{:S(2)}) collective-permute-start(bf16[128,512]{1,0:T(8,128)(2,1)S(1)} %get-tuple-element.84), channel_id=1, source_target_pairs={{0,96},{32,64},{64,32},{96,0},{1,97},{33,65},{65,33},{97,1},{2,98}... | collective-permute-start | bytes 393224 | tf_op jit(solution)/shard_map/ppermute | solution.py:733

commit v6 on v5

--- a/solution.py
+++ b/solution.py
@@ -78,7 +78,7 @@
     target = owner * CAP + rank
     copies[3].wait()
     feat = feat_ref[...]
-    step = 256
+    step = 1024
     for at in range(0, SLOTS, step):
         pick = (iota((step, OBS), 0) + at == target).astype(F32).astype(BF16)
         rows = jnp.dot(pick, feat, preferred_element_type=F32).astype(BF16)
@@ -190,7 +190,7 @@
         emb_ref[at : at + step, :] = gelu(product).astype(BF16)
     gain = gain_ref[0:1, :]
     fetch_grid.wait()
-    chunk = 512
+    chunk = 1024
     for start in range(0, CELLS, chunk):
         total = jnp.dot(hot_ref[start : start + chunk, :], emb_ref[...], preferred_element_type=F32)
         for sub in range(chunk // COLUMN):

time: 88.3 us -> 88.7 us (level)
  no operation moved by 1% of the time
where the time goes in v6:
time: 88.7 us; the launch traced here: 88.4 us
  Pallas kernels  35.1 us (40%)
  starting transfers between devices  30.6 us (34%)
  waiting for transfers between devices  16.3 us (18%)
  local copies, waits for them, and re-layouts  5.88 us (7%)
    all_to_all x1, waiting for transfers between devices, local(): lax.all_to_all(on_chip(send), ('lat', 'lon'), split_axis=0, concat_axis=0...  16.3 us
    all_to_all x1, starting transfers between devices, local(): lax.all_to_all(on_chip(send), ('lat', 'lon'), split_axis=0, concat_axis=0...  11.5 us
    pallas_call x2, Pallas kernels, project(): pl.pallas_call(project_kernel, out_shape=(shape, shape, pltpu.VMEM((D, CE...  9.84 us
    pallas_call x2, Pallas kernels, far(): pl.pallas_call(make_far_kernel(last), out_shape=out_shape, in_specs=[VMEM...  8.95 us
    ppermute x2, starting transfers between devices, local(): second = lax.ppermute(trades[1], 'lat', lat_second)  5.27 us
    ppermute x2, starting transfers between devices, local(): corner_second = lax.ppermute(on_chip(corner[1]), 'lat', lat_round)  5.17 us
    pallas_call x1, Pallas kernels, combine(): pl.pallas_call(combine_kernel, out_shape=(pltpu.VMEM((CELLS, D), F32),) +...  5.13 us
    pallas_call x2, Pallas kernels, edges(): pl.pallas_call(make_edge_kernel(last), out_shape=out_shape, in_specs=[VME...  4.21 us
  transfers between devices with their start and end apart: 13, of which 1 were waited for; matrix products, arithmetic and copies ran while one was open for 7% of the time, Pallas kernels for 25%

profile of v6, /device:TPU:1, one launch (start us, length us, event | category | flops | bytes accessed | tf_op | source)
XLA Modules:
  0.0 88.4 jit_solution(10722419018007827230)
XLA Ops:
  0.0 3.7 %dispatch.1 = bf16[128,40,128]{2,1,0:T(8,128)(2,1)} custom-call(s32[1,1024]{1,0:T(1,128)} %bitcast.29, s32[1,1024]{1,0:T(1,128)} %bitcast.30, s32[1,1024]{1,0:T(1,128)} %bitcast.31, bf16[1024,256]{1,0:T(8,128)(2,1)} %feat_hbm.1), custom_call_target="tpu_custom_call" | custom-call | tf_op jit(solution)/shard_map/dispatch/pallas_call | solution.py:92
  3.7 11.5 %all-to-all-start = ((bf16[128,40,128]{2,1,0:T(8,128)(2,1)}), bf16[128,40,128]{2,1,0:T(8,128)(2,1)S(1)}, u32[]{:S(2)}, u32[]{:S(2)}) async-start(bf16[128,40,128]{2,1,0:T(8,128)(2,1)} %dispatch.1), calls=%async_computation | async-start | bytes 2621440 | tf_op jit(solution)/shard_map/all_to_all | solution.py:709
  15.2 0.0 copy-done.4
  15.2 1.3 %fusion = (bf16[1,512,512]{2,1,0:T(8,128)(2,1)S(1)}, bf16[1,512,512]{2,1,0:T(8,128)(2,1)S(1)}) fusion(bf16[2,512,512]{2,1,0:T(8,128)(2,1)} %param.20), kind=kLoop, calls=%fused_computation.6 | loop fusion | bytes 2097152 | tf_op jit(solution)/shard_map/slice | solution.py:723
  16.5 0.2 copy.25
  16.7 0.2 copy.24
  16.9 0.0 copy-start.5
  16.9 0.0 copy-start.6
  17.0 2.4 %slice_bitcast_fusion.2 = (bf16[512,512]{1,0:T(8,128)(2,1)}, bf16[512,512]{1,0:T(8,128)(2,1)}) fusion(bf16[2,512,512]{2,1,0:T(8,128)(2,1)} %param.18), kind=kLoop, calls=%fused_computation.2 | loop fusion | bytes 2097152 | tf_op jit(solution)/shard_map/squeeze | solution.py:730
  19.4 0.9 slice_bitcast_fusion.1
  20.2 0.9 slice_bitcast_fusion
  21.1 16.3 %all-to-all-done.got_ref = bf16[128,40,128]{2,1,0:T(8,128)(2,1)S(1)} async-done(((bf16[128,40,128]{2,1,0:T(8,128)(2,1)}), bf16[128,40,128]{2,1,0:T(8,128)(2,1)S(1)}, u32[]{:S(2)}, u32[]{:S(2)}) %all-to-all-start) | async-done | bytes 1310752 | tf_op jit(solution)/shard_map/all_to_all | solution.py:709
  37.4 5.1 %combine.1 = (f32[1024,512]{1,0:T(8,128)S(1)}, bf16[1024,512]{1,0:T(8,128)(2,1)S(1)}, bf16[512,512]{1,0:T(8,128)(2,1)S(1)}, bf16[512,512]{1,0:T(8,128)(2,1)S(1)}...) custom-call(bf16[128,40,128]{2,1,0:T(8,128)(2,1)S(1)} %all-to-all-done.got_ref, bf16[256,512]{1,0:T(8,128)(2,1)} %embed_hbm.1, ...), custom_call_target="tpu_custom_call" | custom-call | tf_op jit(solution)/shard_map/combine/pallas_call | solution.py:217
  42.5 0.1 collective-permute-start
  42.6 1.7 %collective-permute-start.1 = (bf16[128,512]{1,0:T(8,128)(2,1)S(1)}, bf16[128,512]{1,0:T(8,128)(2,1)S(1)}, u32[]{:S(2)}, u32[]{:S(2)}) collective-permute-start(bf16[128,512]{1,0:T(8,128)(2,1)S(1)} %get-tuple-element.53), channel_id=1, source_target_pairs={{0,31},{1,2},{2,1},{3,4},{4,3},{5,6},{6,5},{7,8},{8,7},{9,10},{10,... | collective-permute-start | bytes 393224 | tf_op jit(solution)/shard_map/ppermute | solution.py:727
  44.4 1.4 %collective-permute-start.4 = (bf16[512,512]{1,0:T(8,128)(2,1)S(1)}, bf16[512,512]{1,0:T(8,128)(2,1)S(1)}, u32[]{:S(2)}, u32[]{:S(2)}) collective-permute-start(bf16[512,512]{1,0:T(8,128)(2,1)S(1)} %get-tuple-element.63), channel_id=1, source_target_pairs={{0,32},{32,0},{64,96},{96,64},{1,33},{33,1},{65,97},{97,65},{2,34}... | collective-permute-start | bytes 1572872 | tf_op jit(solution)/shard_map/ppermute | solution.py:729
  45.8 2.5 %collective-permute-start.5 = (bf16[512,512]{1,0:T(8,128)(2,1)S(1)}, bf16[512,512]{1,0:T(8,128)(2,1)S(1)}, u32[]{:S(2)}, u32[]{:S(2)}) collective-permute-start(bf16[512,512]{1,0:T(8,128)(2,1)S(1)} %get-tuple-element.64), channel_id=1, source_target_pairs={{0,0},{96,96},{32,64},{64,32},{1,1},{97,97},{33,65},{65,33},{2,2},... | collective-permute-start | bytes 1572872 | tf_op jit(solution)/shard_map/ppermute | solution.py:728
  48.3 4.9 %project.2 = (bf16[1024,512]{1,0:T(8,128)(2,1)S(1)}, bf16[1024,512]{1,0:T(8,128)(2,1)S(1)}, bf16[512,1024]{1,0:T(8,128)(2,1)S(1)}, f32[512,1024]{1,0:T(8,128)S(1...) custom-call(bf16[1024,512]{1,0:T(8,128)(2,1)S(1)} %get-tuple-element.48.normed_ref, bf16[512,512]{1,0:T(8,128)(2,1)S(1)} %copy-done.3, ...), custom_call_target="tpu_custom_call" | custom-call | flops 1610612736 | bytes 5242880 | tf_op jit(solution)/shard_map/project/pallas_call | solution.py:321
  53.3 0.0 collective-permute-done.third_ref
  53.3 0.0 collective-permute-done.1.fourth_ref
  53.3 0.1 corners.2
  53.3 0.3 collective-permute-start.2
  53.6 2.7 %collective-permute-start.3 = (bf16[128,512]{1,0:T(8,128)(2,1)S(1)}, bf16[128,512]{1,0:T(8,128)(2,1)S(1)}, u32[]{:S(2)}, u32[]{:S(2)}) collective-permute-start(bf16[128,512]{1,0:T(8,128)(2,1)S(1)} %get-tuple-element.61), channel_id=1, source_target_pairs={{0,96},{32,64},{64,32},{96,0},{1,97},{33,65},{65,33},{97,1},{2,98}... | collective-permute-start | bytes 393224 | tf_op jit(solution)/shard_map/ppermute | solution.py:733
  56.3 1.6 %near.2 = (f32[512,1024]{1,0:T(8,128)S(1)}, f32[8,1024]{1,0:T(8,128)S(1)}, f32[8,1024]{1,0:T(8,128)S(1)}) custom-call(bf16[1024,512]{1,0:T(8,128)(2,1)S(1)} %get-tuple-element.49.query_ref, bf16[1024,512]{1,0:T(8,128)(2,1)S(1)} %get-tuple-element.50.key_ref, ...), custom_call_target="tpu_custom_call", output_to_operand_aliasing={{0}: (7, {}), {1}: (8, {}), {2}: (9, {})} | custom-call | flops 8589934592 | bytes 8388608 | tf_op jit(solution)/shard_map/near/pallas_call | solution.py:396
  57.9 0.0 collective-permute-done.4.first_ref
  57.9 0.0 collective-permute-done.5.second_ref
  57.9 4.6 %far.2 = (f32[1024,512]{1,0:T(8,128)S(1)}, bf16[2,512,512]{2,1,0:T(8,128)(2,1)S(1)}, bf16[2,512,512]{2,1,0:T(8,128)(2,1)S(1)}, bf16[1024,512]{1,0:T(8,128)(2,1)S...) custom-call(bf16[1024,512]{1,0:T(8,128)(2,1)S(1)} %get-tuple-element.49.query_ref, ...), custom_call_target="tpu_custom_call" | custom-call | flops 8589934592 | bytes 8388608 | tf_op jit(solution)/shard_map/far/pallas_call | solution.py:544
  62.5 0.0 collective-permute-done.2.first_ref
  62.6 0.0 collective-permute-done.3.second_ref
  62.6 0.0 copy-start.2
  62.6 1.7 %edges.2 = (f32[1024,512]{1,0:T(8,128)S(1)}, bf16[1024,512]{1,0:T(8,128)(2,1)S(1)}, bf16[512,512]{1,0:T(8,128)(2,1)S(1)}, bf16[512,512]{1,0:T(8,128)(2,1)S(1)}, ...) custom-call(bf16[1024,512]{1,0:T(8,128)(2,1)S(1)} %get-tuple-element, ...), custom_call_target="tpu_custom_call", output_to_operand_aliasing={{0}: (13, {}), {1}: (14, {}), {2}: (15, {}), {3}: (16, {})} | custom-call | tf_op jit(solution)/shard_map/edges/pallas_call | solution.py:687
  64.3 2.4 %collective-permute-start.6 = (bf16[128,512]{1,0:T(8,128)(2,1)S(1)}, bf16[128,512]{1,0:T(8,128)(2,1)S(1)}, u32[]{:S(2)}, u32[]{:S(2)}) collective-permute-start(bf16[128,512]{1,0:T(8,128)(2,1)S(1)} %get-tuple-element.75), channel_id=1, source_target_pairs={{0,1},{1,0},{2,3},{3,2},{4,5},{5,4},{6,7},{7,6},{8,9},{9,8},{10,11... | collective-permute-start | bytes 393224 | tf_op jit(solution)/shard_map/ppermute | solution.py:726
  66.7 1.8 %collective-permute-start.7 = (bf16[128,512]{1,0:T(8,128)(2,1)S(1)}, bf16[128,512]{1,0:T(8,128)(2,1)S(1)}, u32[]{:S(2)}, u32[]{:S(2)}) collective-permute-start(bf16[128,512]{1,0:T(8,128)(2,1)S(1)} %get-tuple-element.76), channel_id=1, source_target_pairs={{0,31},{1,2},{2,1},{3,4},{4,3},{5,6},{6,5},{7,8},{8,7},{9,10},{10,... | collective-permute-start | bytes 393224 | tf_op jit(solution)/shard_map/ppermute | solution.py:727
  68.5 0.7 collective-permute-start.10
  69.2 2.7 %collective-permute-start.11 = (bf16[512,512]{1,0:T(8,128)(2,1)S(1)}, bf16[512,512]{1,0:T(8,128)(2,1)S(1)}, u32[]{:S(2)}, u32[]{:S(2)}) collective-permute-start(bf16[512,512]{1,0:T(8,128)(2,1)S(1)} %get-tuple-element.87), channel_id=1, source_target_pairs={{0,0},{96,96},{32,64},{64,32},{1,1},{97,97},{33,65},{65,33},{2,2},... | collective-permute-start | bytes 1572872 | tf_op jit(solution)/shard_map/ppermute | solution.py:728
  72.0 4.9 %project.3 = (bf16[1024,512]{1,0:T(8,128)(2,1)S(1)}, bf16[1024,512]{1,0:T(8,128)(2,1)S(1)}, bf16[512,1024]{1,0:T(8,128)(2,1)S(1)}, f32[512,1024]{1,0:T(8,128)S(1...) custom-call(bf16[1024,512]{1,0:T(8,128)(2,1)S(1)} %get-tuple-element.71.normed_ref, bf16[512,512]{1,0:T(8,128)(2,1)S(1)} %copy-done.2, ...), custom_call_target="tpu_custom_call" | custom-call | flops 1610612736 | bytes 5242880 | tf_op jit(solution)/shard_map/project/pallas_call | solution.py:321
  76.9 0.0 collective-permute-done.6.third_ref
  76.9 0.0 collective-permute-done.7.fourth_ref
  76.9 0.1 corners.3
  77.0 0.3 collective-permute-start.8
  77.3 2.5 %collective-permute-start.9 = (bf16[128,512]{1,0:T(8,128)(2,1)S(1)}, bf16[128,512]{1,0:T(8,128)(2,1)S(1)}, u32[]{:S(2)}, u32[]{:S(2)}) collective-permute-start(bf16[128,512]{1,0:T(8,128)(2,1)S(1)} %get-tuple-element.84), channel_id=1, source_target_pairs={{0,96},{32,64},{64,32},{96,0},{1,97},{33,65},{65,33},{97,1},{2,98}... | collective-permute-start | bytes 393224 | tf_op jit(solution)/shard_map/ppermute | solution.py:733
  79.8 1.6 %near.3 = (f32[512,1024]{1,0:T(8,128)S(1)}, f32[8,1024]{1,0:T(8,128)S(1)}, f32[8,1024]{1,0:T(8,128)S(1)}) custom-call(bf16[1024,512]{1,0:T(8,128)(2,1)S(1)} %get-tuple-element.72.query_ref, bf16[1024,512]{1,0:T(8,128)(2,1)S(1)} %get-tuple-element.73.key_ref, ...), custom_call_target="tpu_custom_call", output_to_operand_aliasing={{0}: (7, {}), {1}: (8, {}), {2}: (9, {})} | custom-call | flops 8589934592 | bytes 8388608 | tf_op jit(solution)/shard_map/near/pallas_call | solution.py:396
  81.4 0.0 collective-permute-done.10.first_ref
  81.4 0.0 collective-permute-done.11.second_ref
  81.4 4.3 %far.3 = (f32[1024,512]{1,0:T(8,128)S(1)}, bf16[2,512,512]{2,1,0:T(8,128)(2,1)S(1)}, bf16[2,512,512]{2,1,0:T(8,128)(2,1)S(1)}) custom-call(bf16[1024,512]{1,0:T(8,128)(2,1)S(1)} %get-tuple-element.72.query_ref, f32[512,1024]{1,0:T(8,128)S(1)} %get-tuple-element.80.mixed_ref, f32[8,1024]{1,0:T(8,128)S(1)} %get-tuple-element.81.highest_ref, ...), custom_call_target="tpu_custom_call" | custom-call | flops 8589934592 | bytes 8388608 | tf_op jit(solution)/shard_map/far/pallas_call | solution.py:544
  85.7 0.0 collective-permute-done.8.first_ref
  85.7 0.0 collective-permute-done.9.second_ref
  85.7 2.5 %edges.3 = bf16[16,64,512]{2,1,0:T(8,128)(2,1)} custom-call(bf16[1024,512]{1,0:T(8,128)(2,1)S(1)} %get-tuple-element.72.query_ref, f32[512,1024]{1,0:T(8,128)S(1)} %get-tuple-element.80.mixed_ref, f32[8,1024]{1,0:T(8,128)S(1)} %get-tuple-element.81.highest_ref, f32[8,1024]{1,0:T(8,128)S(1)} %get-tuple-element.82.total_ref, ...), custom_call_target="tpu_custom_call" | custom-call | tf_op jit(solution)/shard_map/edges/pallas_call | solution.py:687
  (11 shorter events, 0.0 us)
Async XLA Ops:
  0.0 15.2 %copy-start.4 = (f32[2,512]{1,0:T(2,128)S(1)}, f32[2,512]{1,0:T(2,128)}, u32[]{:S(2)}) copy-start(f32[2,512]{1,0:T(2,128)} %gain_ref.1) | copy-start | bytes 12292
  3.7 33.7 %all-to-all-start = ((bf16[128,40,128]{2,1,0:T(8,128)(2,1)}), bf16[128,40,128]{2,1,0:T(8,128)(2,1)S(1)}, u32[]{:S(2)}, u32[]{:S(2)}) async-start(bf16[128,40,128]{2,1,0:T(8,128)(2,1)} %dispatch.1), calls=%async_computation | async-start | bytes 2621440 | tf_op jit(solution)/shard_map/all_to_all | solution.py:709
  16.9 2.4 %copy-start.5 = (bf16[2,512,512]{2,1,0:T(8,128)(2,1)S(1)}, bf16[2,512,512]{2,1,0:T(8,128)(2,1)}, u32[]{:S(2)}) copy-start(bf16[2,512,512]{2,1,0:T(8,128)(2,1)} %param.19) | copy-start | bytes 3145732
  16.9 3.3 %copy-start.6 = (bf16[2,512,512]{2,1,0:T(8,128)(2,1)S(1)}, bf16[2,512,512]{2,1,0:T(8,128)(2,1)}, u32[]{:S(2)}) copy-start(bf16[2,512,512]{2,1,0:T(8,128)(2,1)} %param.21) | copy-start | bytes 3145732
  37.4 10.9 %copy-start = (bf16[512,512]{1,0:T(8,128)(2,1)S(1)}, bf16[512,512]{1,0:T(8,128)(2,1)}, u32[]{:S(2)}) copy-start(bf16[512,512]{1,0:T(8,128)(2,1)} %get-tuple-element.96.key_w) | copy-start | bytes 1572868
  37.4 10.9 %copy-start.3 = (bf16[512,512]{1,0:T(8,128)(2,1)S(1)}, bf16[512,512]{1,0:T(8,128)(2,1)}, u32[]{:S(2)}) copy-start(bf16[512,512]{1,0:T(8,128)(2,1)} %get-tuple-element.98.query_w) | copy-start | bytes 1572868
  42.5 10.7 %collective-permute-start = (bf16[128,512]{1,0:T(8,128)(2,1)S(1)}, bf16[128,512]{1,0:T(8,128)(2,1)S(1)}, u32[]{:S(2)}, u32[]{:S(2)}) collective-permute-start(bf16[128,512]{1,0:T(8,128)(2,1)S(1)} %get-tuple-element.52), channel_id=1, source_target_pairs={{0,1},{1,0},{2,3},{3,2},{4,5},{5,4},{6,7},{7,6},{8,9},{9,8},{10,11... | collective-permute-start | bytes 393224 | tf_op jit(solution)/shard_map/ppermute | solution.py:726
  42.6 10.6 %collective-permute-start.1 = (bf16[128,512]{1,0:T(8,128)(2,1)S(1)}, bf16[128,512]{1,0:T(8,128)(2,1)S(1)}, u32[]{:S(2)}, u32[]{:S(2)}) collective-permute-start(bf16[128,512]{1,0:T(8,128)(2,1)S(1)} %get-tuple-element.53), channel_id=1, source_target_pairs={{0,31},{1,2},{2,1},{3,4},{4,3},{5,6},{6,5},{7,8},{8,7},{9,10},{10,... | collective-permute-start | bytes 393224 | tf_op jit(solution)/shard_map/ppermute | solution.py:727
  44.4 13.5 %collective-permute-start.4 = (bf16[512,512]{1,0:T(8,128)(2,1)S(1)}, bf16[512,512]{1,0:T(8,128)(2,1)S(1)}, u32[]{:S(2)}, u32[]{:S(2)}) collective-permute-start(bf16[512,512]{1,0:T(8,128)(2,1)S(1)} %get-tuple-element.63), channel_id=1, source_target_pairs={{0,32},{32,0},{64,96},{96,64},{1,33},{33,1},{65,97},{97,65},{2,34}... | collective-permute-start | bytes 1572872 | tf_op jit(solution)/shard_map/ppermute | solution.py:729
  45.8 12.1 %collective-permute-start.5 = (bf16[512,512]{1,0:T(8,128)(2,1)S(1)}, bf16[512,512]{1,0:T(8,128)(2,1)S(1)}, u32[]{:S(2)}, u32[]{:S(2)}) collective-permute-start(bf16[512,512]{1,0:T(8,128)(2,1)S(1)} %get-tuple-element.64), channel_id=1, source_target_pairs={{0,0},{96,96},{32,64},{64,32},{1,1},{97,97},{33,65},{65,33},{2,2},... | collective-permute-start | bytes 1572872 | tf_op jit(solution)/shard_map/ppermute | solution.py:728
  53.3 9.2 %collective-permute-start.2 = (bf16[128,512]{1,0:T(8,128)(2,1)S(1)}, bf16[128,512]{1,0:T(8,128)(2,1)S(1)}, u32[]{:S(2)}, u32[]{:S(2)}) collective-permute-start(bf16[128,512]{1,0:T(8,128)(2,1)S(1)} %get-tuple-element.60), channel_id=1, source_target_pairs={{0,32},{32,0},{64,96},{96,64},{1,33},{33,1},{65,97},{97,65},{2,34}... | collective-permute-start | bytes 393224 | tf_op jit(solution)/shard_map/ppermute | solution.py:734
  53.6 8.9 %collective-permute-start.3 = (bf16[128,512]{1,0:T(8,128)(2,1)S(1)}, bf16[128,512]{1,0:T(8,128)(2,1)S(1)}, u32[]{:S(2)}, u32[]{:S(2)}) collective-permute-start(bf16[128,512]{1,0:T(8,128)(2,1)S(1)} %get-tuple-element.61), channel_id=1, source_target_pairs={{0,96},{32,64},{64,32},{96,0},{1,97},{33,65},{65,33},{97,1},{2,98}... | collective-permute-start | bytes 393224 | tf_op jit(solution)/shard_map/ppermute | solution.py:733
  56.3 1.6 %copy-start.1 = (bf16[512,512]{1,0:T(8,128)(2,1)S(1)}, bf16[512,512]{1,0:T(8,128)(2,1)}, u32[]{:S(2)}) copy-start(bf16[512,512]{1,0:T(8,128)(2,1)} %get-tuple-element.92.out_w) | copy-start | bytes 1572868
  62.6 9.4 %copy-start.2 = (bf16[512,512]{1,0:T(8,128)(2,1)S(1)}, bf16[512,512]{1,0:T(8,128)(2,1)}, u32[]{:S(2)}) copy-start(bf16[512,512]{1,0:T(8,128)(2,1)} %get-tuple-element.97.query_w) | copy-start | bytes 1572868
  64.3 12.6 %collective-permute-start.6 = (bf16[128,512]{1,0:T(8,128)(2,1)S(1)}, bf16[128,512]{1,0:T(8,128)(2,1)S(1)}, u32[]{:S(2)}, u32[]{:S(2)}) collective-permute-start(bf16[128,512]{1,0:T(8,128)(2,1)S(1)} %get-tuple-element.75), channel_id=1, source_target_pairs={{0,1},{1,0},{2,3},{3,2},{4,5},{5,4},{6,7},{7,6},{8,9},{9,8},{10,11... | collective-permute-start | bytes 393224 | tf_op jit(solution)/shard_map/ppermute | solution.py:726
  66.7 10.2 %collective-permute-start.7 = (bf16[128,512]{1,0:T(8,128)(2,1)S(1)}, bf16[128,512]{1,0:T(8,128)(2,1)S(1)}, u32[]{:S(2)}, u32[]{:S(2)}) collective-permute-start(bf16[128,512]{1,0:T(8,128)(2,1)S(1)} %get-tuple-element.76), channel_id=1, source_target_pairs={{0,31},{1,2},{2,1},{3,4},{4,3},{5,6},{6,5},{7,8},{8,7},{9,10},{10,... | collective-permute-start | bytes 393224 | tf_op jit(solution)/shard_map/ppermute | solution.py:727
  68.5 12.9 %collective-permute-start.10 = (bf16[512,512]{1,0:T(8,128)(2,1)S(1)}, bf16[512,512]{1,0:T(8,128)(2,1)S(1)}, u32[]{:S(2)}, u32[]{:S(2)}) collective-permute-start(bf16[512,512]{1,0:T(8,128)(2,1)S(1)} %get-tuple-element.86), channel_id=1, source_target_pairs={{0,32},{32,0},{64,96},{96,64},{1,33},{33,1},{65,97},{97,65},{2,34}... | collective-permute-start | bytes 1572872 | tf_op jit(solution)/shard_map/ppermute | solution.py:729
  69.2 12.2 %collective-permute-start.11 = (bf16[512,512]{1,0:T(8,128)(2,1)S(1)}, bf16[512,512]{1,0:T(8,128)(2,1)S(1)}, u32[]{:S(2)}, u32[]{:S(2)}) collective-permute-start(bf16[512,512]{1,0:T(8,128)(2,1)S(1)} %get-tuple-element.87), channel_id=1, source_target_pairs={{0,0},{96,96},{32,64},{64,32},{1,1},{97,97},{33,65},{65,33},{2,2},... | collective-permute-start | bytes 1572872 | tf_op jit(solution)/shard_map/ppermute | solution.py:728
  77.0 8.7 %collective-permute-start.8 = (bf16[128,512]{1,0:T(8,128)(2,1)S(1)}, bf16[128,512]{1,0:T(8,128)(2,1)S(1)}, u32[]{:S(2)}, u32[]{:S(2)}) collective-permute-start(bf16[128,512]{1,0:T(8,128)(2,1)S(1)} %get-tuple-element.83), channel_id=1, source_target_pairs={{0,32},{32,0},{64,96},{96,64},{1,33},{33,1},{65,97},{97,65},{2,34}... | collective-permute-start | bytes 393224 | tf_op jit(solution)/shard_map/ppermute | solution.py:734
  77.3 8.4 %collective-permute-start.9 = (bf16[128,512]{1,0:T(8,128)(2,1)S(1)}, bf16[128,512]{1,0:T(8,128)(2,1)S(1)}, u32[]{:S(2)}, u32[]{:S(2)}) collective-permute-start(bf16[128,512]{1,0:T(8,128)(2,1)S(1)} %get-tuple-element.84), channel_id=1, source_target_pairs={{0,96},{32,64},{64,32},{96,0},{1,97},{33,65},{65,33},{97,1},{2,98}... | collective-permute-start | bytes 393224 | tf_op jit(solution)/shard_map/ppermute | solution.py:733
